TPU v7x, 32 devices: a whole 2x2x4 slice. The times are simulated.
32 devices in a mesh: sx: 4 (over x, core), sy: 2 (over y), cr: 4 (over z).
Axes of the slice: x: 2, y: 2, z: 4, core: 2. Of those that a mesh axis runs over, the one named last changes fastest.
Arguments:
- adjoint: float32 [256, 64, 256], P('cr', 'sx', 'sy'), may hold values from -6 to 6
- sensor_rows: bfloat16 [3072, 64, 256], P('cr', 'sx', 'sy'), may hold values from -0.046875 to 0.046875
- cell_ids: int32 [64, 256], P('sx', 'sy'), may hold values from 0 to 15
- mat_diag: float32 [16], replicated, may hold values from -0.15 to 0.15
- mat_cond: float32 [16], replicated, may hold values from 0.2 to 0.45
- cheb_coef: float32 [9], replicated, may hold values from 0.3 to 1
Outputs:
- smoothed: float32 [256, 64, 256], P('cr', 'sx', 'sy')
- panel: float32 [3072, 256], P('cr', ('sx', 'sy'))
All inputs are finite; a program needn't handle non-finite values.
Results may differ from a plain program's by a relative error of at most 0.0029.
Values may be sent and summed in bfloat16 or wider, within the bound.
No kernel may reach another device: no remote copies, remote signals or barrier semaphores. Data moves between devices by JAX's collectives and lax.ppermute only.
A program may use at most 64 MiB of HBM per device.

v0:
```python
import jax
import jax.numpy as jnp
from jax import lax
from jax.sharding import PartitionSpec as P

DEG = 8


def padded(value, sides, width):
    for axis, dim in sides:
        size, length = (lax.axis_size(axis), value.shape[dim])
        up = [(i, (i + 1) % size) for i in range(size - 1)]
        down = [(j, i) for i, j in up]
        last = lax.slice_in_dim(value, length - width, length, axis=dim)
        first = lax.slice_in_dim(value, 0, width, axis=dim)
        before = lax.ppermute(last, axis, up)
        after = lax.ppermute(first, axis, down)
        value = jnp.concatenate([before, value, after], axis=dim)
    return value


def apply_inner(field, diag, cond):
    weighted = cond * field
    beside = weighted[:, :-2, 1:-1] + weighted[:, 2:, 1:-1]
    beside = beside + weighted[:, 1:-1, :-2] + weighted[:, 1:-1, 2:]
    return diag[1:-1, 1:-1] * field[:, 1:-1, 1:-1] + cond[1:-1, 1:-1] * beside


def trim(array, have, want):
    offset = have - want
    return array[..., offset : array.shape[-2] - offset, offset : array.shape[-1] - offset]


def on_device(adjoint, sensor_rows, cell_ids, mat_diag, mat_cond, cheb_coef):
    width_x = adjoint.shape[1]
    width_y = adjoint.shape[2]
    depth = 4
    ids_wide = padded(cell_ids, (("sx", 0), ("sy", 1)), depth)
    materials = jnp.arange(mat_diag.shape[0], dtype=jnp.int32)
    onehot = (ids_wide[None, :, :] == materials[:, None, None]).astype(jnp.float32)
    diag_wide = jnp.sum(onehot * mat_diag[:, None, None], axis=0)
    cond_wide = jnp.sum(onehot * mat_cond[:, None, None], axis=0)
    start_x = lax.axis_index("sx") * width_x - depth
    start_y = lax.axis_index("sy") * width_y - depth
    pos_x = lax.broadcasted_iota(jnp.int32, (width_x + 2 * depth, width_y + 2 * depth), 0) + start_x
    pos_y = lax.broadcasted_iota(jnp.int32, (width_x + 2 * depth, width_y + 2 * depth), 1) + start_y
    inside = (
        (pos_x >= 0)
        & (pos_x < width_x * lax.axis_size("sx"))
        & (pos_y >= 0)
        & (pos_y < width_y * lax.axis_size("sy"))
    )
    inside = inside.astype(jnp.float32)
    previous = adjoint
    current = adjoint
    smoothed = cheb_coef[0] * adjoint
    for block in range(DEG // depth):
        stacked = jnp.stack([previous, current])
        widened = padded(stacked, (("sx", 2), ("sy", 3)), depth)
        prev_wide = widened[0]
        curr_wide = widened[1]
        for inner in range(depth):
            margin = depth - inner
            diag_here = trim(diag_wide, depth, margin)
            cond_here = trim(cond_wide, depth, margin)
            applied = apply_inner(curr_wide, diag_here, cond_here)
            order = block * depth + inner
            if order == 0:
                newer = applied
            else:
                newer = 2.0 * applied - prev_wide[:, 1:-1, 1:-1]
            newer = newer * trim(inside, depth, margin - 1)
            prev_wide = curr_wide[:, 1:-1, 1:-1]
            curr_wide = newer
            smoothed = smoothed + cheb_coef[order + 1] * trim(newer, margin - 1, 0)
        previous = prev_wide
        current = curr_wide
    lowered = smoothed.astype(jnp.bfloat16)
    flat_rows = sensor_rows.reshape(sensor_rows.shape[0], -1)
    piece = lax.all_gather(lowered, "cr", axis=0, tiled=True)
    flat_piece = piece.reshape(piece.shape[0], -1)
    partial_panel = lax.dot_general(
        flat_rows, flat_piece, (((1,), (1,)), ((), ())), preferred_element_type=jnp.float32
    )
    panel = lax.psum_scatter(partial_panel, ("sx", "sy"), scatter_dimension=1, tiled=True)
    return (smoothed, panel)


def solution(mesh):
    placed = (P("cr", "sx", "sy"), P("cr", "sx", "sy"), P("sx", "sy"), P(), P(), P())
    return jax.shard_map(
        on_device,
        mesh=mesh,
        in_specs=placed,
        out_specs=(P("cr", "sx", "sy"), P("cr", ("sx", "sy"))),
        check_vma=False,
    )
```

profile of v0, /device:TPU:0, one launch (start us, length us, event | category | flops | bytes accessed | tf_op | source)
XLA Modules:
  0.0 194.4 jit_solution(8921182428083322243)
XLA Ops:
  8.1 2.5 %collective-permute-start = (s32[4,128]{1,0:T(4,128)S(1)}, s32[4,128]{1,0:T(4,128)S(1)}, u32[]{:S(2)}, u32[]{:S(2)}) collective-permute-start(s32[4,128]{1,0:T(4,128)S(1)} %get-tuple-element.40), channel_id=1, source_target_pairs={{0,8},{8,16},{16,24},{1,9},{9,17},{17,25},{2,10},{10,18},{18,26},{... | collective-permute-start | bytes 6152 | tf_op jit(solution)/shard_map/ppermute | solution.py:16
  14.8 5.1 %collective-permute-start.4 = (f32[2,64,4,128]{3,1,2,0:T(8,128)}, f32[2,64,4,128]{3,1,2,0:T(8,128)S(1)}, u32[]{:S(2)}, u32[]{:S(2)}) collective-permute-start(f32[2,64,4,128]{3,1,2,0:T(8,128)} %get-tuple-element.36), channel_id=1, source_target_pairs={{0,8},{8,16},{16,24},{1,9},{9,17},{17,25},{2,10},{10,18},{18,26},{... | collective-permute-start | bytes 786440 | tf_op jit(solution)/shard_map/ppermute | solution.py:16
  22.0 3.4 %collective-permute-start.2 = (s32[24,4]{1,0:T(8,128)S(1)}, s32[24,4]{1,0:T(8,128)S(1)}, u32[]{:S(2)}, u32[]{:S(2)}) collective-permute-start(s32[24,4]{1,0:T(8,128)S(1)} %get-tuple-element.38), channel_id=1, source_target_pairs={{0,4},{1,5},{2,6},{3,7},{8,12},{9,13},{10,14},{11,15},{16,20},{17,... | collective-permute-start | bytes 1160 | tf_op jit(solution)/shard_map/ppermute | solution.py:16
  27.7 3.3 %collective-permute-done.3 = s32[24,4]{1,0:T(8,128)S(1)} collective-permute-done((s32[24,4]{1,0:T(8,128)S(1)}, s32[24,4]{1,0:T(8,128)S(1)}, u32[]{:S(2)}, u32[]{:S(2)}) %collective-permute-start.3) | collective-permute-done | bytes 416 | tf_op jit(solution)/shard_map/ppermute | solution.py:17
  33.1 2.2 %fusion.60 = (f32[2,64,24,4]{3,1,2,0:T(8,128)}, f32[2,64,24,4]{3,1,2,0:T(8,128)}) fusion(f32[2,64,24,128]{3,1,2,0:T(8,128)S(1)} %pad_maximum_fusion.6), kind=kLoop, calls=%fused_computation.119 | loop fusion | bytes 196608 | tf_op jit(solution)/shard_map/slice | solution.py:14
  35.3 2.6 %copy.26 = f32[2,64,24,4]{1,2,3,0:T(8,128)} copy(f32[2,64,24,4]{3,1,2,0:T(8,128)} %get-tuple-element.30) | data formatting | bytes 98304 | tf_op jit(solution)/shard_map/slice | solution.py:14
  37.9 2.6 %copy.27 = f32[2,64,24,4]{1,2,3,0:T(8,128)} copy(f32[2,64,24,4]{3,1,2,0:T(8,128)} %get-tuple-element.31) | data formatting | bytes 98304 | tf_op jit(solution)/shard_map/slice | solution.py:15
  41.8 5.8 %collective-permute-start.6 = (f32[2,64,24,4]{1,2,3,0:T(8,128)}, f32[2,64,24,4]{1,2,3,0:T(8,128)}, u32[]{:S(2)}, u32[]{:S(2)}) collective-permute-start(f32[2,64,24,4]{1,2,3,0:T(8,128)} %copy.26), channel_id=1, source_target_pairs={{0,4},{1,5},{2,6},{3,7},{8,12},{9,13},{10,14},{11,15},{16,20},{17,... | collective-permute-start | bytes 147464 | tf_op jit(solution)/shard_map/ppermute | solution.py:16
  52.0 2.6 %copy.28 = f32[2,64,24,4]{3,1,2,0:T(8,128)} copy(f32[2,64,24,4]{1,2,3,0:T(8,128)} %collective-permute-done.6) | data formatting | bytes 98304 | tf_op jit(solution)/shard_map/ppermute | solution.py:16
  54.6 2.6 %copy.29 = f32[2,64,24,4]{3,1,2,0:T(8,128)} copy(f32[2,64,24,4]{1,2,3,0:T(8,128)} %collective-permute-done.7) | data formatting | bytes 98304 | tf_op jit(solution)/shard_map/ppermute | solution.py:17
  57.2 2.3 %broadcast_multiply_fusion.1 = (f32[64,24,136]{2,0,1:T(8,128)S(1)}, f32[64,24,136]{2,0,1:T(8,128)S(1)}) fusion(f32[24,136]{1,0:T(8,128)S(1)} %get-tuple-element.9, f32[2,64,24,4]{3,1,2,0:T(8,128)} %copy.29, f32[2,64,4,128]{3,1,2,0:T(8,128)} %collective-permute-done.5, f32[1,64,16,128]{3,1,2,0:T(8,128)} %bitcast.34, ...), kind=kLoop, calls=%fused_computation.67 | loop fusion | flops 1253376 | bytes 2831104 | tf_op jit(solution)/shard_map/mul | solution.py:23
  59.5 1.6 broadcast_multiply_fusion.3
  61.1 1.8 broadcast_multiply_fusion.5
  63.0 1.6 broadcast_multiply_fusion.7
  65.7 2.3 %collective-permute-start.8 = (f32[2,64,4,128]{3,1,2,0:T(8,128)S(1)}, f32[2,64,4,128]{3,1,2,0:T(8,128)S(1)}, u32[]{:S(2)}, u32[]{:S(2)}) collective-permute-start(f32[2,64,4,128]{3,1,2,0:T(8,128)S(1)} %get-tuple-element.34), channel_id=1, source_target_pairs={{0,8},{8,16},{16,24},{1,9},{9,17},{17,25},{2,10},{10,18},{18,26},{... | collective-permute-start | bytes 786440 | tf_op jit(solution)/shard_map/ppermute | solution.py:16
  69.3 5.3 %collective-permute-done.9 = f32[2,64,4,128]{3,1,2,0:T(8,128)S(1)} collective-permute-done((f32[2,64,4,128]{3,1,2,0:T(8,128)S(1)}, f32[2,64,4,128]{3,1,2,0:T(8,128)S(1)}, u32[]{:S(2)}, u32[]{:S(2)}) %collective-permute-start.9) | collective-permute-done | bytes 262176 | tf_op jit(solution)/shard_map/ppermute | solution.py:17
  75.5 2.2 %fusion.59 = (f32[2,64,24,4]{3,1,2,0:T(8,128)}, f32[2,64,24,4]{3,1,2,0:T(8,128)}) fusion(f32[2,64,24,128]{3,1,2,0:T(8,128)S(1)} %pad_maximum_fusion.7), kind=kLoop, calls=%fused_computation.118 | loop fusion | bytes 196608 | tf_op jit(solution)/shard_map/slice | solution.py:14
  77.7 2.6 %copy.30 = f32[2,64,24,4]{1,2,3,0:T(8,128)} copy(f32[2,64,24,4]{3,1,2,0:T(8,128)} %get-tuple-element.28) | data formatting | bytes 98304 | tf_op jit(solution)/shard_map/slice | solution.py:14
  80.2 2.6 %copy.31 = f32[2,64,24,4]{1,2,3,0:T(8,128)} copy(f32[2,64,24,4]{3,1,2,0:T(8,128)} %get-tuple-element.29) | data formatting | bytes 98304 | tf_op jit(solution)/shard_map/slice | solution.py:15
  84.1 5.8 %collective-permute-start.10 = (f32[2,64,24,4]{1,2,3,0:T(8,128)}, f32[2,64,24,4]{1,2,3,0:T(8,128)}, u32[]{:S(2)}, u32[]{:S(2)}) collective-permute-start(f32[2,64,24,4]{1,2,3,0:T(8,128)} %copy.30), channel_id=1, source_target_pairs={{0,4},{1,5},{2,6},{3,7},{8,12},{9,13},{10,14},{11,15},{16,20},{17,... | collective-permute-start | bytes 147464 | tf_op jit(solution)/shard_map/ppermute | solution.py:16
  89.9 1.7 fusion.63
  91.8 2.6 %copy.32 = f32[2,64,24,4]{3,1,2,0:T(8,128)} copy(f32[2,64,24,4]{1,2,3,0:T(8,128)} %collective-permute-done.10) | data formatting | bytes 98304 | tf_op jit(solution)/shard_map/ppermute | solution.py:16
  94.4 2.6 %copy.33 = f32[2,64,24,4]{3,1,2,0:T(8,128)} copy(f32[2,64,24,4]{1,2,3,0:T(8,128)} %collective-permute-done.11) | data formatting | bytes 98304 | tf_op jit(solution)/shard_map/ppermute | solution.py:17
  97.0 3.6 %pad_maximum_fusion = f32[2,64,24,136]{3,1,2,0:T(8,128)S(1)} fusion(f32[2,64,24,4]{3,1,2,0:T(8,128)} %copy.33, f32[2,64,4,128]{3,1,2,0:T(8,128)} %copy-done.9, f32[1,64,16,128]{3,1,2,0:T(8,128)} %bitcast.31, f32[1,64,16,128]{3,1,2,0:T(8,128)} %copy-done.6, f32[2,64,4,128]{3,1,2,0:T(8,128)S(1)} %collective-permute-done.8, f32[2,64,24,4]{3,1,2,0:T(8,128)} %copy.32), kind=kLoop, calls=%fused_computation | loop fusion | flops 2088960 | bytes 3342336 | tf_op jit(solution)/shard_map/concatenate | solution.py:18
  101.0 1.9 %broadcast_multiply_fusion.2 = (f32[64,22,134]{2,0,1:T(8,128)S(1)}, f32[64,22,134]{2,0,1:T(8,128)S(1)}) fusion(f32[22,134]{1,0:T(8,128)S(1)} %slice.393, f32[22,134]{1,0:T(8,128)S(1)} %slice.398, f32[64,24,136]{2,0,1:T(8,128)S(1)} %get-tuple-element.27, f32[64,24,136]{2,0,1:T(8,128)S(1)} %broadcast_multiply_fusion, f32[64,24,136]{2,0,1:T(8,128)S(1)} %get-tuple-element.26, ...), kind=kLoop, calls=%fused_computation.68 | loop fusion | flops 1886720 | bytes 6072880 | tf_op jit(solution)/shard_map/mul | solution.py:23
  103.0 1.8 broadcast_multiply_fusion.4
  104.9 1.6 broadcast_multiply_fusion.6
  106.6 9.7 %fusion.50 = (bf16[64,16,128]{2,0,1:T(8,128)(2,1)}, f32[64,16,128]{2,0,1:T(8,128)}) fusion(f32[16,128]{1,0:T(8,128)S(1)} %copy-done.19, f32[64,18,130]{2,0,1:T(8,128)S(1)} %get-tuple-element.12, f32[16,128]{1,0:T(8,128)S(1)} %copy-done.23, f32[16,128]{1,0:T(8,128)S(1)} %copy-done.21, f32[]{:T(128)} %bitcast.14, f32[64,18,130]{2,0,1:T(8,128)S(1)} %get-tuple-element.13, ...), kind=kLoop, calls=%fused_computation.117 | loop fusion | flops 3538944 | bytes 7102500 | tf_op jit(solution)/shard_map/convert_element_type | solution.py:78
  116.3 33.2 %all-gather.2.cloned.1.call-done = bf16[256,16,128]{2,0,1:T(8,128)(2,1)} async-done(((bf16[64,16,128]{2,0,1:T(8,128)(2,1)}), bf16[256,16,128]{2,0,1:T(8,128)(2,1)}) %all-gather.2.cloned.1.call-update) | async-done | bytes 1048592 | tf_op jit(solution)/shard_map/all_gather | solution.py:80
  149.5 3.1 %fusion.18 = f32[768,256]{0,1:T(8,128)} fusion(bf16[256,16,128]{2,0,1:T(8,128)(2,1)} %all-gather.2.cloned.1.call-done, bf16[768,16,128]{2,1,0:T(8,128)(2,1)S(1)} %copy-done), kind=kOutput, calls=%fused_computation.47 | convolution fusion | flops 805306368 | bytes 4980736 | tf_op jit(solution)/shard_map/dot_general | solution.py:82
  152.7 2.1 %copy.35 = f32[64,16,128]{2,1,0:T(8,128)} copy(f32[64,16,128]{2,0,1:T(8,128)} %get-tuple-element.11) | data formatting | bytes 1048576
  154.8 32.8 %reduce-scatter.2.cloned.1.call-done = f32[768,32]{0,1:T(8,128)} async-done(((f32[768,256]{0,1:T(8,128)}), f32[768,32]{0,1:T(8,128)}) %reduce-scatter.2.cloned.1.call-update) | async-done | bytes 98320 | tf_op jit(solution)/shard_map/reduce_scatter | solution.py:85
  (104 shorter events, 22.3 us)
Async XLA Ops:
  7.2 142.3 %copy-start = (bf16[768,16,128]{2,1,0:T(8,128)(2,1)S(1)}, bf16[768,16,128]{2,1,0:T(8,128)(2,1)}, u32[]{:S(2)}) copy-start(bf16[768,16,128]{2,1,0:T(8,128)(2,1)} %param.7) | copy-start | bytes 9437188
  7.2 14.7 %copy-start.24 = (s32[16,128]{1,0:T(8,128)S(1)}, s32[16,128]{1,0:T(8,128)}, u32[]{:S(2)}) copy-start(s32[16,128]{1,0:T(8,128)} %param.8) | copy-start | bytes 24580
  7.2 142.3 %all-gather.2.cloned.1.call-start = ((), (), s32[]{:S(2)}) async-start(), calls=%async_computation.1 | async-start | bytes 1310720 | tf_op jit(solution)/shard_map/all_gather | solution.py:80
  8.1 13.2 %collective-permute-start = (s32[4,128]{1,0:T(4,128)S(1)}, s32[4,128]{1,0:T(4,128)S(1)}, u32[]{:S(2)}, u32[]{:S(2)}) collective-permute-start(s32[4,128]{1,0:T(4,128)S(1)} %get-tuple-element.40), channel_id=1, source_target_pairs={{0,8},{8,16},{16,24},{1,9},{9,17},{17,25},{2,10},{10,18},{18,26},{... | collective-permute-start | bytes 6152 | tf_op jit(solution)/shard_map/ppermute | solution.py:16
  10.6 10.7 %collective-permute-start.1 = (s32[4,128]{1,0:T(4,128)S(1)}, s32[4,128]{1,0:T(4,128)S(1)}, u32[]{:S(2)}, u32[]{:S(2)}) collective-permute-start(s32[4,128]{1,0:T(4,128)S(1)} %get-tuple-element.41), channel_id=1, source_target_pairs={{8,0},{16,8},{24,16},{9,1},{17,9},{25,17},{10,2},{18,10},{26,18},{... | collective-permute-start | bytes 6152 | tf_op jit(solution)/shard_map/ppermute | solution.py:17
  14.8 16.9 %collective-permute-start.4 = (f32[2,64,4,128]{3,1,2,0:T(8,128)}, f32[2,64,4,128]{3,1,2,0:T(8,128)S(1)}, u32[]{:S(2)}, u32[]{:S(2)}) collective-permute-start(f32[2,64,4,128]{3,1,2,0:T(8,128)} %get-tuple-element.36), channel_id=1, source_target_pairs={{0,8},{8,16},{16,24},{1,9},{9,17},{17,25},{2,10},{10,18},{18,26},{... | collective-permute-start | bytes 786440 | tf_op jit(solution)/shard_map/ppermute | solution.py:16
  19.9 11.8 %collective-permute-start.5 = (f32[2,64,4,128]{3,1,2,0:T(8,128)}, f32[2,64,4,128]{3,1,2,0:T(8,128)}, u32[]{:S(2)}, u32[]{:S(2)}) collective-permute-start(f32[2,64,4,128]{3,1,2,0:T(8,128)} %get-tuple-element.37), channel_id=1, source_target_pairs={{8,0},{16,8},{24,16},{9,1},{17,9},{25,17},{10,2},{18,10},{26,18},{... | collective-permute-start | bytes 786440 | tf_op jit(solution)/shard_map/ppermute | solution.py:17
  22.0 5.7 %collective-permute-start.2 = (s32[24,4]{1,0:T(8,128)S(1)}, s32[24,4]{1,0:T(8,128)S(1)}, u32[]{:S(2)}, u32[]{:S(2)}) collective-permute-start(s32[24,4]{1,0:T(8,128)S(1)} %get-tuple-element.38), channel_id=1, source_target_pairs={{0,4},{1,5},{2,6},{3,7},{8,12},{9,13},{10,14},{11,15},{16,20},{17,... | collective-permute-start | bytes 1160 | tf_op jit(solution)/shard_map/ppermute | solution.py:16
  25.4 5.6 %collective-permute-start.3 = (s32[24,4]{1,0:T(8,128)S(1)}, s32[24,4]{1,0:T(8,128)S(1)}, u32[]{:S(2)}, u32[]{:S(2)}) collective-permute-start(s32[24,4]{1,0:T(8,128)S(1)} %get-tuple-element.39), channel_id=1, source_target_pairs={{4,0},{5,1},{6,2},{7,3},{12,8},{13,9},{14,10},{15,11},{20,16},{21,... | collective-permute-start | bytes 1160 | tf_op jit(solution)/shard_map/ppermute | solution.py:17
  35.3 12.3 %copy-start.26 = (f32[16]{0:T(128)S(1)}, f32[16]{0:T(128)}, u32[]{:S(2)}) copy-start(f32[16]{0:T(128)} %param.9) | copy-start | bytes 196
  35.3 12.3 %copy-start.27 = (f32[16]{0:T(128)S(1)}, f32[16]{0:T(128)}, u32[]{:S(2)}) copy-start(f32[16]{0:T(128)} %param.10) | copy-start | bytes 196
  40.5 14.1 %collective-permute-start.7 = (f32[2,64,24,4]{1,2,3,0:T(8,128)}, f32[2,64,24,4]{1,2,3,0:T(8,128)}, u32[]{:S(2)}, u32[]{:S(2)}) collective-permute-start(f32[2,64,24,4]{1,2,3,0:T(8,128)} %copy.27), channel_id=1, source_target_pairs={{4,0},{5,1},{6,2},{7,3},{12,8},{13,9},{14,10},{15,11},{20,16},{21,... | collective-permute-start | bytes 147464 | tf_op jit(solution)/shard_map/ppermute | solution.py:17
  41.8 10.2 %collective-permute-start.6 = (f32[2,64,24,4]{1,2,3,0:T(8,128)}, f32[2,64,24,4]{1,2,3,0:T(8,128)}, u32[]{:S(2)}, u32[]{:S(2)}) collective-permute-start(f32[2,64,24,4]{1,2,3,0:T(8,128)} %copy.26), channel_id=1, source_target_pairs={{0,4},{1,5},{2,6},{3,7},{8,12},{9,13},{10,14},{11,15},{16,20},{17,... | collective-permute-start | bytes 147464 | tf_op jit(solution)/shard_map/ppermute | solution.py:16
  61.1 1.9 copy-start.1
  61.1 1.8 copy-start.10
  61.1 1.8 copy-start.12
  62.9 1.7 copy-start.4
  65.6 9.8 %copy-start.2 = (f32[64,16,128]{2,0,1:T(8,128)}, f32[64,16,128]{2,0,1:T(8,128)S(1)}, u32[]{:S(2)}) copy-start(f32[64,16,128]{2,0,1:T(8,128)S(1)} %get-tuple-element.33) | copy-start | bytes 1572868
  65.6 9.8 %copy-start.6 = (f32[1,64,16,128]{3,1,2,0:T(8,128)}, f32[1,64,16,128]{3,1,2,0:T(8,128)S(1)}, u32[]{:S(2)}) copy-start(f32[1,64,16,128]{3,1,2,0:T(8,128)S(1)} %get-tuple-element.32) | copy-start | bytes 1572868
  65.7 3.6 %collective-permute-start.8 = (f32[2,64,4,128]{3,1,2,0:T(8,128)S(1)}, f32[2,64,4,128]{3,1,2,0:T(8,128)S(1)}, u32[]{:S(2)}, u32[]{:S(2)}) collective-permute-start(f32[2,64,4,128]{3,1,2,0:T(8,128)S(1)} %get-tuple-element.34), channel_id=1, source_target_pairs={{0,8},{8,16},{16,24},{1,9},{9,17},{17,25},{2,10},{10,18},{18,26},{... | collective-permute-start | bytes 786440 | tf_op jit(solution)/shard_map/ppermute | solution.py:16
  68.0 6.6 %collective-permute-start.9 = (f32[2,64,4,128]{3,1,2,0:T(8,128)S(1)}, f32[2,64,4,128]{3,1,2,0:T(8,128)S(1)}, u32[]{:S(2)}, u32[]{:S(2)}) collective-permute-start(f32[2,64,4,128]{3,1,2,0:T(8,128)S(1)} %get-tuple-element.35), channel_id=1, source_target_pairs={{8,0},{16,8},{24,16},{9,1},{17,9},{25,17},{10,2},{18,10},{26,18},{... | collective-permute-start | bytes 786440 | tf_op jit(solution)/shard_map/ppermute | solution.py:17
  82.8 11.6 %collective-permute-start.11 = (f32[2,64,24,4]{1,2,3,0:T(8,128)}, f32[2,64,24,4]{1,2,3,0:T(8,128)}, u32[]{:S(2)}, u32[]{:S(2)}) collective-permute-start(f32[2,64,24,4]{1,2,3,0:T(8,128)} %copy.31), channel_id=1, source_target_pairs={{4,0},{5,1},{6,2},{7,3},{12,8},{13,9},{14,10},{15,11},{20,16},{21,... | collective-permute-start | bytes 147464 | tf_op jit(solution)/shard_map/ppermute | solution.py:17
  84.1 7.7 %collective-permute-start.10 = (f32[2,64,24,4]{1,2,3,0:T(8,128)}, f32[2,64,24,4]{1,2,3,0:T(8,128)}, u32[]{:S(2)}, u32[]{:S(2)}) collective-permute-start(f32[2,64,24,4]{1,2,3,0:T(8,128)} %copy.30), channel_id=1, source_target_pairs={{0,4},{1,5},{2,6},{3,7},{8,12},{9,13},{10,14},{11,15},{16,20},{17,... | collective-permute-start | bytes 147464 | tf_op jit(solution)/shard_map/ppermute | solution.py:16
  101.0 2.0 %copy-start.15 = (f32[20,132]{1,0:T(8,128)S(1)}, f32[20,132]{1,0:T(8,128)}, u32[]{:S(2)}) copy-start(f32[20,132]{1,0:T(8,128)} %slice.400) | copy-start | bytes 31684
  101.0 2.0 %copy-start.17 = (f32[20,132]{1,0:T(8,128)S(1)}, f32[20,132]{1,0:T(8,128)}, u32[]{:S(2)}) copy-start(f32[20,132]{1,0:T(8,128)} %slice.402) | copy-start | bytes 31684
  103.0 1.8 copy-start.11
  103.0 1.8 copy-start.13
  104.8 1.7 copy-start.3
  104.8 1.7 copy-start.8
  104.8 1.7 copy-start.19
  104.9 1.7 copy-start.21
  116.2 71.4 %reduce-scatter.2.cloned.1.call-start = ((), (), s32[]{:S(2)}) async-start(), calls=%async_computation.2 | async-start | bytes 884736 | tf_op jit(solution)/shard_map/reduce_scatter | solution.py:85
  (10 other events, 13.1 us)
Sparse Core Ops, SparseCore 0:
  116.4 33.0 all-gather.1
  153.2 34.3 reduce-scatter.1
where the time goes:
time: 195 us; the launch traced here: 194 us
  waiting for transfers between devices  74.9 us (38%)
  local copies, waits for them, and re-layouts  38.9 us (20%)
  starting transfers between devices  32.8 us (17%)
  other arithmetic  30.1 us (15%)
  between operations  14.6 us (7%)
  matrix products  3.14 us (2%)
    all_gather x1, waiting for transfers between devices, on_device(): piece = lax.all_gather(lowered, 'cr', axis=0, tiled=True)  33.2 us
    reduce_scatter x1, waiting for transfers between devices, on_device(): lax.psum_scatter(partial_panel, ('sx', 'sy'), scatter_dimension=1, tiled=...  32.8 us
    ppermute x6, starting transfers between devices, padded(): before = lax.ppermute(last, axis, up)  25 us
    mul x8, other arithmetic, apply_inner(): weighted = cond * field  12.8 us
    slice x6, local copies, waits for them, and re-layouts, padded(): last = lax.slice_in_dim(value, length - width, length, axis=dim)  10.5 us
    convert_element_type x1, other arithmetic, on_device(): lowered = smoothed.astype(jnp.bfloat16)  9.66 us
    ppermute x6, waiting for transfers between devices, padded(): after = lax.ppermute(first, axis, down)  8.65 us
    ppermute x6, starting transfers between devices, padded(): after = lax.ppermute(first, axis, down)  7.73 us
  transfers between devices with their start and end apart: 14, of which 5 were waited for; matrix products, arithmetic and copies ran while one was open for 9% of the time, Pallas kernels for 0%

commit v1 on v0

v1 whole, which is shorter than its diff:
```python
import functools

import jax
import jax.numpy as jnp
from jax import lax
from jax.experimental import pallas as pl
from jax.experimental.pallas import tpu as pltpu
from jax.sharding import PartitionSpec as P

DEG = 8
SUB = 8
LANES = 128
SIDE = 2 * DEG
F32 = jnp.float32
BF16 = jnp.bfloat16


def partner(i, odd, size):
    j = i ^ 1 if not odd else ((i + 1) ^ 1) - 1
    return j if 0 <= j < size else None


def pairing(kind_x, kind_y, size_x, size_y):
    pairs = []
    for i in range(size_x):
        for j in range(size_y):
            a = i if kind_x is None else partner(i, kind_x, size_x)
            b = j if kind_y is None else partner(j, kind_y, size_y)
            if a is not None and b is not None:
                pairs.append((i * size_y + j, a * size_y + b))
    return pairs


def edge_lanes():
    place = lax.broadcasted_iota(jnp.int32, (SUB, LANES), 1) & (SIDE - 1)
    return jnp.where(place < DEG, DEG - 1 - place, LANES - 1 + DEG - place)


def lane_gather(tile, index):
    return jnp.take_along_axis(tile, index, axis=1, mode="promise_in_bounds")


def pack_kernel(groups, width_x, n_edge, flags, adj_ref, ids_ref, *out_refs):
    row_refs = out_refs[:2]
    strip_refs = out_refs[2:]
    ids = ids_ref[...].astype(F32) + 1.0
    for which in range(2):
        upper = flags[0] if which == 0 else 1 - flags[0]
        base = jnp.where(upper == 1, width_x - DEG, 0)
        base = pl.multiple_of(base, SUB)

        for row in range(DEG):
            for g in range(groups):
                row_refs[which][row * groups + g] = adj_ref[pl.ds(g * SUB * width_x + base + row, SUB, stride=width_x), :]
        row_refs[which][DEG * groups] = ids_ref[pl.ds(base, SUB), :].astype(F32) + 1.0
    index = edge_lanes()
    lane = lax.broadcasted_iota(jnp.int32, (SUB, LANES), 1)
    low_side = (lane & (SIDE - 1)) < DEG
    n_kinds = len(strip_refs) // 3
    for row in range(width_x):
        strip = jnp.zeros((SUB, LANES), F32)
        for g in range(groups):
            tile = adj_ref[pl.ds(g * SUB * width_x + row, SUB, stride=width_x), :]
            strip = jnp.where((lane // SIDE) == g, lane_gather(tile, index), strip)
        for kind in range(n_kinds):
            upper = flags[1] if kind == 0 else 1 - flags[1]
            keep = jnp.where(low_side, 1 - upper, upper) == 1
            strip_refs[3 * kind][row] = jnp.where(keep, strip, 0.0)
    for tile_x in range(width_x // SUB):
        strip = lane_gather(ids[tile_x * SUB : (tile_x + 1) * SUB], index)
        for kind in range(n_kinds):
            upper = flags[1] if kind == 0 else 1 - flags[1]
            keep = jnp.where(low_side, 1 - upper, upper) == 1
            strip_refs[3 * kind][width_x + tile_x] = jnp.where(keep, strip, 0.0)
    for kind in range(n_kinds):
        for which in range(2):
            upper = flags[0] if which == 0 else 1 - flags[0]
            base = jnp.where(upper == 1, width_x - DEG, 0)
            tile_base = jnp.where(upper == 1, width_x // SUB - 1, 0)
            for row in range(DEG):
                strip_refs[3 * kind + 1 + which][row] = strip_refs[3 * kind][base + row]
            strip_refs[3 * kind + 1 + which][DEG] = strip_refs[3 * kind][width_x + tile_base]


def filter_kernel(
    groups, width_x, flags, diag_ref, cond_ref, coef_ref, adj_ref, ids_ref, even_ref, odd_ref, strip_ref, strip_even_ref,
    strip_odd_ref, smooth_ref, low_ref, u_ref, a_ref, b_ref, c2_ref, d2_ref, c2s_ref, d2s_ref, cond_t, ratio_t, inv_t,
):
    tall = width_x + 2 * DEG
    n_mat = diag_ref.shape[0]
    lane = lax.broadcasted_iota(jnp.int32, (SUB, LANES), 1)
    is_even = flags[0] == 1

    def lookup(ids):
        diag = jnp.zeros_like(ids)
        cond = jnp.zeros_like(ids)
        for m in range(n_mat):
            hit = ids == float(m + 1)
            diag = jnp.where(hit, diag_ref[m], diag)
            cond = jnp.where(hit, cond_ref[m], cond)
        return diag, cond

    def spread(row_tile, x0, c_ref, d_ref, own):
        diag, cond = lookup(row_tile)
        for s in range(SUB):
            c_row = jnp.broadcast_to(cond[s : s + 1], (SUB, LANES))
            d_row = jnp.broadcast_to(diag[s : s + 1], (SUB, LANES))
            c_ref[x0 + s] = 2.0 * c_row * c_row
            d_ref[x0 + s] = 2.0 * d_row
            if own:
                inverse = 1.0 / c_row
                cond_t[x0 + s - DEG] = c_row
                inv_t[x0 + s - DEG] = inverse
                ratio_t[x0 + s - DEG] = d_row * inverse
        return cond

    def scaled(tiles, cond_row):
        return tiles * jnp.broadcast_to(cond_row, (SUB, LANES))

    repeat = lane & (SIDE - 1)
    for high in (False, True):
        x0 = tall - DEG if high else 0
        from_even = is_even if high else jnp.logical_not(is_even)
        ids = jnp.where(from_even, even_ref[DEG * groups], odd_ref[DEG * groups])
        cond = spread(ids, x0, c2_ref, d2_ref, False)
        ids_s = jnp.where(from_even, strip_even_ref[DEG], strip_odd_ref[DEG])
        cond_s = spread(lane_gather(ids_s, repeat), x0, c2s_ref, d2s_ref, False)
        for row in range(DEG):
            for g in range(groups):
                tile = jnp.where(from_even, even_ref[row * groups + g], odd_ref[row * groups + g])
                u_ref[x0 + row, g] = scaled(tile, cond[row : row + 1])
            tile = jnp.where(from_even, strip_even_ref[row], strip_odd_ref[row])
            u_ref[x0 + row, groups] = scaled(tile, cond_s[row : row + 1])
    for tile_x in range(width_x // SUB):
        x0 = DEG + tile_x * SUB
        cond = spread(ids_ref[tile_x * SUB : (tile_x + 1) * SUB, :].astype(F32) + 1.0, x0, c2_ref, d2_ref, True)
        cond_s = spread(lane_gather(strip_ref[width_x + tile_x], repeat), x0, c2s_ref, d2s_ref, False)
        for row in range(SUB):
            for g in range(groups):
                tile = adj_ref[pl.ds(g * SUB * width_x + tile_x * SUB + row, SUB, stride=width_x), :]
                u_ref[x0 + row, g] = scaled(tile, cond[row : row + 1])
            u_ref[x0 + row, groups] = scaled(strip_ref[tile_x * SUB + row], cond_s[row : row + 1])

    first_lane = lane == 0
    last_lane = lane == LANES - 1
    place = lane & (SIDE - 1)
    at_high = place == DEG - 1
    at_low = place == DEG
    junction = lane // SIDE

    def across(tiles, strip):
        sums = []
        meet = None
        for g, tile in enumerate(tiles):
            off = g * SIDE + DEG
            edge = pltpu.roll(strip, LANES - off, 1)
            left = jnp.where(first_lane, edge, pltpu.roll(tile, 1, 1))
            right = jnp.where(last_lane, edge, pltpu.roll(tile, LANES - 1, 1))
            sums.append(left + right)
            moved = pltpu.roll(tile, off, 1)
            meet = moved if meet is None else jnp.where(junction == g, moved, meet)
        up = jnp.where(at_high, meet, pltpu.roll(strip, LANES - 1, 1))
        down = jnp.where(at_low, meet, pltpu.roll(strip, 1, 1))
        return sums, up + down

    def neighbours(src, x, with_strip):
        tiles = [src[x, g] for g in range(groups)]
        strip = src[x, groups]
        sums, strip_sum = across(tiles, strip)
        sums = [s + (src[x - 1, g] + src[x + 1, g]) for g, s in enumerate(sums)]
        if with_strip:
            strip_sum = strip_sum + (src[x - 1, groups] + src[x + 1, groups])
        return tiles, strip, sums, strip_sum

    top = coef_ref[DEG]
    for order in range(DEG - 1, 0, -1):
        lo = DEG - order
        src = u_ref if order == DEG - 1 else (a_ref if (order % 2 == 0) else b_ref)
        dst = b_ref if (order % 2 == 0) else a_ref
        coef = coef_ref[order]

        def step(x, carry, order=order, src=src, dst=dst, coef=coef):
            tiles, strip, sums, strip_sum = neighbours(src, x, True)
            c2 = c2_ref[x]
            d2 = d2_ref[x]
            c2s = c2s_ref[x]
            d2s = d2s_ref[x]
            for g in range(groups + 1):
                tile, total = (tiles[g], sums[g]) if g < groups else (strip, strip_sum)
                cc, dd = (c2, d2) if g < groups else (c2s, d2s)
                applied = dd * tile + cc * total
                if order == DEG - 1:
                    value = coef * tile + top * applied
                elif order == DEG - 2:
                    value = (coef - top) * u_ref[x, g] + applied
                else:
                    value = coef * u_ref[x, g] + (applied - dst[x, g])
                dst[x, g] = value
            return carry

        lax.fori_loop(lo, tall - lo, step, 0)
    first = a_ref
    second = b_ref

    def last(i, carry):
        x = i + DEG
        tiles, _, sums, _ = neighbours(first, x, False)
        cond = cond_t[i]
        ratio = ratio_t[i]
        inverse = inv_t[i]
        out = []
        for g in range(groups):
            start = coef_ref[0] * u_ref[x, g] - second[x, g]
            value = inverse * start + (ratio * tiles[g] + cond * sums[g])
            smooth_ref[pl.ds(g * SUB * width_x + i, SUB, stride=width_x), :] = value
            out.append(value)
        column = pl.multiple_of(i * LANES, LANES)
        for g in range(0, groups, 2):
            both = jnp.concatenate(out[g : g + 2], axis=0)
            low_ref[pl.ds(g * SUB, 2 * SUB), pl.ds(column, LANES)] = both.astype(BF16)
        return carry

    lax.fori_loop(0, width_x, last, 0)


def vmem():
    return pl.BlockSpec(memory_space=pltpu.VMEM)


def smem():
    return pl.BlockSpec(memory_space=pltpu.SMEM)


def filtered(adjoint, cell_ids, mat_diag, mat_cond, cheb_coef):
    cols, width_x, width_y = adjoint.shape
    groups = cols // SUB
    assert width_y == LANES and width_x % SUB == 0 and width_x >= DEG
    assert cols % SIDE == 0 and groups * SIDE <= LANES
    size_x = lax.axis_size("sx")
    size_y = lax.axis_size("sy")
    even_x = 1 - lax.axis_index("sx") % 2
    even_y = 1 - lax.axis_index("sy") % 2
    flags = jnp.stack([even_x, even_y]).astype(jnp.int32)
    flat = adjoint.reshape(cols * width_x, width_y)
    n_kinds = 2 if size_y > 2 else 1
    row_shape = jax.ShapeDtypeStruct((DEG * groups + 1, SUB, LANES), F32)
    strip_shape = jax.ShapeDtypeStruct((width_x + width_x // SUB, SUB, LANES), F32)
    corner_shape = jax.ShapeDtypeStruct((DEG + 1, SUB, LANES), F32)
    packed = pl.pallas_call(
        functools.partial(pack_kernel, groups, width_x, n_kinds),
        out_shape=[row_shape] * 2 + [strip_shape, corner_shape, corner_shape] * n_kinds,
        in_specs=[smem(), vmem(), vmem()],
        out_specs=[vmem()] * (2 + 3 * n_kinds),
        name="pack",
    )(flags, flat, cell_ids)

    def swap(value, kind_x, kind_y):
        pairs = pairing(kind_x, kind_y, size_x, size_y)
        if not pairs:
            return jnp.zeros_like(value)
        return lax.ppermute(value, ("sx", "sy"), pairs)

    odd = swap(packed[1], 1, None)
    even = swap(packed[0], 0, None)
    strips = []
    for kind in range(n_kinds):
        strips.append(
            (
                swap(packed[2 + 3 * kind], None, kind),
                swap(packed[3 + 3 * kind], 0, kind),
                swap(packed[4 + 3 * kind], 1, kind),
            )
        )
    strip, strip_even, strip_odd = (functools.reduce(jnp.add, part) for part in zip(*strips))
    tall = width_x + 2 * DEG
    table = pltpu.VMEM((tall, SUB, LANES), F32)
    own_table = pltpu.VMEM((width_x, SUB, LANES), F32)
    field = pltpu.VMEM((tall, groups + 1, SUB, LANES), F32)
    smooth, low = pl.pallas_call(
        functools.partial(filter_kernel, groups, width_x),
        out_shape=[
            jax.ShapeDtypeStruct((cols * width_x, width_y), F32),
            jax.ShapeDtypeStruct((cols, width_x * width_y), BF16),
        ],
        in_specs=[smem()] * 4 + [vmem()] * 7,
        out_specs=[vmem()] * 2,
        scratch_shapes=[field] * 3 + [table] * 4 + [own_table] * 3,
        name="filter",
    )(flags, mat_diag, mat_cond, cheb_coef, flat, cell_ids, even, odd, strip, strip_even, strip_odd)
    return smooth.reshape(adjoint.shape), low


def ring_order(size):
    return [0] + list(range(1, size, 2)) + list(range(2, size, 2))[::-1]


def gathered_product(low, rows):
    size = lax.axis_size("cr")
    order = ring_order(size)
    me = lax.axis_index("cr")
    hop = [(order[i], order[(i + 1) % size]) for i in range(size)] if size > 1 else []
    before = [0] * size
    for a, b in hop:
        before[b] = a
    table = jnp.array(before, jnp.int32)
    products = []
    owners = []
    owner = me
    piece = low
    for step in range(size):
        following = lax.ppermute(piece, "cr", hop) if step < size - 1 else None
        products.append(
            lax.dot_general(piece, rows, (((1,), (1,)), ((), ())), preferred_element_type=F32)
        )
        owners.append(owner)
        piece = following
        owner = table[owner]
    return products, owners


def reduced(products, owners):
    size = len(products)
    cols, n_rows = products[0].shape
    size_x = lax.axis_size("sx")
    size_y = lax.axis_size("sy")
    plane = size_x * size_y
    share = size * cols // plane
    whole = jnp.zeros((size, cols, n_rows), F32)
    for product, owner in zip(products, owners):
        whole = lax.dynamic_update_slice(whole, product[None], (owner, 0, 0))
    whole = whole.reshape(size_x // 2, 2, size_y, share, n_rows)
    core = lax.axis_index("sx") % 2
    keep = lax.dynamic_index_in_dim(whole, core, 1, keepdims=False)
    send = lax.dynamic_index_in_dim(whole, 1 - core, 1, keepdims=False).astype(BF16)
    half = pairing(0, None, size_x, size_y)
    total = keep + lax.ppermute(send, ("sx", "sy"), half).astype(F32)
    total = total.reshape(plane // 2, share, n_rows)
    sy = lax.axis_index("sy")
    spot = (lax.axis_index("sx") // 2) * size_y + sy
    mine = lax.dynamic_index_in_dim(total, spot, 0, keepdims=False)
    arrived = []
    for shift in range(1, plane // 2):
        pairs = []
        for i in range(size_x):
            for j in range(size_y):
                other = ((i // 2) * size_y + j) ^ shift
                pairs.append((i * size_y + j, ((other // size_y) * 2 + i % 2) * size_y + other % size_y))
        out = lax.dynamic_index_in_dim(total, spot ^ shift, 0, keepdims=False).astype(BF16)
        arrived.append(lax.ppermute(out, ("sx", "sy"), pairs))
    for part in arrived:
        mine = mine + part.astype(F32)
    return mine.T


def on_device(adjoint, sensor_rows, cell_ids, mat_diag, mat_cond, cheb_coef):
    smoothed, low = filtered(adjoint, cell_ids, mat_diag, mat_cond, cheb_coef)
    rows = sensor_rows.reshape(sensor_rows.shape[0], -1)
    products, owners = gathered_product(low, rows)
    return smoothed, reduced(products, owners)


def solution(mesh):
    placed = (P("cr", "sx", "sy"), P("cr", "sx", "sy"), P("sx", "sy"), P(), P(), P())
    return jax.shard_map(
        on_device,
        mesh=mesh,
        in_specs=placed,
        out_specs=(P("cr", "sx", "sy"), P("cr", ("sx", "sy"))),
        check_vma=False,
    )
```

time: 195 us -> 83.1 us (0.43)
  waiting for transfers between devices: 74.9 us -> 24.8 us
  local copies, waits for them, and re-layouts: 38.9 us -> 5.27 us
  other arithmetic: 30.1 us -> 1.36 us
  Pallas kernels: 0 us -> 24.8 us
  starting transfers between devices: 32.8 us -> 13.9 us
  between operations: 14.6 us -> 6.43 us
  matrix products: 3.14 us -> 6.3 us
    all_gather x1 -> x0, waiting for transfers between devices: 33.2 us -> none  [on_device(): piece = lax.all_gather(lowered, 'cr', axis=0, tiled=True)]
    reduce_scatter x1 -> x0, waiting for transfers between devices: 32.8 us -> none  [on_device(): lax.psum_scatter(partial_panel, ('sx', 'sy'), scatter_dimension=1, tiled=...]
    pallas_call x0 -> x2, Pallas kernels: none -> 24.8 us  [the longest x1 22.6 us: filtered(): pl.pallas_call(functools.partial(filter_kernel, groups, width_x), out_sha...]
    slice x21 -> x0, local copies, waits for them, and re-layouts: 22.4 us -> none  [the longest x6 10.5 us: padded(): last = lax.slice_in_dim(value, length - width, length, axis=dim)]
    ppermute x12, starting transfers between devices: 32.7 us -> 13.9 us  [the longest x5 7.06 us: swap(): return lax.ppermute(value, ('sx', 'sy'), pairs)]
    ppermute x12, waiting for transfers between devices: 8.87 us -> 24.8 us  [the longest x3 19.8 us: gathered_product(): following = lax.ppermute(piece, 'cr', hop) if step < size - 1 else None]
    mul x8 -> x0, other arithmetic: 12.8 us -> none  [apply_inner(): weighted = cond * field]
    ppermute x4 -> x0, local copies, waits for them, and re-layouts: 10.4 us -> none  [the longest x2 5.25 us: padded(): before = lax.ppermute(last, axis, up)]
  transfers between devices with their start and end apart: 14 -> 12, of which waited for: 5 -> 7; matrix products, arithmetic and copies ran while one was open for 9% -> 11% of each run, Pallas kernels for 0% -> 0%
where the time goes in v1:
time: 83.1 us; the launch traced here: 82.8 us
  Pallas kernels  24.8 us (30%)
  waiting for transfers between devices  24.8 us (30%)
  starting transfers between devices  13.9 us (17%)
  between operations  6.43 us (8%)
  matrix products  6.3 us (8%)
  local copies, waits for them, and re-layouts  5.27 us (6%)
  other arithmetic  1.36 us (2%)
    pallas_call x1, Pallas kernels, filtered(): pl.pallas_call(functools.partial(filter_kernel, groups, width_x), out_sha...  22.6 us
    ppermute x3, waiting for transfers between devices, gathered_product(): following = lax.ppermute(piece, 'cr', hop) if step < size - 1 else None  19.8 us
    ppermute x5, starting transfers between devices, swap(): return lax.ppermute(value, ('sx', 'sy'), pairs)  7.06 us
    dot_general x4, matrix products, gathered_product(): lax.dot_general(piece, rows, (((1,), (1,)), ((), ())), preferred_element_...  6.3 us
    dynamic_slice x3, local copies, waits for them, and re-layouts, gathered_product(): owner = table[owner]  3.76 us
    ppermute x3, waiting for transfers between devices, reduced(): arrived.append(lax.ppermute(out, ('sx', 'sy'), pairs))  3.64 us
    ppermute x3, starting transfers between devices, reduced(): arrived.append(lax.ppermute(out, ('sx', 'sy'), pairs))  3.55 us
    ppermute x3, starting transfers between devices, gathered_product(): following = lax.ppermute(piece, 'cr', hop) if step < size - 1 else None  3.2 us
  transfers between devices with their start and end apart: 12, of which 7 were waited for; matrix products, arithmetic and copies ran while one was open for 11% of the time, Pallas kernels for 0%

profile of v1, /device:TPU:0, one launch (start us, length us, event | category | flops | bytes accessed | tf_op | source)
XLA Modules:
  0.0 82.8 jit_solution(6699605868752548189)
XLA Ops:
  0.7 0.7 pad_add_fusion.flags
  1.3 2.1 %pack.1 = (f32[65,8,128]{2,1,0:T(8,128)}, f32[65,8,128]{2,1,0:T(8,128)}, f32[18,8,128]{2,1,0:T(8,128)}, f32[9,8,128]{2,1,0:T(8,128)}, f32[9,8,128]{2,1,0:T(8,128)}) custom-call(s32[2]{0:T(128)} %pad_add_fusion.flags, f32[1024,128]{1,0:T(8,128)} %bitcast.77, s32[16,128]{1,0:T(8,128)} %ids_ref.3), custom_call_target="tpu_custom_call" | custom-call | tf_op jit(solution)/shard_map/pack/pallas_call | solution.py:249
  3.4 0.5 collective-permute-start
  3.9 0.7 collective-permute-start.1
  4.6 2.6 %collective-permute-start.2 = (f32[18,8,128]{2,1,0:T(8,128)}, f32[18,8,128]{2,1,0:T(8,128)S(1)}, u32[]{:S(2)}, u32[]{:S(2)}) collective-permute-start(f32[18,8,128]{2,1,0:T(8,128)} %get-tuple-element.11), channel_id=1, source_target_pairs={{0,4},{4,0},{8,12},{12,8},{16,20},{20,16},{24,28},{28,24},{1,5},{5... | collective-permute-start | bytes 221192 | tf_op jit(solution)/shard_map/ppermute | solution.py:261
  7.2 2.7 %collective-permute-start.3 = (f32[9,8,128]{2,1,0:T(8,128)}, f32[9,8,128]{2,1,0:T(8,128)S(1)}, u32[]{:S(2)}, u32[]{:S(2)}) collective-permute-start(f32[9,8,128]{2,1,0:T(8,128)} %get-tuple-element.12), channel_id=1, source_target_pairs={{0,12},{4,8},{8,4},{12,0},{16,28},{20,24},{24,20},{28,16},{1,13},{... | collective-permute-start | bytes 110600 | tf_op jit(solution)/shard_map/ppermute | solution.py:261
  9.9 0.7 collective-permute-start.4
  10.5 1.3 %dynamic_slice.29 = s32[1]{0:T(128)} dynamic-slice(s32[4]{0:T(128)} %constant.69.clone, s32[]{:T(128)S(6)} %select_n.54), dynamic_slice_sizes={1} | dynamic-slice | bytes 12 | tf_op jit(solution)/shard_map/dynamic_slice | solution.py:317
  13.6 1.3 %dynamic_slice.30 = s32[1]{0:T(128)} dynamic-slice(s32[4]{0:T(128)} %constant.69.clone, s32[]{:T(128)S(6)} %select_n.55), dynamic_slice_sizes={1} | dynamic-slice | bytes 12 | tf_op jit(solution)/shard_map/dynamic_slice | solution.py:317
  16.7 1.3 %dynamic_slice.31 = s32[1]{0:T(128)} dynamic-slice(s32[4]{0:T(128)} %constant.69.clone, s32[]{:T(128)S(6)} %select_n.56), dynamic_slice_sizes={1} | dynamic-slice | bytes 12 | tf_op jit(solution)/shard_map/dynamic_slice | solution.py:317
  20.0 0.5 copy-done.3
  20.6 0.1 copy-done
  20.7 0.7 copy-done.1
  21.4 22.6 %filter.1 = (f32[1024,128]{1,0:T(8,128)}, bf16[64,2048]{1,0:T(8,128)(2,1)}) custom-call(s32[2]{0:T(128)} %pad_add_fusion.flags, f32[16]{0:T(128)} %diag_ref.1, f32[16]{0:T(128)} %cond_ref.1, f32[9]{0:T(128)} %coef_ref.1, f32[1024,128]{1,0:T(8,128)} %bitcast.78, s32[16,128]{1,0:T(8,128)} %ids_ref.3, f32[65,8,128]{2,1,0:T(8,128)} %copy-done, ...), custom_call_target="tpu_custom_call" | custom-call | tf_op jit(solution)/shard_map/filter/pallas_call | solution.py:279
  44.0 1.6 %collective-permute-start.5 = (bf16[64,2048]{1,0:T(8,128)(2,1)}, bf16[64,2048]{1,0:T(8,128)(2,1)S(1)}, u32[]{:S(2)}, u32[]{:S(2)}) collective-permute-start(bf16[64,2048]{1,0:T(8,128)(2,1)} %get-tuple-element.15), channel_id=1, source_target_pairs={{0,1},{1,3},{3,2},{2,0},{4,5},{5,7},{7,6},{6,4},{8,9},{9,11},{11,1... | collective-permute-start | bytes 786440 | tf_op jit(solution)/shard_map/ppermute | solution.py:311
  45.6 3.1 %fusion.15 = f32[4,64,768]{2,1,0:T(8,128)S(1)} fusion(f32[4,64,768]{2,1,0:T(8,128)S(1)} %broadcast_in_dim.15, s32[]{:T(128)S(6)} %select_n.54, bf16[64,2048]{1,0:T(8,128)(2,1)} %get-tuple-element.15, bf16[96,8,16,128]{3,2,1,0:T(8,128)(2,1)} %bitcast.81), kind=kOutput, calls=%fused_computation.13 | convolution fusion | flops 201326592 | bytes 3604484 | tf_op jit(solution)/shard_map/dot_general | solution.py:313
  48.7 4.6 %collective-permute-done.5 = bf16[64,2048]{1,0:T(8,128)(2,1)S(1)} collective-permute-done((bf16[64,2048]{1,0:T(8,128)(2,1)}, bf16[64,2048]{1,0:T(8,128)(2,1)S(1)}, u32[]{:S(2)}, u32[]{:S(2)}) %collective-permute-start.5) | collective-permute-done | bytes 262176 | tf_op jit(solution)/shard_map/ppermute | solution.py:311
  53.3 0.8 %collective-permute-start.6 = (bf16[64,2048]{1,0:T(8,128)(2,1)S(1)}, bf16[64,2048]{1,0:T(8,128)(2,1)S(1)}, u32[]{:S(2)}, u32[]{:S(2)}) collective-permute-start(bf16[64,2048]{1,0:T(8,128)(2,1)S(1)} %collective-permute-done.5), channel_id=1, source_target_pairs={{0,1},{1,3},{3,2},{2,0},{4,5},{5,7},{7,6},{6,4},{8,9},{9,11},{11,1... | collective-permute-start | bytes 786440 | tf_op jit(solution)/shard_map/ppermute | solution.py:311
  54.1 1.1 %fusion.21 = f32[4,64,768]{2,1,0:T(8,128)S(1)} fusion(f32[4,64,768]{2,1,0:T(8,128)S(1)} %fusion.15, s32[]{:T(128)S(6)} %select_n.55, bf16[64,2048]{1,0:T(8,128)(2,1)S(1)} %collective-permute-done.5, bf16[96,8,16,128]{3,2,1,0:T(8,128)(2,1)S(1)} %bitcast.82), kind=kOutput, calls=%fused_computation.15 | convolution fusion | flops 201326592 | bytes 3604484 | tf_op jit(solution)/shard_map/dot_general | solution.py:313
  55.2 8.0 %collective-permute-done.6 = bf16[64,2048]{1,0:T(8,128)(2,1)S(1)} collective-permute-done((bf16[64,2048]{1,0:T(8,128)(2,1)S(1)}, bf16[64,2048]{1,0:T(8,128)(2,1)S(1)}, u32[]{:S(2)}, u32[]{:S(2)}) %collective-permute-start.6) | collective-permute-done | bytes 262176 | tf_op jit(solution)/shard_map/ppermute | solution.py:311
  63.2 0.8 collective-permute-start.7
  64.0 1.1 %fusion.27 = f32[4,64,768]{2,1,0:T(8,128)S(1)} fusion(f32[4,64,768]{2,1,0:T(8,128)S(1)} %fusion.21, s32[]{:T(128)S(6)} %select_n.56, bf16[64,2048]{1,0:T(8,128)(2,1)S(1)} %collective-permute-done.6, bf16[96,8,16,128]{3,2,1,0:T(8,128)(2,1)S(1)} %bitcast.83), kind=kOutput, calls=%fused_computation.17 | convolution fusion | flops 201326592 | bytes 3604484 | tf_op jit(solution)/shard_map/dot_general | solution.py:313
  65.1 7.2 %collective-permute-done.7 = bf16[64,2048]{1,0:T(8,128)(2,1)S(1)} collective-permute-done((bf16[64,2048]{1,0:T(8,128)(2,1)S(1)}, bf16[64,2048]{1,0:T(8,128)(2,1)S(1)}, u32[]{:S(2)}, u32[]{:S(2)}) %collective-permute-start.7) | collective-permute-done | bytes 262176 | tf_op jit(solution)/shard_map/ppermute | solution.py:311
  72.2 1.1 %fusion.33 = f32[4,64,768]{2,1,0:T(8,128)S(1)} fusion(f32[4,64,768]{2,1,0:T(8,128)S(1)} %fusion.27, s32[]{:T(128)S(6)} %select_n.57, bf16[64,2048]{1,0:T(8,128)(2,1)S(1)} %collective-permute-done.7, bf16[96,8,16,128]{3,2,1,0:T(8,128)(2,1)S(1)} %bitcast.84), kind=kOutput, calls=%fused_computation.19 | convolution fusion | flops 201326592 | bytes 3604484 | tf_op jit(solution)/shard_map/dot_general | solution.py:313
  73.4 0.1 collective-permute-start.8
  73.5 1.4 %collective-permute-done.8 = bf16[2,2,32,768]{3,2,1,0:T(8,128)(2,1)S(1)} collective-permute-done((bf16[2,2,32,768]{3,2,1,0:T(8,128)(2,1)S(1)}, bf16[2,2,32,768]{3,2,1,0:T(8,128)(2,1)S(1)}, u32[]{:S(2)}, u32[]{:S(2)}) %collective-permute-start.8) | collective-permute-done | bytes 196640 | tf_op jit(solution)/shard_map/ppermute | solution.py:336
  75.0 3.0 %collective-permute-start.10 = (bf16[32,768]{1,0:T(8,128)(2,1)S(1)}, bf16[32,768]{1,0:T(8,128)(2,1)S(1)}, u32[]{:S(2)}, u32[]{:S(2)}) collective-permute-start(bf16[32,768]{1,0:T(8,128)(2,1)S(1)} %get-tuple-element.18), channel_id=1, source_target_pairs={{0,16},{4,20},{8,24},{12,28},{16,0},{20,4},{24,8},{28,12},{1,17},{... | collective-permute-start | bytes 147464 | tf_op jit(solution)/shard_map/ppermute | solution.py:349
  78.0 0.5 collective-permute-start.9
  78.5 1.7 %collective-permute-done.11 = bf16[32,768]{1,0:T(8,128)(2,1)S(1)} collective-permute-done((bf16[32,768]{1,0:T(8,128)(2,1)S(1)}, bf16[32,768]{1,0:T(8,128)(2,1)S(1)}, u32[]{:S(2)}, u32[]{:S(2)}) %collective-permute-start.11) | collective-permute-done | bytes 49184 | tf_op jit(solution)/shard_map/ppermute | solution.py:349
  80.2 0.6 collective-permute-done.10
  80.9 1.3 %collective-permute-done.9 = bf16[32,768]{1,0:T(8,128)(2,1)S(1)} collective-permute-done((bf16[32,768]{1,0:T(8,128)(2,1)S(1)}, bf16[32,768]{1,0:T(8,128)(2,1)S(1)}, u32[]{:S(2)}, u32[]{:S(2)}) %collective-permute-start.9) | collective-permute-done | bytes 49184 | tf_op jit(solution)/shard_map/ppermute | solution.py:349
  82.1 0.7 fusion.39
  (19 shorter events, 0.3 us)
Async XLA Ops:
  3.4 16.5 %collective-permute-start = (f32[65,8,128]{2,1,0:T(8,128)}, f32[65,8,128]{2,1,0:T(8,128)S(1)}, u32[]{:S(2)}, u32[]{:S(2)}) collective-permute-start(f32[65,8,128]{2,1,0:T(8,128)} %get-tuple-element.9), channel_id=1, source_target_pairs={{0,8},{4,12},{8,0},{12,4},{16,24},{20,28},{24,16},{28,20},{1,9},{5... | collective-permute-start | bytes 798728 | tf_op jit(solution)/shard_map/ppermute | solution.py:261
  3.9 16.0 %collective-permute-start.1 = (f32[65,8,128]{2,1,0:T(8,128)}, f32[65,8,128]{2,1,0:T(8,128)S(1)}, u32[]{:S(2)}, u32[]{:S(2)}) collective-permute-start(f32[65,8,128]{2,1,0:T(8,128)} %get-tuple-element.10), channel_id=1, source_target_pairs={{8,16},{12,20},{16,8},{20,12},{9,17},{13,21},{17,9},{21,13},{10,18... | collective-permute-start | bytes 798728 | tf_op jit(solution)/shard_map/ppermute | solution.py:261
  4.6 15.3 %collective-permute-start.2 = (f32[18,8,128]{2,1,0:T(8,128)}, f32[18,8,128]{2,1,0:T(8,128)S(1)}, u32[]{:S(2)}, u32[]{:S(2)}) collective-permute-start(f32[18,8,128]{2,1,0:T(8,128)} %get-tuple-element.11), channel_id=1, source_target_pairs={{0,4},{4,0},{8,12},{12,8},{16,20},{20,16},{24,28},{28,24},{1,5},{5... | collective-permute-start | bytes 221192 | tf_op jit(solution)/shard_map/ppermute | solution.py:261
  7.2 12.7 %collective-permute-start.3 = (f32[9,8,128]{2,1,0:T(8,128)}, f32[9,8,128]{2,1,0:T(8,128)S(1)}, u32[]{:S(2)}, u32[]{:S(2)}) collective-permute-start(f32[9,8,128]{2,1,0:T(8,128)} %get-tuple-element.12), channel_id=1, source_target_pairs={{0,12},{4,8},{8,4},{12,0},{16,28},{20,24},{24,20},{28,16},{1,13},{... | collective-permute-start | bytes 110600 | tf_op jit(solution)/shard_map/ppermute | solution.py:261
  9.9 10.0 %collective-permute-start.4 = (f32[9,8,128]{2,1,0:T(8,128)}, f32[9,8,128]{2,1,0:T(8,128)S(1)}, u32[]{:S(2)}, u32[]{:S(2)}) collective-permute-start(f32[9,8,128]{2,1,0:T(8,128)} %get-tuple-element.13), channel_id=1, source_target_pairs={{8,20},{12,16},{16,12},{20,8},{9,21},{13,17},{17,13},{21,9},{10,22... | collective-permute-start | bytes 110600 | tf_op jit(solution)/shard_map/ppermute | solution.py:261
  19.9 0.6 copy-start.3
  19.9 0.6 copy-start.4
  19.9 0.6 copy-start.2
  19.9 0.7 copy-start
  20.7 0.7 copy-start.1
  44.0 10.2 %copy-start.5 = (bf16[768,16,128]{2,1,0:T(8,128)(2,1)S(1)}, bf16[768,16,128]{2,1,0:T(8,128)(2,1)}, u32[]{:S(2)}) copy-start(bf16[768,16,128]{2,1,0:T(8,128)(2,1)} %param.8) | copy-start | bytes 9437188
  44.0 9.3 %collective-permute-start.5 = (bf16[64,2048]{1,0:T(8,128)(2,1)}, bf16[64,2048]{1,0:T(8,128)(2,1)S(1)}, u32[]{:S(2)}, u32[]{:S(2)}) collective-permute-start(bf16[64,2048]{1,0:T(8,128)(2,1)} %get-tuple-element.15), channel_id=1, source_target_pairs={{0,1},{1,3},{3,2},{2,0},{4,5},{5,7},{7,6},{6,4},{8,9},{9,11},{11,1... | collective-permute-start | bytes 786440 | tf_op jit(solution)/shard_map/ppermute | solution.py:311
  53.3 9.9 %collective-permute-start.6 = (bf16[64,2048]{1,0:T(8,128)(2,1)S(1)}, bf16[64,2048]{1,0:T(8,128)(2,1)S(1)}, u32[]{:S(2)}, u32[]{:S(2)}) collective-permute-start(bf16[64,2048]{1,0:T(8,128)(2,1)S(1)} %collective-permute-done.5), channel_id=1, source_target_pairs={{0,1},{1,3},{3,2},{2,0},{4,5},{5,7},{7,6},{6,4},{8,9},{9,11},{11,1... | collective-permute-start | bytes 786440 | tf_op jit(solution)/shard_map/ppermute | solution.py:311
  63.2 9.1 %collective-permute-start.7 = (bf16[64,2048]{1,0:T(8,128)(2,1)S(1)}, bf16[64,2048]{1,0:T(8,128)(2,1)S(1)}, u32[]{:S(2)}, u32[]{:S(2)}) collective-permute-start(bf16[64,2048]{1,0:T(8,128)(2,1)S(1)} %collective-permute-done.6), channel_id=1, source_target_pairs={{0,1},{1,3},{3,2},{2,0},{4,5},{5,7},{7,6},{6,4},{8,9},{9,11},{11,1... | collective-permute-start | bytes 786440 | tf_op jit(solution)/shard_map/ppermute | solution.py:311
  73.4 1.5 %collective-permute-start.8 = (bf16[2,2,32,768]{3,2,1,0:T(8,128)(2,1)S(1)}, bf16[2,2,32,768]{3,2,1,0:T(8,128)(2,1)S(1)}, u32[]{:S(2)}, u32[]{:S(2)}) collective-permute-start(bf16[2,2,32,768]{3,2,1,0:T(8,128)(2,1)S(1)} %fusion.36), channel_id=1, source_target_pairs={{0,8},{4,12},{8,0},{12,4},{16,24},{20,28},{24,16},{28,20},{1,9},{5... | collective-permute-start | bytes 589832 | tf_op jit(solution)/shard_map/ppermute | solution.py:336
  74.9 5.3 %collective-permute-start.11 = (bf16[32,768]{1,0:T(8,128)(2,1)S(1)}, bf16[32,768]{1,0:T(8,128)(2,1)S(1)}, u32[]{:S(2)}, u32[]{:S(2)}) collective-permute-start(bf16[32,768]{1,0:T(8,128)(2,1)S(1)} %get-tuple-element.17), channel_id=1, source_target_pairs={{0,20},{4,16},{8,28},{12,24},{16,4},{20,0},{24,12},{28,8},{1,21},{... | collective-permute-start | bytes 147464 | tf_op jit(solution)/shard_map/ppermute | solution.py:349
  75.0 5.8 %collective-permute-start.10 = (bf16[32,768]{1,0:T(8,128)(2,1)S(1)}, bf16[32,768]{1,0:T(8,128)(2,1)S(1)}, u32[]{:S(2)}, u32[]{:S(2)}) collective-permute-start(bf16[32,768]{1,0:T(8,128)(2,1)S(1)} %get-tuple-element.18), channel_id=1, source_target_pairs={{0,16},{4,20},{8,24},{12,28},{16,0},{20,4},{24,8},{28,12},{1,17},{... | collective-permute-start | bytes 147464 | tf_op jit(solution)/shard_map/ppermute | solution.py:349
  78.0 4.1 %collective-permute-start.9 = (bf16[32,768]{1,0:T(8,128)(2,1)S(1)}, bf16[32,768]{1,0:T(8,128)(2,1)S(1)}, u32[]{:S(2)}, u32[]{:S(2)}) collective-permute-start(bf16[32,768]{1,0:T(8,128)(2,1)S(1)} %get-tuple-element.16), channel_id=1, source_target_pairs={{0,4},{4,0},{8,12},{12,8},{16,20},{20,16},{24,28},{28,24},{1,5},{5... | collective-permute-start | bytes 147464 | tf_op jit(solution)/shard_map/ppermute | solution.py:349

commit v2 on v1

v2 whole, which is shorter than its diff:
```python
import functools

import jax
import jax.numpy as jnp
from jax import lax
from jax.experimental import pallas as pl
from jax.experimental.pallas import tpu as pltpu
from jax.sharding import PartitionSpec as P

DEG = 8
SUB = 8
LANES = 128
SIDE = 2 * DEG
UNROLL = 4
CHUNKS = 2
VMEM_GRANT = 16 * 1024 * 1024
F32 = jnp.float32
BF16 = jnp.bfloat16


def partner(i, odd, size):
    j = i ^ 1 if not odd else ((i + 1) ^ 1) - 1
    return j if 0 <= j < size else None


def pairing(kind_x, kind_y, size_x, size_y):
    pairs = []
    for i in range(size_x):
        for j in range(size_y):
            a = i if kind_x is None else partner(i, kind_x, size_x)
            b = j if kind_y is None else partner(j, kind_y, size_y)
            if a is not None and b is not None:
                pairs.append((i * size_y + j, a * size_y + b))
    return pairs


def edge_lanes():
    place = lax.broadcasted_iota(jnp.int32, (SUB, LANES), 1) & (SIDE - 1)
    return jnp.where(place < DEG, DEG - 1 - place, LANES - 1 + DEG - place)


def lane_gather(tile, index):
    return jnp.take_along_axis(tile, index, axis=1, mode="promise_in_bounds")


def is_even(axis):
    return lax.axis_index(axis) % 2 == 0


def pack_kernel(groups, width_x, n_kinds, adj_ref, ids_ref, *out_refs):
    row_refs = out_refs[:2]
    strip_refs = out_refs[2:]
    upper_x = jnp.where(is_even("sx"), 1, 0)
    upper_y = jnp.where(is_even("sy"), 1, 0)
    index = edge_lanes()
    lane = lax.broadcasted_iota(jnp.int32, (SUB, LANES), 1)
    low_side = jnp.where((lane & (SIDE - 1)) < DEG, 1, 0)
    for which in range(2):
        upper = upper_x if which == 0 else 1 - upper_x
        base = pl.multiple_of(upper * (width_x - DEG), SUB)
        for row in range(DEG):
            for g in range(groups):
                row_refs[which][row * groups + g] = adj_ref[pl.ds(g * SUB * width_x + base + row, SUB, stride=width_x), :]
        row_refs[which][DEG * groups] = ids_ref[pl.ds(base, SUB), :].astype(F32) + 1.0
    for kind in range(n_kinds):
        upper = upper_y if kind == 0 else 1 - upper_y
        keep = (low_side ^ upper) == 1
        for row in range(width_x):
            strip = jnp.zeros((SUB, LANES), F32)
            for g in range(groups):
                tile = adj_ref[pl.ds(g * SUB * width_x + row, SUB, stride=width_x), :]
                strip = jnp.where((lane // SIDE) == g, lane_gather(tile, index), strip)
            strip_refs[3 * kind][row] = jnp.where(keep, strip, 0.0)
        for tile_x in range(width_x // SUB):
            ids = ids_ref[tile_x * SUB : (tile_x + 1) * SUB, :].astype(F32) + 1.0
            strip_refs[3 * kind][width_x + tile_x] = jnp.where(keep, lane_gather(ids, index), 0.0)
        for which in range(2):
            upper = upper_x if which == 0 else 1 - upper_x
            base = upper * (width_x - DEG)
            for row in range(DEG):
                strip_refs[3 * kind + 1 + which][row] = strip_refs[3 * kind][base + row]
            strip_refs[3 * kind + 1 + which][DEG] = strip_refs[3 * kind][width_x + upper * (width_x // SUB - 1)]


def power_terms():
    polys = [[1], [0, 1]]
    for _ in range(2, DEG + 1):
        doubled = [0] + [2 * t for t in polys[-1]]
        older = polys[-2] + [0] * (len(doubled) - len(polys[-2]))
        polys.append([p - q for p, q in zip(doubled, older)])
    return [[p[k] if k < len(p) else 0 for p in polys] for k in range(DEG + 1)]


def filter_kernel(
    groups, all_groups, offset, width_x, diag_ref, cond_ref, coef_ref, adj_ref, ids_ref, even_ref, odd_ref, strip_ref,
    strip_even_ref, strip_odd_ref, smooth_ref, low_ref, u_ref, a_ref, b_ref, cond_t, c2_t, d_t, cond_s, c2_s, d_s, inv_t,
):
    tall = width_x + 2 * DEG
    n_mat = diag_ref.shape[0]
    lane = lax.broadcasted_iota(jnp.int32, (SUB, LANES), 1)
    even_x = is_even("sx")
    power = []
    for terms in power_terms():
        parts = [coef_ref[j] if t == 1 else coef_ref[j] * float(t) for j, t in enumerate(terms) if t]
        power.append(functools.reduce(lambda p, q: p + q, parts))

    def lookup(ids, x0, cond_ref_t, c2_ref_t, d_ref_t):
        diag = jnp.zeros_like(ids)
        cond = jnp.zeros_like(ids)
        for m in range(n_mat):
            hit = ids == float(m + 1)
            diag = jnp.where(hit, diag_ref[m], diag)
            cond = jnp.where(hit, cond_ref[m], cond)
        cond_ref_t[x0 : x0 + SUB, :] = cond
        c2_ref_t[x0 : x0 + SUB, :] = cond * cond
        d_ref_t[x0 : x0 + SUB, :] = diag
        return cond

    def spread(ref, x):
        return ref[pl.ds(x, SUB, stride=0), :]

    repeat = lane & (SIDE - 1)
    for high in (False, True):
        x0 = tall - DEG if high else 0
        from_even = even_x if high else jnp.logical_not(even_x)
        ids = jnp.where(from_even, even_ref[DEG * all_groups], odd_ref[DEG * all_groups])
        lookup(ids, x0, cond_t, c2_t, d_t)
        ids = jnp.where(from_even, strip_even_ref[DEG], strip_odd_ref[DEG])
        lookup(lane_gather(ids, repeat), x0, cond_s, c2_s, d_s)
        for row in range(DEG):
            scale = spread(cond_t, x0 + row)
            for g in range(groups):
                at = row * all_groups + offset + g
                u_ref[x0 + row, g] = jnp.where(from_even, even_ref[at], odd_ref[at]) * scale
            tile = jnp.where(from_even, strip_even_ref[row], strip_odd_ref[row])
            u_ref[x0 + row, groups] = tile * spread(cond_s, x0 + row)
    for tile_x in range(width_x // SUB):
        x0 = DEG + tile_x * SUB
        cond = lookup(ids_ref[tile_x * SUB : (tile_x + 1) * SUB, :].astype(F32) + 1.0, x0, cond_t, c2_t, d_t)
        inv_t[tile_x * SUB : (tile_x + 1) * SUB, :] = 1.0 / cond
        lookup(lane_gather(strip_ref[width_x + tile_x], repeat), x0, cond_s, c2_s, d_s)
        for row in range(SUB):
            scale = spread(cond_t, x0 + row)
            for g in range(groups):
                start = (offset + g) * SUB * width_x + tile_x * SUB + row
                u_ref[x0 + row, g] = adj_ref[pl.ds(start, SUB, stride=width_x), :] * scale
            u_ref[x0 + row, groups] = strip_ref[tile_x * SUB + row] * spread(cond_s, x0 + row)

    first_lane = lane == 0
    last_lane = lane == LANES - 1
    place = lane & (SIDE - 1)
    at_high = place == DEG - 1
    at_low = place == DEG
    junction = lane // SIDE

    def across(tiles, strip, with_strip):
        sums = []
        meet = None
        for g, tile in enumerate(tiles):
            off = (offset + g) * SIDE + DEG
            edge = pltpu.roll(strip, LANES - off, 1)
            left = jnp.where(first_lane, edge, pltpu.roll(tile, 1, 1))
            right = jnp.where(last_lane, edge, pltpu.roll(tile, LANES - 1, 1))
            sums.append(left + right)
            if with_strip:
                moved = pltpu.roll(tile, off, 1)
                meet = moved if meet is None else jnp.where(junction == offset + g, moved, meet)
        if with_strip:
            up = jnp.where(at_high, meet, pltpu.roll(strip, LANES - 1, 1))
            down = jnp.where(at_low, meet, pltpu.roll(strip, 1, 1))
            sums.append(up + down)
        return sums

    def neighbours(src, x, count, with_strip):
        rows = [[src[x + r, g] for g in range(groups + 1)] for r in range(-1, count + 1)]
        out = []
        for r in range(1, count + 1):
            sums = across(rows[r][:groups], rows[r][groups], with_strip)
            sums = [s + (rows[r - 1][g] + rows[r + 1][g]) for g, s in enumerate(sums)]
            out.append((rows[r], sums))
        return out

    def swept(lo, body):
        n = tall - 2 * lo
        whole = n // UNROLL

        def run(i, carry):
            body(lo + i * UNROLL, UNROLL)
            return carry

        lax.fori_loop(0, whole, run, 0)
        if n % UNROLL:
            body(lo + whole * UNROLL, n % UNROLL)

    src = u_ref
    for order in range(DEG - 1, 0, -1):
        dst = a_ref if src is not a_ref else b_ref

        def body(x, count, order=order, src=src, dst=dst):
            for r, (tiles, sums) in enumerate(neighbours(src, x, count, True)):
                c2 = spread(c2_t, x + r)
                d = spread(d_t, x + r)
                c2s = spread(c2_s, x + r)
                ds = spread(d_s, x + r)
                for g in range(groups + 1):
                    cc, dd = (c2, d) if g < groups else (c2s, ds)
                    applied = dd * tiles[g] + cc * sums[g]
                    if order == DEG - 1:
                        value = power[order] * tiles[g] + power[DEG] * applied
                    else:
                        value = power[order] * u_ref[x + r, g] + applied
                    dst[x + r, g] = value

        swept(DEG - order, body)
        src = dst

    def last(x, count):
        for r, (tiles, sums) in enumerate(neighbours(src, x, count, False)):
            at = x + r - DEG
            cond = spread(cond_t, x + r)
            d = spread(d_t, x + r)
            inverse = spread(inv_t, at)
            out = []
            for g in range(groups):
                value = inverse * (power[0] * u_ref[x + r, g] + d * tiles[g]) + cond * sums[g]
                smooth_ref[pl.ds(g * SUB * width_x + at, SUB, stride=width_x), :] = value
                out.append(value)
            column = at * LANES if isinstance(at, int) else pl.multiple_of(at * LANES, LANES)
            for g in range(0, groups, 2):
                both = jnp.concatenate(out[g : g + 2], axis=0)
                low_ref[pl.ds(g * SUB, 2 * SUB), pl.ds(column, LANES)] = both.astype(BF16)

    swept(DEG, last)


def vmem():
    return pl.BlockSpec(memory_space=pltpu.VMEM)


def smem():
    return pl.BlockSpec(memory_space=pltpu.SMEM)


def filtered(adjoint, cell_ids, mat_diag, mat_cond, cheb_coef):
    cols, width_x, width_y = adjoint.shape
    groups = cols // SUB
    assert width_y == LANES and width_x % SUB == 0 and width_x >= DEG
    assert cols % SIDE == 0 and groups * SIDE <= LANES
    size_x = lax.axis_size("sx")
    size_y = lax.axis_size("sy")
    flat = adjoint.reshape(cols * width_x, width_y)
    n_kinds = 2 if size_y > 2 else 1
    row_shape = jax.ShapeDtypeStruct((DEG * groups + 1, SUB, LANES), F32)
    strip_shape = jax.ShapeDtypeStruct((width_x + width_x // SUB, SUB, LANES), F32)
    corner_shape = jax.ShapeDtypeStruct((DEG + 1, SUB, LANES), F32)
    packed = pl.pallas_call(
        functools.partial(pack_kernel, groups, width_x, n_kinds),
        out_shape=[row_shape] * 2 + [strip_shape, corner_shape, corner_shape] * n_kinds,
        in_specs=[vmem(), vmem()],
        out_specs=[vmem()] * (2 + 3 * n_kinds),
        compiler_params=pltpu.CompilerParams(vmem_limit_bytes=VMEM_GRANT),
        name="pack",
    )(flat, cell_ids)

    def swap(value, kind_x, kind_y):
        pairs = pairing(kind_x, kind_y, size_x, size_y)
        if not pairs:
            return jnp.zeros_like(value)
        return lax.ppermute(value, ("sx", "sy"), pairs)

    odd = swap(packed[1], 1, None)
    even = swap(packed[0], 0, None)
    strips = []
    for kind in range(n_kinds):
        strips.append(
            (
                swap(packed[2 + 3 * kind], None, kind),
                swap(packed[3 + 3 * kind], 0, kind),
                swap(packed[4 + 3 * kind], 1, kind),
            )
        )
    strip, strip_even, strip_odd = (functools.reduce(jnp.add, part) for part in zip(*strips))
    tall = width_x + 2 * DEG
    n_chunks = CHUNKS if groups % (2 * CHUNKS) == 0 else 1
    part = groups // n_chunks
    table = pltpu.VMEM((tall, LANES), F32)
    field = pltpu.VMEM((tall, part + 1, SUB, LANES), F32)
    smooth = []
    low = []
    for chunk in range(n_chunks):
        one, other = pl.pallas_call(
            functools.partial(filter_kernel, part, groups, chunk * part, width_x),
            out_shape=[
                jax.ShapeDtypeStruct((part * SUB * width_x, width_y), F32),
                jax.ShapeDtypeStruct((part * SUB, width_x * width_y), BF16),
            ],
            in_specs=[smem()] * 3 + [vmem()] * 7,
            out_specs=[vmem()] * 2,
            scratch_shapes=[field] * 3 + [table] * 6 + [pltpu.VMEM((width_x, LANES), F32)],
            compiler_params=pltpu.CompilerParams(vmem_limit_bytes=VMEM_GRANT),
            cost_estimate=pl.CostEstimate(flops=part * 3000000, bytes_accessed=part * 200000, transcendentals=0),
            name=f"filter{chunk}",
        )(mat_diag, mat_cond, cheb_coef, flat, cell_ids, even, odd, strip, strip_even, strip_odd)
        smooth.append(one)
        low.append(other)
    smooth = smooth[0] if n_chunks == 1 else jnp.concatenate(smooth)
    return smooth.reshape(adjoint.shape), low


def ring_order(size):
    return [0] + list(range(1, size, 2)) + list(range(2, size, 2))[::-1]


def stepped(before, me, steps):
    found = jnp.int32(0)
    for start in range(len(before)):
        spot = start
        for _ in range(steps):
            spot = before[spot]
        found = jnp.where(me == start, spot, found)
    return found


def gathered_product(low, rows):
    size = lax.axis_size("cr")
    order = ring_order(size)
    me = lax.axis_index("cr")
    hop = [(order[i], order[(i + 1) % size]) for i in range(size)] if size > 1 else []
    before = [0] * size
    for a, b in hop:
        before[b] = a
    products = []
    owners = []
    pieces = list(low)
    for step in range(size):
        following = [lax.ppermute(p, "cr", hop) for p in pieces] if step < size - 1 else None
        piece = pieces[0] if len(pieces) == 1 else jnp.concatenate(pieces)
        products.append(lax.dot_general(piece, rows, (((1,), (1,)), ((), ())), preferred_element_type=F32))
        owners.append(stepped(before, me, step))
        pieces = following
    return products, owners


def reduced(products, owners):
    size = len(products)
    cols, n_rows = products[0].shape
    size_x = lax.axis_size("sx")
    size_y = lax.axis_size("sy")
    plane = size_x * size_y
    share = size * cols // plane
    whole = jnp.zeros((size, cols, n_rows), F32)
    for product, owner in zip(products, owners):
        whole = lax.dynamic_update_slice(whole, product[None], (owner, 0, 0))
    whole = whole.reshape(size_x // 2, 2, size_y, share, n_rows)
    core = lax.axis_index("sx") % 2
    keep = lax.dynamic_index_in_dim(whole, core, 1, keepdims=False)
    send = lax.dynamic_index_in_dim(whole, 1 - core, 1, keepdims=False).astype(BF16)
    half = pairing(0, None, size_x, size_y)
    total = keep + lax.ppermute(send, ("sx", "sy"), half).astype(F32)
    total = total.reshape(plane // 2, share, n_rows)
    sy = lax.axis_index("sy")
    spot = (lax.axis_index("sx") // 2) * size_y + sy
    mine = lax.dynamic_index_in_dim(total, spot, 0, keepdims=False)
    arrived = []
    for shift in range(1, plane // 2):
        pairs = []
        for i in range(size_x):
            for j in range(size_y):
                other = ((i // 2) * size_y + j) ^ shift
                pairs.append((i * size_y + j, ((other // size_y) * 2 + i % 2) * size_y + other % size_y))
        out = lax.dynamic_index_in_dim(total, spot ^ shift, 0, keepdims=False).astype(BF16)
        arrived.append(lax.ppermute(out, ("sx", "sy"), pairs))
    for part in arrived:
        mine = mine + part.astype(F32)
    return mine.T


def on_device(adjoint, sensor_rows, cell_ids, mat_diag, mat_cond, cheb_coef):
    smoothed, low = filtered(adjoint, cell_ids, mat_diag, mat_cond, cheb_coef)
    rows = sensor_rows.reshape(sensor_rows.shape[0], -1)
    products, owners = gathered_product(low, rows)
    return smoothed, reduced(products, owners)


def solution(mesh):
    placed = (P("cr", "sx", "sy"), P("cr", "sx", "sy"), P("sx", "sy"), P(), P(), P())
    return jax.shard_map(
        on_device,
        mesh=mesh,
        in_specs=placed,
        out_specs=(P("cr", "sx", "sy"), P("cr", ("sx", "sy"))),
        check_vma=False,
    )
```

time: 83.1 us -> 66.6 us (0.80)
  Pallas kernels: 24.8 us -> 15.7 us
  waiting for transfers between devices: 24.8 us -> 16.1 us
  starting transfers between devices: 13.9 us -> 19.7 us
  between operations: 6.43 us -> 0.81 us
  local copies, waits for them, and re-layouts: 5.27 us -> 6.2 us
    ppermute x3 -> x6, waiting for transfers between devices: 19.8 us -> 11.2 us  [gathered_product(): lax.ppermute(p, 'cr', hop)]
    pallas_call x1 -> x2, Pallas kernels: 22.6 us -> 15.3 us  [filtered(): pl.pallas_call(functools.partial(filter_kernel, part, groups, chunk * par...]
    unnamed x12 -> x18, local copies, waits for them, and re-layouts: 1.4 us -> 6.09 us
    dynamic_slice x3 -> x0, local copies, waits for them, and re-layouts: 3.76 us -> none  [gathered_product(): owner = table[owner]]
    ppermute x3 -> x6, starting transfers between devices: 3.2 us -> 6.2 us  [gathered_product(): lax.ppermute(p, 'cr', hop)]
    ppermute x3, starting transfers between devices: 3.55 us -> 5.62 us  [reduced(): arrived.append(lax.ppermute(out, ('sx', 'sy'), pairs))]
    pallas_call x1, Pallas kernels: 2.13 us -> 0.39 us  [filtered(): pl.pallas_call(functools.partial(pack_kernel, groups, width_x, n_kinds),...]
    ppermute x5, waiting for transfers between devices: 0.01 us -> 1.72 us  [swap(): return lax.ppermute(value, ('sx', 'sy'), pairs)]
  transfers between devices with their start and end apart: 12 -> 15, of which waited for: 7 -> 8; matrix products, arithmetic and copies ran while one was open for 11% -> 9% of each run, Pallas kernels for 0% -> 12%
where the time goes in v2:
time: 66.6 us; the launch traced here: 66.2 us
  starting transfers between devices  19.7 us (30%)
  waiting for transfers between devices  16.1 us (24%)
  Pallas kernels  15.7 us (24%)
  matrix products  6.21 us (9%)
  local copies, waits for them, and re-layouts  6.2 us (9%)
  other arithmetic  1.53 us (2%)
  between operations  0.81 us (1%)
    pallas_call x2, Pallas kernels, filtered(): pl.pallas_call(functools.partial(filter_kernel, part, groups, chunk * par...  15.3 us
    ppermute x6, waiting for transfers between devices, gathered_product(): lax.ppermute(p, 'cr', hop)  11.2 us
    ppermute x5, starting transfers between devices, swap(): return lax.ppermute(value, ('sx', 'sy'), pairs)  7.09 us
    dot_general x4, matrix products, gathered_product(): lax.dot_general(piece, rows, (((1,), (1,)), ((), ())), preferred_element_...  6.21 us
    ppermute x6, starting transfers between devices, gathered_product(): lax.ppermute(p, 'cr', hop)  6.2 us
    unnamed x18, local copies, waits for them, and re-layouts  6.09 us
    ppermute x3, starting transfers between devices, reduced(): arrived.append(lax.ppermute(out, ('sx', 'sy'), pairs))  5.62 us
    ppermute x3, waiting for transfers between devices, reduced(): arrived.append(lax.ppermute(out, ('sx', 'sy'), pairs))  2.07 us
  transfers between devices with their start and end apart: 15, of which 8 were waited for; matrix products, arithmetic and copies ran while one was open for 9% of the time, Pallas kernels for 12%

profile of v2, /device:TPU:0, one launch (start us, length us, event | category | flops | bytes accessed | tf_op | source)
XLA Modules:
  0.0 66.2 jit_solution(15116570278901220480)
XLA Ops:
  0.6 1.0 %copy-done = f32[64,16,128]{2,1,0:T(8,128)S(1)} copy-done((f32[64,16,128]{2,1,0:T(8,128)S(1)}, f32[64,16,128]{2,1,0:T(8,128)}, u32[]{:S(2)}) %copy-start) | copy-done | bytes 524312
  1.7 0.7 %copy-done.2 = s32[16,128]{1,0:T(8,128)S(1)} copy-done((s32[16,128]{1,0:T(8,128)S(1)}, s32[16,128]{1,0:T(8,128)}, u32[]{:S(2)}) %copy-start.2) | copy-done | bytes 8216
  3.3 0.7 %collective-permute-start.1 = (f32[65,8,128]{2,1,0:T(8,128)S(1)}, f32[65,8,128]{2,1,0:T(8,128)S(1)}, u32[]{:S(2)}, u32[]{:S(2)}) collective-permute-start(f32[65,8,128]{2,1,0:T(8,128)S(1)} %get-tuple-element.12), channel_id=1, source_target_pairs={{8,16},{12,20},{16,8},{20,12},{9,17},{13,21},{17,9},{21,13},{10,18... | collective-permute-start | bytes 798728 | tf_op jit(solution)/shard_map/ppermute | solution.py:269
  3.9 2.6 %collective-permute-start.2 = (f32[18,8,128]{2,1,0:T(8,128)S(1)}, f32[18,8,128]{2,1,0:T(8,128)S(1)}, u32[]{:S(2)}, u32[]{:S(2)}) collective-permute-start(f32[18,8,128]{2,1,0:T(8,128)S(1)} %get-tuple-element.13), channel_id=1, source_target_pairs={{0,4},{4,0},{8,12},{12,8},{16,20},{20,16},{24,28},{28,24},{1,5},{5... | collective-permute-start | bytes 221192 | tf_op jit(solution)/shard_map/ppermute | solution.py:269
  6.5 2.7 %collective-permute-start.3 = (f32[9,8,128]{2,1,0:T(8,128)S(1)}, f32[9,8,128]{2,1,0:T(8,128)S(1)}, u32[]{:S(2)}, u32[]{:S(2)}) collective-permute-start(f32[9,8,128]{2,1,0:T(8,128)S(1)} %get-tuple-element.14), channel_id=1, source_target_pairs={{0,12},{4,8},{8,4},{12,0},{16,28},{20,24},{24,20},{28,16},{1,13},{... | collective-permute-start | bytes 110600 | tf_op jit(solution)/shard_map/ppermute | solution.py:269
  9.9 1.7 %collective-permute-done.3.strip_even_ref = f32[9,8,128]{2,1,0:T(8,128)S(1)} collective-permute-done((f32[9,8,128]{2,1,0:T(8,128)S(1)}, f32[9,8,128]{2,1,0:T(8,128)S(1)}, u32[]{:S(2)}, u32[]{:S(2)}) %collective-permute-start.3) | collective-permute-done | bytes 36896 | tf_op jit(solution)/shard_map/ppermute | solution.py:269
  11.7 1.0 %copy-done.1 = f32[64,16,128]{2,1,0:T(8,128)S(1)} copy-done((f32[64,16,128]{2,1,0:T(8,128)S(1)}, f32[64,16,128]{2,1,0:T(8,128)}, u32[]{:S(2)}) %copy-start.1) | copy-done | bytes 524312
  12.7 0.7 %copy-done.3 = s32[16,128]{1,0:T(8,128)S(1)} copy-done((s32[16,128]{1,0:T(8,128)S(1)}, s32[16,128]{1,0:T(8,128)}, u32[]{:S(2)}) %copy-start.3) | copy-done | bytes 8216
  13.4 0.7 copy-done.4
  14.1 0.7 copy-done.5
  15.4 7.6 %filter1.1 = (f32[512,128]{1,0:T(8,128)S(1)}, bf16[32,2048]{1,0:T(8,128)(2,1)S(1)}) custom-call(f32[16]{0:T(128)S(1)} %copy-done.4, f32[16]{0:T(128)S(1)} %copy-done.5, f32[9]{0:T(128)S(1)} %copy-done.6, f32[1024,128]{1,0:T(8,128)S(1)} %bitcast.67, s32[16,128]{1,0:T(8,128)S(1)} %copy-done.3, f32[65,8,128]{2,1,0:T(8,128)S(1)} %collective-permute-done.even_ref, ...), custom_call_target="tpu_custom_call" | custom-call | flops 12000000 | bytes 800000 | tf_op jit(solution)/shard_map/filter1/pallas_call | solution.py:291
  23.0 1.6 %collective-permute-start.6 = (bf16[32,2048]{1,0:T(8,128)(2,1)S(1)}, bf16[32,2048]{1,0:T(8,128)(2,1)S(1)}, u32[]{:S(2)}, u32[]{:S(2)}) collective-permute-start(bf16[32,2048]{1,0:T(8,128)(2,1)S(1)} %get-tuple-element.19), channel_id=1, source_target_pairs={{0,1},{1,3},{3,2},{2,0},{4,5},{5,7},{7,6},{6,4},{8,9},{9,11},{11,1... | collective-permute-start | bytes 393224 | tf_op jit(solution)/shard_map/ppermute | solution.py:336
  25.3 7.6 %filter0.1 = (f32[512,128]{1,0:T(8,128)S(1)}, bf16[32,2048]{1,0:T(8,128)(2,1)S(1)}) custom-call(f32[16]{0:T(128)S(1)} %copy-done.4, f32[16]{0:T(128)S(1)} %copy-done.5, f32[9]{0:T(128)S(1)} %copy-done.7, f32[1024,128]{1,0:T(8,128)S(1)} %bitcast.68, s32[16,128]{1,0:T(8,128)S(1)} %copy-done.3, f32[65,8,128]{2,1,0:T(8,128)S(1)} %collective-permute-done.even_ref, ...), custom_call_target="tpu_custom_call" | custom-call | flops 12000000 | bytes 800000 | tf_op jit(solution)/shard_map/filter0/pallas_call | solution.py:291
  32.9 2.6 %collective-permute-start.5 = (bf16[32,2048]{1,0:T(8,128)(2,1)S(1)}, bf16[32,2048]{1,0:T(8,128)(2,1)S(1)}, u32[]{:S(2)}, u32[]{:S(2)}) collective-permute-start(bf16[32,2048]{1,0:T(8,128)(2,1)S(1)} %get-tuple-element.18), channel_id=1, source_target_pairs={{0,1},{1,3},{3,2},{2,0},{4,5},{5,7},{7,6},{6,4},{8,9},{9,11},{11,1... | collective-permute-start | bytes 393224 | tf_op jit(solution)/shard_map/ppermute | solution.py:336
  35.6 3.0 %fusion.15 = f32[4,64,768]{2,1,0:T(8,128)S(1)} fusion(f32[4,64,768]{2,1,0:T(8,128)S(1)} %broadcast_in_dim.15, s32[]{:T(128)S(6)} %select_n.84, bf16[96,8,16,128]{3,2,1,0:T(8,128)(2,1)} %bitcast.74, bf16[32,2048]{1,0:T(8,128)(2,1)S(1)} %get-tuple-element.19, bf16[32,2048]{1,0:T(8,128)(2,1)S(1)} %get-tuple-element.18), kind=kOutput, calls=%fused_computation.13 | convolution fusion | flops 201850880 | bytes 3604484 | tf_op jit(solution)/shard_map/dot_general | solution.py:338
  39.1 1.4 %collective-permute-start.7 = (bf16[32,2048]{1,0:T(8,128)(2,1)S(1)}, bf16[32,2048]{1,0:T(8,128)(2,1)S(1)}, u32[]{:S(2)}, u32[]{:S(2)}) collective-permute-start(bf16[32,2048]{1,0:T(8,128)(2,1)S(1)} %collective-permute-done.5), channel_id=1, source_target_pairs={{0,1},{1,3},{3,2},{2,0},{4,5},{5,7},{7,6},{6,4},{8,9},{9,11},{11,1... | collective-permute-start | bytes 393224 | tf_op jit(solution)/shard_map/ppermute | solution.py:336
  40.6 1.1 %fusion.21 = f32[4,64,768]{2,1,0:T(8,128)S(1)} fusion(f32[4,64,768]{2,1,0:T(8,128)S(1)} %fusion.15, s32[]{:T(128)S(6)} %select_n.88, bf16[96,8,16,128]{3,2,1,0:T(8,128)(2,1)S(1)} %bitcast.75, bf16[32,2048]{1,0:T(8,128)(2,1)S(1)} %collective-permute-done.6, bf16[32,2048]{1,0:T(8,128)(2,1)S(1)} %collective-permute-done.5), kind=kOutput, calls=%fused_computation.15 | convolution fusion | flops 201850880 | bytes 3604484 | tf_op jit(solution)/shard_map/dot_general | solution.py:338
  41.6 2.9 %collective-permute-done.8 = bf16[32,2048]{1,0:T(8,128)(2,1)S(1)} collective-permute-done((bf16[32,2048]{1,0:T(8,128)(2,1)S(1)}, bf16[32,2048]{1,0:T(8,128)(2,1)S(1)}, u32[]{:S(2)}, u32[]{:S(2)}) %collective-permute-start.8) | collective-permute-done | bytes 131104 | tf_op jit(solution)/shard_map/ppermute | solution.py:336
  44.6 2.1 %collective-permute-done.7 = bf16[32,2048]{1,0:T(8,128)(2,1)S(1)} collective-permute-done((bf16[32,2048]{1,0:T(8,128)(2,1)S(1)}, bf16[32,2048]{1,0:T(8,128)(2,1)S(1)}, u32[]{:S(2)}, u32[]{:S(2)}) %collective-permute-start.7) | collective-permute-done | bytes 131104 | tf_op jit(solution)/shard_map/ppermute | solution.py:336
  46.7 1.1 %fusion.27 = f32[4,64,768]{2,1,0:T(8,128)S(1)} fusion(f32[4,64,768]{2,1,0:T(8,128)S(1)} %fusion.21, s32[]{:T(128)S(6)} %select_n.92, bf16[96,8,16,128]{3,2,1,0:T(8,128)(2,1)S(1)} %bitcast.76, bf16[32,2048]{1,0:T(8,128)(2,1)S(1)} %collective-permute-done.8, bf16[32,2048]{1,0:T(8,128)(2,1)S(1)} %collective-permute-done.7), kind=kOutput, calls=%fused_computation.17 | convolution fusion | flops 201850880 | bytes 3604484 | tf_op jit(solution)/shard_map/dot_general | solution.py:338
  47.8 2.7 %collective-permute-done.10 = bf16[32,2048]{1,0:T(8,128)(2,1)S(1)} collective-permute-done((bf16[32,2048]{1,0:T(8,128)(2,1)S(1)}, bf16[32,2048]{1,0:T(8,128)(2,1)S(1)}, u32[]{:S(2)}, u32[]{:S(2)}) %collective-permute-start.10) | collective-permute-done | bytes 131104 | tf_op jit(solution)/shard_map/ppermute | solution.py:336
  50.4 3.5 %collective-permute-done.9 = bf16[32,2048]{1,0:T(8,128)(2,1)S(1)} collective-permute-done((bf16[32,2048]{1,0:T(8,128)(2,1)S(1)}, bf16[32,2048]{1,0:T(8,128)(2,1)S(1)}, u32[]{:S(2)}, u32[]{:S(2)}) %collective-permute-start.9) | collective-permute-done | bytes 131104 | tf_op jit(solution)/shard_map/ppermute | solution.py:336
  53.9 1.1 %fusion.33 = f32[4,64,768]{2,1,0:T(8,128)S(1)} fusion(f32[4,64,768]{2,1,0:T(8,128)S(1)} %fusion.27, s32[]{:T(128)S(6)} %select_n.96, bf16[96,8,16,128]{3,2,1,0:T(8,128)(2,1)S(1)} %bitcast.77, bf16[32,2048]{1,0:T(8,128)(2,1)S(1)} %collective-permute-done.10, bf16[32,2048]{1,0:T(8,128)(2,1)S(1)} %collective-permute-done.9), kind=kOutput, calls=%fused_computation.19 | convolution fusion | flops 201850880 | bytes 3604484 | tf_op jit(solution)/shard_map/dot_general | solution.py:338
  55.1 0.8 %collective-permute-start.11 = (bf16[2,2,32,768]{3,2,1,0:T(8,128)(2,1)S(1)}, bf16[2,2,32,768]{3,2,1,0:T(8,128)(2,1)S(1)}, u32[]{:S(2)}, u32[]{:S(2)}) collective-permute-start(bf16[2,2,32,768]{3,2,1,0:T(8,128)(2,1)S(1)} %fusion.48), channel_id=1, source_target_pairs={{0,8},{4,12},{8,0},{12,4},{16,24},{20,28},{24,16},{28,20},{1,9},{5... | collective-permute-start | bytes 589832 | tf_op jit(solution)/shard_map/ppermute | solution.py:359
  55.9 1.1 %collective-permute-done.11 = bf16[2,2,32,768]{3,2,1,0:T(8,128)(2,1)S(1)} collective-permute-done((bf16[2,2,32,768]{3,2,1,0:T(8,128)(2,1)S(1)}, bf16[2,2,32,768]{3,2,1,0:T(8,128)(2,1)S(1)}, u32[]{:S(2)}, u32[]{:S(2)}) %collective-permute-start.11) | collective-permute-done | bytes 196640 | tf_op jit(solution)/shard_map/ppermute | solution.py:359
  57.0 3.0 %collective-permute-start.14 = (bf16[32,768]{1,0:T(8,128)(2,1)S(1)}, bf16[32,768]{1,0:T(8,128)(2,1)S(1)}, u32[]{:S(2)}, u32[]{:S(2)}) collective-permute-start(bf16[32,768]{1,0:T(8,128)(2,1)S(1)} %get-tuple-element.21), channel_id=1, source_target_pairs={{0,20},{4,16},{8,28},{12,24},{16,4},{20,0},{24,12},{28,8},{1,21},{... | collective-permute-start | bytes 147464 | tf_op jit(solution)/shard_map/ppermute | solution.py:372
  60.0 1.4 %collective-permute-start.13 = (bf16[32,768]{1,0:T(8,128)(2,1)S(1)}, bf16[32,768]{1,0:T(8,128)(2,1)S(1)}, u32[]{:S(2)}, u32[]{:S(2)}) collective-permute-start(bf16[32,768]{1,0:T(8,128)(2,1)S(1)} %get-tuple-element.22), channel_id=1, source_target_pairs={{0,16},{4,20},{8,24},{12,28},{16,0},{20,4},{24,8},{28,12},{1,17},{... | collective-permute-start | bytes 147464 | tf_op jit(solution)/shard_map/ppermute | solution.py:372
  61.5 1.2 %collective-permute-start.12 = (bf16[32,768]{1,0:T(8,128)(2,1)S(1)}, bf16[32,768]{1,0:T(8,128)(2,1)S(1)}, u32[]{:S(2)}, u32[]{:S(2)}) collective-permute-start(bf16[32,768]{1,0:T(8,128)(2,1)S(1)} %get-tuple-element.20), channel_id=1, source_target_pairs={{0,4},{4,0},{8,12},{12,8},{16,20},{20,16},{24,28},{28,24},{1,5},{5... | collective-permute-start | bytes 147464 | tf_op jit(solution)/shard_map/ppermute | solution.py:372
  62.7 0.8 %pad_maximum_fusion = f32[1024,128]{1,0:T(8,128)} fusion(f32[512,128]{1,0:T(8,128)S(1)} %get-tuple-element.17, f32[512,128]{1,0:T(8,128)S(1)} %get-tuple-element.16), kind=kLoop, calls=%fused_computation.20 | loop fusion | flops 131072 | bytes 1048576 | tf_op jit(solution)/shard_map/concatenate | solution.py:306
  63.5 0.8 %collective-permute-done.13 = bf16[32,768]{1,0:T(8,128)(2,1)S(1)} collective-permute-done((bf16[32,768]{1,0:T(8,128)(2,1)S(1)}, bf16[32,768]{1,0:T(8,128)(2,1)S(1)}, u32[]{:S(2)}, u32[]{:S(2)}) %collective-permute-start.13) | collective-permute-done | bytes 49184 | tf_op jit(solution)/shard_map/ppermute | solution.py:372
  64.3 1.3 %collective-permute-done.12 = bf16[32,768]{1,0:T(8,128)(2,1)S(1)} collective-permute-done((bf16[32,768]{1,0:T(8,128)(2,1)S(1)}, bf16[32,768]{1,0:T(8,128)(2,1)S(1)}, u32[]{:S(2)}, u32[]{:S(2)}) %collective-permute-start.12) | collective-permute-done | bytes 49184 | tf_op jit(solution)/shard_map/ppermute | solution.py:372
  65.5 0.7 %fusion.51 = f32[768,32]{0,1:T(8,128)} fusion(bf16[32,768]{1,0:T(8,128)(2,1)S(1)} %collective-permute-done.14, bf16[32,768]{1,0:T(8,128)(2,1)S(1)} %collective-permute-done.13, bf16[32,768]{1,0:T(8,128)(2,1)S(1)} %collective-permute-done.12, f32[4,32,768]{2,1,0:T(8,128)S(1)} %bitcast.72, s32[]{:T(128)S(6)} %select_n.101), kind=kLoop, calls=%fused_computation.39 | loop fusion | flops 147456 | bytes 344068 | tf_op jit(solution)/shard_map/transpose | solution.py:375
  (29 shorter events, 3.5 us)
Async XLA Ops:
  0.6 1.0 %copy-start = (f32[64,16,128]{2,1,0:T(8,128)S(1)}, f32[64,16,128]{2,1,0:T(8,128)}, u32[]{:S(2)}) copy-start(f32[64,16,128]{2,1,0:T(8,128)} %param.6) | copy-start | bytes 1572868
  1.7 0.7 %copy-start.2 = (s32[16,128]{1,0:T(8,128)S(1)}, s32[16,128]{1,0:T(8,128)}, u32[]{:S(2)}) copy-start(s32[16,128]{1,0:T(8,128)} %ids_ref.5) | copy-start | bytes 24580
  2.8 8.9 %collective-permute-start = (f32[65,8,128]{2,1,0:T(8,128)S(1)}, f32[65,8,128]{2,1,0:T(8,128)S(1)}, u32[]{:S(2)}, u32[]{:S(2)}) collective-permute-start(f32[65,8,128]{2,1,0:T(8,128)S(1)} %get-tuple-element.11), channel_id=1, source_target_pairs={{0,8},{4,12},{8,0},{12,4},{16,24},{20,28},{24,16},{28,20},{1,9},{5... | collective-permute-start | bytes 798728 | tf_op jit(solution)/shard_map/ppermute | solution.py:269
  3.3 8.4 %collective-permute-start.1 = (f32[65,8,128]{2,1,0:T(8,128)S(1)}, f32[65,8,128]{2,1,0:T(8,128)S(1)}, u32[]{:S(2)}, u32[]{:S(2)}) collective-permute-start(f32[65,8,128]{2,1,0:T(8,128)S(1)} %get-tuple-element.12), channel_id=1, source_target_pairs={{8,16},{12,20},{16,8},{20,12},{9,17},{13,21},{17,9},{21,13},{10,18... | collective-permute-start | bytes 798728 | tf_op jit(solution)/shard_map/ppermute | solution.py:269
  3.9 7.7 %collective-permute-start.2 = (f32[18,8,128]{2,1,0:T(8,128)S(1)}, f32[18,8,128]{2,1,0:T(8,128)S(1)}, u32[]{:S(2)}, u32[]{:S(2)}) collective-permute-start(f32[18,8,128]{2,1,0:T(8,128)S(1)} %get-tuple-element.13), channel_id=1, source_target_pairs={{0,4},{4,0},{8,12},{12,8},{16,20},{20,16},{24,28},{28,24},{1,5},{5... | collective-permute-start | bytes 221192 | tf_op jit(solution)/shard_map/ppermute | solution.py:269
  6.5 5.1 %collective-permute-start.3 = (f32[9,8,128]{2,1,0:T(8,128)S(1)}, f32[9,8,128]{2,1,0:T(8,128)S(1)}, u32[]{:S(2)}, u32[]{:S(2)}) collective-permute-start(f32[9,8,128]{2,1,0:T(8,128)S(1)} %get-tuple-element.14), channel_id=1, source_target_pairs={{0,12},{4,8},{8,4},{12,0},{16,28},{20,24},{24,20},{28,16},{1,13},{... | collective-permute-start | bytes 110600 | tf_op jit(solution)/shard_map/ppermute | solution.py:269
  9.2 2.4 %collective-permute-start.4 = (f32[9,8,128]{2,1,0:T(8,128)S(1)}, f32[9,8,128]{2,1,0:T(8,128)S(1)}, u32[]{:S(2)}, u32[]{:S(2)}) collective-permute-start(f32[9,8,128]{2,1,0:T(8,128)S(1)} %get-tuple-element.15), channel_id=1, source_target_pairs={{8,20},{12,16},{16,12},{20,8},{9,21},{13,17},{17,13},{21,9},{10,22... | collective-permute-start | bytes 110600 | tf_op jit(solution)/shard_map/ppermute | solution.py:269
  11.7 1.0 %copy-start.1 = (f32[64,16,128]{2,1,0:T(8,128)S(1)}, f32[64,16,128]{2,1,0:T(8,128)}, u32[]{:S(2)}) copy-start(f32[64,16,128]{2,1,0:T(8,128)} %param.6) | copy-start | bytes 1572868
  12.7 0.7 %copy-start.3 = (s32[16,128]{1,0:T(8,128)S(1)}, s32[16,128]{1,0:T(8,128)}, u32[]{:S(2)}) copy-start(s32[16,128]{1,0:T(8,128)} %ids_ref.5) | copy-start | bytes 24580
  13.4 0.7 copy-start.4
  14.1 0.7 copy-start.5
  14.7 0.7 copy-start.6
  23.0 15.6 %collective-permute-start.6 = (bf16[32,2048]{1,0:T(8,128)(2,1)S(1)}, bf16[32,2048]{1,0:T(8,128)(2,1)S(1)}, u32[]{:S(2)}, u32[]{:S(2)}) collective-permute-start(bf16[32,2048]{1,0:T(8,128)(2,1)S(1)} %get-tuple-element.19), channel_id=1, source_target_pairs={{0,1},{1,3},{3,2},{2,0},{4,5},{5,7},{7,6},{6,4},{8,9},{9,11},{11,1... | collective-permute-start | bytes 393224 | tf_op jit(solution)/shard_map/ppermute | solution.py:336
  24.6 0.7 copy-start.7
  25.3 15.3 %copy-start.8 = (bf16[768,16,128]{2,1,0:T(8,128)(2,1)S(1)}, bf16[768,16,128]{2,1,0:T(8,128)(2,1)}, u32[]{:S(2)}) copy-start(bf16[768,16,128]{2,1,0:T(8,128)(2,1)} %param.7) | copy-start | bytes 9437188
  32.9 6.2 %collective-permute-start.5 = (bf16[32,2048]{1,0:T(8,128)(2,1)S(1)}, bf16[32,2048]{1,0:T(8,128)(2,1)S(1)}, u32[]{:S(2)}, u32[]{:S(2)}) collective-permute-start(bf16[32,2048]{1,0:T(8,128)(2,1)S(1)} %get-tuple-element.18), channel_id=1, source_target_pairs={{0,1},{1,3},{3,2},{2,0},{4,5},{5,7},{7,6},{6,4},{8,9},{9,11},{11,1... | collective-permute-start | bytes 393224 | tf_op jit(solution)/shard_map/ppermute | solution.py:336
  38.6 5.9 %collective-permute-start.8 = (bf16[32,2048]{1,0:T(8,128)(2,1)S(1)}, bf16[32,2048]{1,0:T(8,128)(2,1)S(1)}, u32[]{:S(2)}, u32[]{:S(2)}) collective-permute-start(bf16[32,2048]{1,0:T(8,128)(2,1)S(1)} %collective-permute-done.6), channel_id=1, source_target_pairs={{0,1},{1,3},{3,2},{2,0},{4,5},{5,7},{7,6},{6,4},{8,9},{9,11},{11,1... | collective-permute-start | bytes 393224 | tf_op jit(solution)/shard_map/ppermute | solution.py:336
  39.1 7.5 %collective-permute-start.7 = (bf16[32,2048]{1,0:T(8,128)(2,1)S(1)}, bf16[32,2048]{1,0:T(8,128)(2,1)S(1)}, u32[]{:S(2)}, u32[]{:S(2)}) collective-permute-start(bf16[32,2048]{1,0:T(8,128)(2,1)S(1)} %collective-permute-done.5), channel_id=1, source_target_pairs={{0,1},{1,3},{3,2},{2,0},{4,5},{5,7},{7,6},{6,4},{8,9},{9,11},{11,1... | collective-permute-start | bytes 393224 | tf_op jit(solution)/shard_map/ppermute | solution.py:336
  44.6 5.9 %collective-permute-start.10 = (bf16[32,2048]{1,0:T(8,128)(2,1)S(1)}, bf16[32,2048]{1,0:T(8,128)(2,1)S(1)}, u32[]{:S(2)}, u32[]{:S(2)}) collective-permute-start(bf16[32,2048]{1,0:T(8,128)(2,1)S(1)} %collective-permute-done.8), channel_id=1, source_target_pairs={{0,1},{1,3},{3,2},{2,0},{4,5},{5,7},{7,6},{6,4},{8,9},{9,11},{11,1... | collective-permute-start | bytes 393224 | tf_op jit(solution)/shard_map/ppermute | solution.py:336
  46.7 7.3 %collective-permute-start.9 = (bf16[32,2048]{1,0:T(8,128)(2,1)S(1)}, bf16[32,2048]{1,0:T(8,128)(2,1)S(1)}, u32[]{:S(2)}, u32[]{:S(2)}) collective-permute-start(bf16[32,2048]{1,0:T(8,128)(2,1)S(1)} %collective-permute-done.7), channel_id=1, source_target_pairs={{0,1},{1,3},{3,2},{2,0},{4,5},{5,7},{7,6},{6,4},{8,9},{9,11},{11,1... | collective-permute-start | bytes 393224 | tf_op jit(solution)/shard_map/ppermute | solution.py:336
  55.1 1.9 %collective-permute-start.11 = (bf16[2,2,32,768]{3,2,1,0:T(8,128)(2,1)S(1)}, bf16[2,2,32,768]{3,2,1,0:T(8,128)(2,1)S(1)}, u32[]{:S(2)}, u32[]{:S(2)}) collective-permute-start(bf16[2,2,32,768]{3,2,1,0:T(8,128)(2,1)S(1)} %fusion.48), channel_id=1, source_target_pairs={{0,8},{4,12},{8,0},{12,4},{16,24},{20,28},{24,16},{28,20},{1,9},{5... | collective-permute-start | bytes 589832 | tf_op jit(solution)/shard_map/ppermute | solution.py:359
  57.0 6.5 %collective-permute-start.14 = (bf16[32,768]{1,0:T(8,128)(2,1)S(1)}, bf16[32,768]{1,0:T(8,128)(2,1)S(1)}, u32[]{:S(2)}, u32[]{:S(2)}) collective-permute-start(bf16[32,768]{1,0:T(8,128)(2,1)S(1)} %get-tuple-element.21), channel_id=1, source_target_pairs={{0,20},{4,16},{8,28},{12,24},{16,4},{20,0},{24,12},{28,8},{1,21},{... | collective-permute-start | bytes 147464 | tf_op jit(solution)/shard_map/ppermute | solution.py:372
  60.0 4.3 %collective-permute-start.13 = (bf16[32,768]{1,0:T(8,128)(2,1)S(1)}, bf16[32,768]{1,0:T(8,128)(2,1)S(1)}, u32[]{:S(2)}, u32[]{:S(2)}) collective-permute-start(bf16[32,768]{1,0:T(8,128)(2,1)S(1)} %get-tuple-element.22), channel_id=1, source_target_pairs={{0,16},{4,20},{8,24},{12,28},{16,0},{20,4},{24,8},{28,12},{1,17},{... | collective-permute-start | bytes 147464 | tf_op jit(solution)/shard_map/ppermute | solution.py:372
  61.5 4.1 %collective-permute-start.12 = (bf16[32,768]{1,0:T(8,128)(2,1)S(1)}, bf16[32,768]{1,0:T(8,128)(2,1)S(1)}, u32[]{:S(2)}, u32[]{:S(2)}) collective-permute-start(bf16[32,768]{1,0:T(8,128)(2,1)S(1)} %get-tuple-element.20), channel_id=1, source_target_pairs={{0,4},{4,0},{8,12},{12,8},{16,20},{20,16},{24,28},{28,24},{1,5},{5... | collective-permute-start | bytes 147464 | tf_op jit(solution)/shard_map/ppermute | solution.py:372

commit v3 on v2

--- a/solution.py
+++ b/solution.py
@@ -11,7 +11,7 @@
 SUB = 8
 LANES = 128
 SIDE = 2 * DEG
-UNROLL = 4
+UNROLL = 8
 CHUNKS = 2
 VMEM_GRANT = 16 * 1024 * 1024
 F32 = jnp.float32
@@ -47,9 +47,17 @@
     return lax.axis_index(axis) % 2 == 0
 
 
-def pack_kernel(groups, width_x, n_kinds, adj_ref, ids_ref, *out_refs):
-    row_refs = out_refs[:2]
-    strip_refs = out_refs[2:]
+def pack_kernel(groups, width_x, n_kinds, *refs):
+    adj_hbm, ids_hbm, diag_hbm, cond_hbm, coef_hbm, adj_ref, ids_ref, params_ref = refs[:8]
+    diag_ref, cond_ref, coef_ref, sem = refs[-4:]
+    row_refs = refs[8:10]
+    strip_refs = refs[10:-4]
+    pairs = ((adj_hbm, adj_ref), (ids_hbm, ids_ref), (diag_hbm, diag_ref), (cond_hbm, cond_ref), (coef_hbm, coef_ref))
+    copies = [pltpu.make_async_copy(src, dst, sem.at[i]) for i, (src, dst) in enumerate(pairs)]
+    for copy in copies:
+        copy.start()
+    for copy in copies:
+        copy.wait()
     upper_x = jnp.where(is_even("sx"), 1, 0)
     upper_y = jnp.where(is_even("sy"), 1, 0)
     index = edge_lanes()
@@ -80,6 +88,16 @@
             for row in range(DEG):
                 strip_refs[3 * kind + 1 + which][row] = strip_refs[3 * kind][base + row]
             strip_refs[3 * kind + 1 + which][DEG] = strip_refs[3 * kind][width_x + upper * (width_x // SUB - 1)]
+    for i, ref in enumerate((diag_ref, cond_ref)):
+        tile = jnp.zeros((SUB, LANES), F32)
+        for m in range(ref.shape[0]):
+            tile = jnp.where(lane == m + 1, ref[m], tile)
+        params_ref[i] = tile
+    tile = jnp.zeros((SUB, LANES), F32)
+    for k, terms in enumerate(power_terms()):
+        parts = [coef_ref[j] * float(t) for j, t in enumerate(terms) if t]
+        tile = jnp.where(lane == k, functools.reduce(lambda p, q: p + q, parts), tile)
+    params_ref[2] = tile
 
 
 def power_terms():
@@ -91,60 +109,32 @@
     return [[p[k] if k < len(p) else 0 for p in polys] for k in range(DEG + 1)]
 
 
-def filter_kernel(
-    groups, all_groups, offset, width_x, diag_ref, cond_ref, coef_ref, adj_ref, ids_ref, even_ref, odd_ref, strip_ref,
-    strip_even_ref, strip_odd_ref, smooth_ref, low_ref, u_ref, a_ref, b_ref, cond_t, c2_t, d_t, cond_s, c2_s, d_s, inv_t,
-):
+COND, COND2, DIAG, COND_S, COND2_S, DIAG_S, INVERSE = range(7)
+
+
+def filter_kernel(groups, all_groups, offset, width_x, first, *refs):
+    params_ref, adj_ref, ids_ref, even_ref, odd_ref, strip_ref, strip_even_ref, strip_odd_ref = refs[:8]
+    if first:
+        smooth_ref, low_ref, table = refs[8:11]
+    else:
+        table, smooth_ref, low_ref = refs[8:11]
+    u_ref, a_ref, b_ref, y_ref, power = refs[11:]
     tall = width_x + 2 * DEG
-    n_mat = diag_ref.shape[0]
     lane = lax.broadcasted_iota(jnp.int32, (SUB, LANES), 1)
     even_x = is_even("sx")
-    power = []
-    for terms in power_terms():
-        parts = [coef_ref[j] if t == 1 else coef_ref[j] * float(t) for j, t in enumerate(terms) if t]
-        power.append(functools.reduce(lambda p, q: p + q, parts))
-
-    def lookup(ids, x0, cond_ref_t, c2_ref_t, d_ref_t):
-        diag = jnp.zeros_like(ids)
-        cond = jnp.zeros_like(ids)
-        for m in range(n_mat):
-            hit = ids == float(m + 1)
-            diag = jnp.where(hit, diag_ref[m], diag)
-            cond = jnp.where(hit, cond_ref[m], cond)
-        cond_ref_t[x0 : x0 + SUB, :] = cond
-        c2_ref_t[x0 : x0 + SUB, :] = cond * cond
-        d_ref_t[x0 : x0 + SUB, :] = diag
+    for k in range(DEG + 1):
+        power[k] = lane_gather(params_ref[2], jnp.full((SUB, LANES), k, jnp.int32))
+
+    def lookup(ids, x0, strip):
+        ids = ids.astype(jnp.int32)
+        cond = lane_gather(params_ref[1], ids)
+        table[COND_S if strip else COND, x0 : x0 + SUB, :] = cond
+        table[COND2_S if strip else COND2, x0 : x0 + SUB, :] = cond * cond
+        table[DIAG_S if strip else DIAG, x0 : x0 + SUB, :] = lane_gather(params_ref[0], ids)
         return cond
 
-    def spread(ref, x):
-        return ref[pl.ds(x, SUB, stride=0), :]
-
-    repeat = lane & (SIDE - 1)
-    for high in (False, True):
-        x0 = tall - DEG if high else 0
-        from_even = even_x if high else jnp.logical_not(even_x)
-        ids = jnp.where(from_even, even_ref[DEG * all_groups], odd_ref[DEG * all_groups])
-        lookup(ids, x0, cond_t, c2_t, d_t)
-        ids = jnp.where(from_even, strip_even_ref[DEG], strip_odd_ref[DEG])
-        lookup(lane_gather(ids, repeat), x0, cond_s, c2_s, d_s)
-        for row in range(DEG):
-            scale = spread(cond_t, x0 + row)
-            for g in range(groups):
-                at = row * all_groups + offset + g
-                u_ref[x0 + row, g] = jnp.where(from_even, even_ref[at], odd_ref[at]) * scale
-            tile = jnp.where(from_even, strip_even_ref[row], strip_odd_ref[row])
-            u_ref[x0 + row, groups] = tile * spread(cond_s, x0 + row)
-    for tile_x in range(width_x // SUB):
-        x0 = DEG + tile_x * SUB
-        cond = lookup(ids_ref[tile_x * SUB : (tile_x + 1) * SUB, :].astype(F32) + 1.0, x0, cond_t, c2_t, d_t)
-        inv_t[tile_x * SUB : (tile_x + 1) * SUB, :] = 1.0 / cond
-        lookup(lane_gather(strip_ref[width_x + tile_x], repeat), x0, cond_s, c2_s, d_s)
-        for row in range(SUB):
-            scale = spread(cond_t, x0 + row)
-            for g in range(groups):
-                start = (offset + g) * SUB * width_x + tile_x * SUB + row
-                u_ref[x0 + row, g] = adj_ref[pl.ds(start, SUB, stride=width_x), :] * scale
-            u_ref[x0 + row, groups] = strip_ref[tile_x * SUB + row] * spread(cond_s, x0 + row)
+    def spread(which, x):
+        return table[which, pl.ds(x, SUB, stride=0), :]
 
     first_lane = lane == 0
     last_lane = lane == LANES - 1
@@ -153,76 +143,130 @@
     at_low = place == DEG
     junction = lane // SIDE
 
-    def across(tiles, strip, with_strip):
+    def across(tiles):
         sums = []
         meet = None
-        for g, tile in enumerate(tiles):
+        strip = tiles[groups]
+        for g, tile in enumerate(tiles[:groups]):
             off = (offset + g) * SIDE + DEG
             edge = pltpu.roll(strip, LANES - off, 1)
             left = jnp.where(first_lane, edge, pltpu.roll(tile, 1, 1))
             right = jnp.where(last_lane, edge, pltpu.roll(tile, LANES - 1, 1))
             sums.append(left + right)
-            if with_strip:
-                moved = pltpu.roll(tile, off, 1)
-                meet = moved if meet is None else jnp.where(junction == offset + g, moved, meet)
-        if with_strip:
-            up = jnp.where(at_high, meet, pltpu.roll(strip, LANES - 1, 1))
-            down = jnp.where(at_low, meet, pltpu.roll(strip, 1, 1))
-            sums.append(up + down)
+            moved = pltpu.roll(tile, off, 1)
+            meet = moved if meet is None else jnp.where(junction == offset + g, moved, meet)
+        up = jnp.where(at_high, meet, pltpu.roll(strip, LANES - 1, 1))
+        down = jnp.where(at_low, meet, pltpu.roll(strip, 1, 1))
+        sums.append(up + down)
         return sums
 
-    def neighbours(src, x, count, with_strip):
-        rows = [[src[x + r, g] for g in range(groups + 1)] for r in range(-1, count + 1)]
-        out = []
-        for r in range(1, count + 1):
-            sums = across(rows[r][:groups], rows[r][groups], with_strip)
-            sums = [s + (rows[r - 1][g] + rows[r + 1][g]) for g, s in enumerate(sums)]
-            out.append((rows[r], sums))
-        return out
-
-    def swept(lo, body):
+    def place_row(x, tiles):
+        for g in range(groups + 1):
+            u_ref[x, g] = tiles[g]
+        for g, total in enumerate(across(tiles)):
+            y_ref[x, g] = total
+
+    repeat = lane & (SIDE - 1)
+    if first:
+        for high in (False, True):
+            x0 = tall - DEG if high else 0
+            from_even = even_x if high else jnp.logical_not(even_x)
+            lookup(jnp.where(from_even, even_ref[DEG * all_groups], odd_ref[DEG * all_groups]), x0, False)
+            ids = jnp.where(from_even, strip_even_ref[DEG], strip_odd_ref[DEG])
+            lookup(lane_gather(ids, repeat), x0, True)
+        for tile_x in range(width_x // SUB):
+            x0 = DEG + tile_x * SUB
+            cond = lookup(ids_ref[tile_x * SUB : (tile_x + 1) * SUB, :] + 1, x0, False)
+            table[INVERSE, x0 : x0 + SUB, :] = 1.0 / cond
+            lookup(lane_gather(strip_ref[width_x + tile_x], repeat), x0, True)
+    for high in (False, True):
+        x0 = tall - DEG if high else 0
+        from_even = even_x if high else jnp.logical_not(even_x)
+        for row in range(DEG):
+            scale = spread(COND, x0 + row)
+            tiles = []
+            for g in range(groups):
+                at = row * all_groups + offset + g
+                tiles.append(jnp.where(from_even, even_ref[at], odd_ref[at]) * scale)
+            strip = jnp.where(from_even, strip_even_ref[row], strip_odd_ref[row])
+            place_row(x0 + row, tiles + [strip * spread(COND_S, x0 + row)])
+    for row in range(width_x):
+        x = DEG + row
+        scale = spread(COND, x)
+        tiles = []
+        for g in range(groups):
+            tiles.append(adj_ref[pl.ds((offset + g) * SUB * width_x + row, SUB, stride=width_x), :] * scale)
+        place_row(x, tiles + [strip_ref[row] * spread(COND_S, x)])
+
+    def swept(lo, body, after=None):
         n = tall - 2 * lo
-        whole = n // UNROLL
+        blocks = n // UNROLL
+        rest = n % UNROLL
+
+        def step(x, count, x_before, count_before):
+            body(x, count, None if after is None or not count_before else lambda: after(x_before, count_before))
+
+        step(lo, UNROLL, None, 0)
 
         def run(i, carry):
-            body(lo + i * UNROLL, UNROLL)
+            step(lo + i * UNROLL, UNROLL, lo + (i - 1) * UNROLL, UNROLL)
             return carry
 
-        lax.fori_loop(0, whole, run, 0)
-        if n % UNROLL:
-            body(lo + whole * UNROLL, n % UNROLL)
+        lax.fori_loop(1, blocks, run, 0)
+        x = lo + blocks * UNROLL
+        if rest:
+            step(x, rest, x - UNROLL, UNROLL)
+            if after is not None:
+                for store in after(x, rest):
+                    store()
+        elif after is not None:
+            for store in after(x - UNROLL, UNROLL):
+                store()
 
     src = u_ref
     for order in range(DEG - 1, 0, -1):
         dst = a_ref if src is not a_ref else b_ref
 
-        def body(x, count, order=order, src=src, dst=dst):
-            for r, (tiles, sums) in enumerate(neighbours(src, x, count, True)):
-                c2 = spread(c2_t, x + r)
-                d = spread(d_t, x + r)
-                c2s = spread(c2_s, x + r)
-                ds = spread(d_s, x + r)
+        def body(x, count, before, order=order, src=src, dst=dst):
+            rows = [[src[x + r, g] for g in range(groups + 1)] for r in range(-1, count + 1)]
+            sums = [[y_ref[x + r, g] for g in range(groups + 1)] for r in range(count)]
+            starts = rows[1:-1] if order == DEG - 1 else [[u_ref[x + r, g] for g in range(groups + 1)] for r in range(count)]
+            pending = before() if before is not None else []
+            coef = power[order]
+            for r in range(count):
+                c2, d, c2s, ds = (spread(which, x + r) for which in (COND2, DIAG, COND2_S, DIAG_S))
                 for g in range(groups + 1):
                     cc, dd = (c2, d) if g < groups else (c2s, ds)
-                    applied = dd * tiles[g] + cc * sums[g]
+                    total = sums[r][g] + (rows[r][g] + rows[r + 2][g])
+                    applied = dd * rows[r + 1][g] + cc * total
                     if order == DEG - 1:
-                        value = power[order] * tiles[g] + power[DEG] * applied
-                    else:
-                        value = power[order] * u_ref[x + r, g] + applied
-                    dst[x + r, g] = value
-
-        swept(DEG - order, body)
+                        applied = power[DEG] * applied
+                    dst[x + r, g] = coef * starts[r][g] + applied
+            for store in pending:
+                store()
+
+        def after(x, count, dst=dst):
+            rows = [[dst[x + r, g] for g in range(groups + 1)] for r in range(count)]
+            stores = []
+            for r in range(count):
+                for g, total in enumerate(across(rows[r])):
+                    def put(r=r, g=g, total=total):
+                        y_ref[x + r, g] = total
+                    stores.append(put)
+            return stores
+
+        swept(DEG - order, body, after)
         src = dst
 
-    def last(x, count):
-        for r, (tiles, sums) in enumerate(neighbours(src, x, count, False)):
+    def last(x, count, before):
+        rows = [[src[x + r, g] for g in range(groups)] for r in range(-1, count + 1)]
+        for r in range(count):
             at = x + r - DEG
-            cond = spread(cond_t, x + r)
-            d = spread(d_t, x + r)
-            inverse = spread(inv_t, at)
+            cond, d, inverse = (spread(which, x + r) for which in (COND, DIAG, INVERSE))
             out = []
             for g in range(groups):
-                value = inverse * (power[0] * u_ref[x + r, g] + d * tiles[g]) + cond * sums[g]
+                total = y_ref[x + r, g] + (rows[r][g] + rows[r + 2][g])
+                value = inverse * (power[0] * u_ref[x + r, g] + d * rows[r + 1][g]) + cond * total
                 smooth_ref[pl.ds(g * SUB * width_x + at, SUB, stride=width_x), :] = value
                 out.append(value)
             column = at * LANES if isinstance(at, int) else pl.multiple_of(at * LANES, LANES)
@@ -237,8 +281,8 @@
     return pl.BlockSpec(memory_space=pltpu.VMEM)
 
 
-def smem():
-    return pl.BlockSpec(memory_space=pltpu.SMEM)
+def hbm():
+    return pl.BlockSpec(memory_space=pltpu.HBM)
 
 
 def filtered(adjoint, cell_ids, mat_diag, mat_cond, cheb_coef):
@@ -253,14 +297,22 @@
     row_shape = jax.ShapeDtypeStruct((DEG * groups + 1, SUB, LANES), F32)
     strip_shape = jax.ShapeDtypeStruct((width_x + width_x // SUB, SUB, LANES), F32)
     corner_shape = jax.ShapeDtypeStruct((DEG + 1, SUB, LANES), F32)
-    packed = pl.pallas_call(
+    small = [pltpu.SMEM(v.shape, F32) for v in (mat_diag, mat_cond, cheb_coef)]
+    flat, ids, params, *packed = pl.pallas_call(
         functools.partial(pack_kernel, groups, width_x, n_kinds),
-        out_shape=[row_shape] * 2 + [strip_shape, corner_shape, corner_shape] * n_kinds,
-        in_specs=[vmem(), vmem()],
-        out_specs=[vmem()] * (2 + 3 * n_kinds),
+        out_shape=[
+            jax.ShapeDtypeStruct(flat.shape, F32),
+            jax.ShapeDtypeStruct(cell_ids.shape, jnp.int32),
+            jax.ShapeDtypeStruct((3, SUB, LANES), F32),
+        ]
+        + [row_shape] * 2
+        + [strip_shape, corner_shape, corner_shape] * n_kinds,
+        in_specs=[hbm()] * 5,
+        out_specs=[vmem()] * (5 + 3 * n_kinds),
+        scratch_shapes=small + [pltpu.SemaphoreType.DMA((5,))],
         compiler_params=pltpu.CompilerParams(vmem_limit_bytes=VMEM_GRANT),
         name="pack",
-    )(flat, cell_ids)
+    )(flat, cell_ids, mat_diag, mat_cond, cheb_coef)
 
     def swap(value, kind_x, kind_y):
         pairs = pairing(kind_x, kind_y, size_x, size_y)
@@ -283,26 +335,30 @@
     tall = width_x + 2 * DEG
     n_chunks = CHUNKS if groups % (2 * CHUNKS) == 0 else 1
     part = groups // n_chunks
-    table = pltpu.VMEM((tall, LANES), F32)
+    table_shape = jax.ShapeDtypeStruct((7, tall, LANES), F32)
     field = pltpu.VMEM((tall, part + 1, SUB, LANES), F32)
     smooth = []
     low = []
+    table = []
     for chunk in range(n_chunks):
-        one, other = pl.pallas_call(
-            functools.partial(filter_kernel, part, groups, chunk * part, width_x),
-            out_shape=[
-                jax.ShapeDtypeStruct((part * SUB * width_x, width_y), F32),
-                jax.ShapeDtypeStruct((part * SUB, width_x * width_y), BF16),
-            ],
-            in_specs=[smem()] * 3 + [vmem()] * 7,
-            out_specs=[vmem()] * 2,
-            scratch_shapes=[field] * 3 + [table] * 6 + [pltpu.VMEM((width_x, LANES), F32)],
+        out_shape = [
+            jax.ShapeDtypeStruct((part * SUB * width_x, width_y), F32),
+            jax.ShapeDtypeStruct((part * SUB, width_x * width_y), BF16),
+        ]
+        got = pl.pallas_call(
+            functools.partial(filter_kernel, part, groups, chunk * part, width_x, chunk == 0),
+            out_shape=out_shape + ([table_shape] if chunk == 0 else []),
+            in_specs=[vmem()] * (8 + len(table)),
+            out_specs=[vmem()] * (3 if chunk == 0 else 2),
+            scratch_shapes=[field] * 4 + [pltpu.VMEM((DEG + 1, SUB, LANES), F32)],
             compiler_params=pltpu.CompilerParams(vmem_limit_bytes=VMEM_GRANT),
             cost_estimate=pl.CostEstimate(flops=part * 3000000, bytes_accessed=part * 200000, transcendentals=0),
             name=f"filter{chunk}",
-        )(mat_diag, mat_cond, cheb_coef, flat, cell_ids, even, odd, strip, strip_even, strip_odd)
-        smooth.append(one)
-        low.append(other)
+        )(params, flat, ids, even, odd, strip, strip_even, strip_odd, *table)
+        smooth.append(got[0])
+        low.append(got[1])
+        if chunk == 0:
+            table = got[2:]
     smooth = smooth[0] if n_chunks == 1 else jnp.concatenate(smooth)
     return smooth.reshape(adjoint.shape), low
 

time: 66.6 us -> 58.1 us (0.87)
  Pallas kernels: 15.7 us -> 10.5 us
  starting transfers between devices: 19.7 us -> 23.4 us
  waiting for transfers between devices: 16.1 us -> 13.5 us
  local copies, waits for them, and re-layouts: 6.2 us -> 3.81 us
  matrix products: 6.21 us -> 4.32 us
    pallas_call x2, Pallas kernels: 15.3 us -> 9.5 us  [filtered(): pl.pallas_call(functools.partial(filter_kernel, part, groups, chunk * par...]
    ppermute x6, starting transfers between devices: 6.2 us -> 10.1 us  [gathered_product(): lax.ppermute(p, 'cr', hop)]
    ppermute x6, waiting for transfers between devices: 11.2 us -> 8.72 us  [gathered_product(): lax.ppermute(p, 'cr', hop)]
    unnamed x18 -> x12, local copies, waits for them, and re-layouts: 6.09 us -> 3.7 us
    dot_general x4, matrix products: 6.21 us -> 4.32 us  [gathered_product(): lax.dot_general(piece, rows, (((1,), (1,)), ((), ())), preferred_element_...]
  transfers between devices with their start and end apart: 15 -> 15, of which waited for: 8 -> 10; matrix products, arithmetic and copies ran while one was open for 9% -> 7% of each run, Pallas kernels for 12% -> 0%
where the time goes in v3:
time: 58.1 us; the launch traced here: 57.8 us
  starting transfers between devices  23.4 us (40%)
  waiting for transfers between devices  13.5 us (23%)
  Pallas kernels  10.5 us (18%)
  matrix products  4.32 us (7%)
  local copies, waits for them, and re-layouts  3.81 us (7%)
  other arithmetic  1.53 us (3%)
  between operations  0.81 us (1%)
    ppermute x6, starting transfers between devices, gathered_product(): lax.ppermute(p, 'cr', hop)  10.1 us
    pallas_call x2, Pallas kernels, filtered(): pl.pallas_call(functools.partial(filter_kernel, part, groups, chunk * par...  9.5 us
    ppermute x6, waiting for transfers between devices, gathered_product(): lax.ppermute(p, 'cr', hop)  8.72 us
    ppermute x5, starting transfers between devices, swap(): return lax.ppermute(value, ('sx', 'sy'), pairs)  7.14 us
    ppermute x3, starting transfers between devices, reduced(): arrived.append(lax.ppermute(out, ('sx', 'sy'), pairs))  5.81 us
    dot_general x4, matrix products, gathered_product(): lax.dot_general(piece, rows, (((1,), (1,)), ((), ())), preferred_element_...  4.32 us
    unnamed x12, local copies, waits for them, and re-layouts  3.7 us
    ppermute x3, waiting for transfers between devices, reduced(): arrived.append(lax.ppermute(out, ('sx', 'sy'), pairs))  1.87 us
  transfers between devices with their start and end apart: 15, of which 10 were waited for; matrix products, arithmetic and copies ran while one was open for 7% of the time, Pallas kernels for 0%

profile of v3, /device:TPU:0, one launch (start us, length us, event | category | flops | bytes accessed | tf_op | source)
XLA Modules:
  0.0 57.8 jit_solution(14907391222333610539)
XLA Ops:
  0.6 1.0 %copy-done = f32[64,16,128]{2,1,0:T(8,128)S(1)} copy-done((f32[64,16,128]{2,1,0:T(8,128)S(1)}, f32[64,16,128]{2,1,0:T(8,128)}, u32[]{:S(2)}) %copy-start) | copy-done | bytes 524312
  1.7 0.7 %copy-done.1 = s32[16,128]{1,0:T(8,128)S(1)} copy-done((s32[16,128]{1,0:T(8,128)S(1)}, s32[16,128]{1,0:T(8,128)}, u32[]{:S(2)}) %copy-start.1) | copy-done | bytes 8216
  2.4 0.7 %copy-done.2 = f32[16]{0:T(128)S(1)} copy-done((f32[16]{0:T(128)S(1)}, f32[16]{0:T(128)}, u32[]{:S(2)}) %copy-start.2) | copy-done | bytes 88
  3.7 0.7 %copy-done.4 = f32[9]{0:T(128)S(1)} copy-done((f32[9]{0:T(128)S(1)}, f32[9]{0:T(128)}, u32[]{:S(2)}) %copy-start.4) | copy-done | bytes 60
  4.3 1.0 %pack.1 = (f32[1024,128]{1,0:T(8,128)S(1)}, s32[16,128]{1,0:T(8,128)S(1)}, f32[3,8,128]{2,1,0:T(8,128)S(1)}, f32[65,8,128]{2,1,0:T(8,128)S(1)}, f32[65,8,128]{2,...) custom-call(f32[1024,128]{1,0:T(8,128)S(1)} %bitcast.66, ...), custom_call_target="tpu_custom_call" | custom-call | tf_op jit(solution)/shard_map/pack/pallas_call | solution.py:301
  5.9 0.7 %collective-permute-start.1 = (f32[65,8,128]{2,1,0:T(8,128)S(1)}, f32[65,8,128]{2,1,0:T(8,128)S(1)}, u32[]{:S(2)}, u32[]{:S(2)}) collective-permute-start(f32[65,8,128]{2,1,0:T(8,128)S(1)} %get-tuple-element.19), channel_id=1, source_target_pairs={{8,16},{12,20},{16,8},{20,12},{9,17},{13,21},{17,9},{21,13},{10,18... | collective-permute-start | bytes 798728 | tf_op jit(solution)/shard_map/ppermute | solution.py:321
  6.6 2.6 %collective-permute-start.2 = (f32[18,8,128]{2,1,0:T(8,128)S(1)}, f32[18,8,128]{2,1,0:T(8,128)S(1)}, u32[]{:S(2)}, u32[]{:S(2)}) collective-permute-start(f32[18,8,128]{2,1,0:T(8,128)S(1)} %get-tuple-element.20), channel_id=1, source_target_pairs={{0,4},{4,0},{8,12},{12,8},{16,20},{20,16},{24,28},{28,24},{1,5},{5... | collective-permute-start | bytes 221192 | tf_op jit(solution)/shard_map/ppermute | solution.py:321
  9.2 2.7 %collective-permute-start.3 = (f32[9,8,128]{2,1,0:T(8,128)S(1)}, f32[9,8,128]{2,1,0:T(8,128)S(1)}, u32[]{:S(2)}, u32[]{:S(2)}) collective-permute-start(f32[9,8,128]{2,1,0:T(8,128)S(1)} %get-tuple-element.21), channel_id=1, source_target_pairs={{0,12},{4,8},{8,4},{12,0},{16,28},{20,24},{24,20},{28,16},{1,13},{... | collective-permute-start | bytes 110600 | tf_op jit(solution)/shard_map/ppermute | solution.py:321
  12.6 1.7 %collective-permute-done.3.refs_6_ = f32[9,8,128]{2,1,0:T(8,128)S(1)} collective-permute-done((f32[9,8,128]{2,1,0:T(8,128)S(1)}, f32[9,8,128]{2,1,0:T(8,128)S(1)}, u32[]{:S(2)}, u32[]{:S(2)}) %collective-permute-start.3) | collective-permute-done | bytes 36896 | tf_op jit(solution)/shard_map/ppermute | solution.py:321
  14.3 4.8 %filter0.1 = (f32[512,128]{1,0:T(8,128)S(1)}, bf16[32,2048]{1,0:T(8,128)(2,1)S(1)}, f32[7,32,128]{2,1,0:T(8,128)S(1)}) custom-call(f32[3,8,128]{2,1,0:T(8,128)S(1)} %get-tuple-element.15.refs_0_, f32[1024,128]{1,0:T(8,128)S(1)} %get-tuple-element.16.refs_1_, s32[16,128]{1,0:T(8,128)S(1)} %get-tuple-element.17.refs_2_, ...), custom_call_target="tpu_custom_call" | custom-call | flops 12000000 | bytes 800000 | tf_op jit(solution)/shard_map/filter0/pallas_call | solution.py:348
  19.1 4.7 %filter1.1 = (f32[512,128]{1,0:T(8,128)S(1)}, bf16[32,2048]{1,0:T(8,128)(2,1)S(1)}) custom-call(f32[3,8,128]{2,1,0:T(8,128)S(1)} %get-tuple-element.15.refs_0_, f32[1024,128]{1,0:T(8,128)S(1)} %get-tuple-element.16.refs_1_, s32[16,128]{1,0:T(8,128)S(1)} %get-tuple-element.17.refs_2_, f32[65,8,128]{2,1,0:T(8,128)S(1)} %collective-permute-done.refs_3_, ...), custom_call_target="tpu_custom_call" | custom-call | flops 12000000 | bytes 800000 | tf_op jit(solution)/shard_map/filter1/pallas_call | solution.py:348
  23.8 1.6 %collective-permute-start.6 = (bf16[32,2048]{1,0:T(8,128)(2,1)S(1)}, bf16[32,2048]{1,0:T(8,128)(2,1)S(1)}, u32[]{:S(2)}, u32[]{:S(2)}) collective-permute-start(bf16[32,2048]{1,0:T(8,128)(2,1)S(1)} %get-tuple-element.27), channel_id=1, source_target_pairs={{0,1},{1,3},{3,2},{2,0},{4,5},{5,7},{7,6},{6,4},{8,9},{9,11},{11,1... | collective-permute-start | bytes 393224 | tf_op jit(solution)/shard_map/ppermute | solution.py:392
  25.4 2.6 %collective-permute-start.5 = (bf16[32,2048]{1,0:T(8,128)(2,1)S(1)}, bf16[32,2048]{1,0:T(8,128)(2,1)S(1)}, u32[]{:S(2)}, u32[]{:S(2)}) collective-permute-start(bf16[32,2048]{1,0:T(8,128)(2,1)S(1)} %get-tuple-element.26), channel_id=1, source_target_pairs={{0,1},{1,3},{3,2},{2,0},{4,5},{5,7},{7,6},{6,4},{8,9},{9,11},{11,1... | collective-permute-start | bytes 393224 | tf_op jit(solution)/shard_map/ppermute | solution.py:392
  28.1 1.1 %fusion.15 = f32[4,64,768]{2,1,0:T(8,128)S(1)} fusion(f32[4,64,768]{2,1,0:T(8,128)S(1)} %broadcast_in_dim.15, s32[]{:T(128)S(6)} %select_n.84, bf16[96,8,16,128]{3,2,1,0:T(8,128)(2,1)S(1)} %bitcast.72, bf16[32,2048]{1,0:T(8,128)(2,1)S(1)} %get-tuple-element.27, bf16[32,2048]{1,0:T(8,128)(2,1)S(1)} %get-tuple-element.26), kind=kOutput, calls=%fused_computation.13 | convolution fusion | flops 201850880 | bytes 3604484 | tf_op jit(solution)/shard_map/dot_general | solution.py:394
  29.7 0.8 %collective-permute-start.8 = (bf16[32,2048]{1,0:T(8,128)(2,1)S(1)}, bf16[32,2048]{1,0:T(8,128)(2,1)S(1)}, u32[]{:S(2)}, u32[]{:S(2)}) collective-permute-start(bf16[32,2048]{1,0:T(8,128)(2,1)S(1)} %collective-permute-done.6), channel_id=1, source_target_pairs={{0,1},{1,3},{3,2},{2,0},{4,5},{5,7},{7,6},{6,4},{8,9},{9,11},{11,1... | collective-permute-start | bytes 393224 | tf_op jit(solution)/shard_map/ppermute | solution.py:392
  30.5 1.3 %collective-permute-done.5 = bf16[32,2048]{1,0:T(8,128)(2,1)S(1)} collective-permute-done((bf16[32,2048]{1,0:T(8,128)(2,1)S(1)}, bf16[32,2048]{1,0:T(8,128)(2,1)S(1)}, u32[]{:S(2)}, u32[]{:S(2)}) %collective-permute-start.5) | collective-permute-done | bytes 131104 | tf_op jit(solution)/shard_map/ppermute | solution.py:392
  31.8 2.5 %collective-permute-start.7 = (bf16[32,2048]{1,0:T(8,128)(2,1)S(1)}, bf16[32,2048]{1,0:T(8,128)(2,1)S(1)}, u32[]{:S(2)}, u32[]{:S(2)}) collective-permute-start(bf16[32,2048]{1,0:T(8,128)(2,1)S(1)} %collective-permute-done.5), channel_id=1, source_target_pairs={{0,1},{1,3},{3,2},{2,0},{4,5},{5,7},{7,6},{6,4},{8,9},{9,11},{11,1... | collective-permute-start | bytes 393224 | tf_op jit(solution)/shard_map/ppermute | solution.py:392
  34.3 1.1 %fusion.21 = f32[4,64,768]{2,1,0:T(8,128)S(1)} fusion(f32[4,64,768]{2,1,0:T(8,128)S(1)} %fusion.15, s32[]{:T(128)S(6)} %select_n.88, bf16[96,8,16,128]{3,2,1,0:T(8,128)(2,1)S(1)} %bitcast.73, bf16[32,2048]{1,0:T(8,128)(2,1)S(1)} %collective-permute-done.6, bf16[32,2048]{1,0:T(8,128)(2,1)S(1)} %collective-permute-done.5), kind=kOutput, calls=%fused_computation.15 | convolution fusion | flops 201850880 | bytes 3604484 | tf_op jit(solution)/shard_map/dot_general | solution.py:394
  35.6 1.6 %collective-permute-start.10 = (bf16[32,2048]{1,0:T(8,128)(2,1)S(1)}, bf16[32,2048]{1,0:T(8,128)(2,1)S(1)}, u32[]{:S(2)}, u32[]{:S(2)}) collective-permute-start(bf16[32,2048]{1,0:T(8,128)(2,1)S(1)} %collective-permute-done.8), channel_id=1, source_target_pairs={{0,1},{1,3},{3,2},{2,0},{4,5},{5,7},{7,6},{6,4},{8,9},{9,11},{11,1... | collective-permute-start | bytes 393224 | tf_op jit(solution)/shard_map/ppermute | solution.py:392
  37.1 2.0 %collective-permute-done.7 = bf16[32,2048]{1,0:T(8,128)(2,1)S(1)} collective-permute-done((bf16[32,2048]{1,0:T(8,128)(2,1)S(1)}, bf16[32,2048]{1,0:T(8,128)(2,1)S(1)}, u32[]{:S(2)}, u32[]{:S(2)}) %collective-permute-start.7) | collective-permute-done | bytes 131104 | tf_op jit(solution)/shard_map/ppermute | solution.py:392
  39.1 1.0 %collective-permute-start.9 = (bf16[32,2048]{1,0:T(8,128)(2,1)S(1)}, bf16[32,2048]{1,0:T(8,128)(2,1)S(1)}, u32[]{:S(2)}, u32[]{:S(2)}) collective-permute-start(bf16[32,2048]{1,0:T(8,128)(2,1)S(1)} %collective-permute-done.7), channel_id=1, source_target_pairs={{0,1},{1,3},{3,2},{2,0},{4,5},{5,7},{7,6},{6,4},{8,9},{9,11},{11,1... | collective-permute-start | bytes 393224 | tf_op jit(solution)/shard_map/ppermute | solution.py:392
  40.2 1.1 %fusion.27 = f32[4,64,768]{2,1,0:T(8,128)S(1)} fusion(f32[4,64,768]{2,1,0:T(8,128)S(1)} %fusion.21, s32[]{:T(128)S(6)} %select_n.92, bf16[96,8,16,128]{3,2,1,0:T(8,128)(2,1)S(1)} %bitcast.74, bf16[32,2048]{1,0:T(8,128)(2,1)S(1)} %collective-permute-done.8, bf16[32,2048]{1,0:T(8,128)(2,1)S(1)} %collective-permute-done.7), kind=kOutput, calls=%fused_computation.17 | convolution fusion | flops 201850880 | bytes 3604484 | tf_op jit(solution)/shard_map/dot_general | solution.py:394
  41.6 4.3 %collective-permute-done.9 = bf16[32,2048]{1,0:T(8,128)(2,1)S(1)} collective-permute-done((bf16[32,2048]{1,0:T(8,128)(2,1)S(1)}, bf16[32,2048]{1,0:T(8,128)(2,1)S(1)}, u32[]{:S(2)}, u32[]{:S(2)}) %collective-permute-start.9) | collective-permute-done | bytes 131104 | tf_op jit(solution)/shard_map/ppermute | solution.py:392
  46.0 1.1 %fusion.33 = f32[4,64,768]{2,1,0:T(8,128)S(1)} fusion(f32[4,64,768]{2,1,0:T(8,128)S(1)} %fusion.27, s32[]{:T(128)S(6)} %select_n.96, bf16[96,8,16,128]{3,2,1,0:T(8,128)(2,1)S(1)} %bitcast.75, bf16[32,2048]{1,0:T(8,128)(2,1)S(1)} %collective-permute-done.10, bf16[32,2048]{1,0:T(8,128)(2,1)S(1)} %collective-permute-done.9), kind=kOutput, calls=%fused_computation.19 | convolution fusion | flops 201850880 | bytes 3604484 | tf_op jit(solution)/shard_map/dot_general | solution.py:394
  47.4 1.2 %collective-permute-done.11 = bf16[2,2,32,768]{3,2,1,0:T(8,128)(2,1)S(1)} collective-permute-done((bf16[2,2,32,768]{3,2,1,0:T(8,128)(2,1)S(1)}, bf16[2,2,32,768]{3,2,1,0:T(8,128)(2,1)S(1)}, u32[]{:S(2)}, u32[]{:S(2)}) %collective-permute-start.11) | collective-permute-done | bytes 196640 | tf_op jit(solution)/shard_map/ppermute | solution.py:415
  48.7 3.8 %collective-permute-start.14 = (bf16[32,768]{1,0:T(8,128)(2,1)S(1)}, bf16[32,768]{1,0:T(8,128)(2,1)S(1)}, u32[]{:S(2)}, u32[]{:S(2)}) collective-permute-start(bf16[32,768]{1,0:T(8,128)(2,1)S(1)} %get-tuple-element.29), channel_id=1, source_target_pairs={{0,20},{4,16},{8,28},{12,24},{16,4},{20,0},{24,12},{28,8},{1,21},{... | collective-permute-start | bytes 147464 | tf_op jit(solution)/shard_map/ppermute | solution.py:428
  52.4 0.7 %collective-permute-start.13 = (bf16[32,768]{1,0:T(8,128)(2,1)S(1)}, bf16[32,768]{1,0:T(8,128)(2,1)S(1)}, u32[]{:S(2)}, u32[]{:S(2)}) collective-permute-start(bf16[32,768]{1,0:T(8,128)(2,1)S(1)} %get-tuple-element.30), channel_id=1, source_target_pairs={{0,16},{4,20},{8,24},{12,28},{16,0},{20,4},{24,8},{28,12},{1,17},{... | collective-permute-start | bytes 147464 | tf_op jit(solution)/shard_map/ppermute | solution.py:428
  53.1 1.4 %collective-permute-start.12 = (bf16[32,768]{1,0:T(8,128)(2,1)S(1)}, bf16[32,768]{1,0:T(8,128)(2,1)S(1)}, u32[]{:S(2)}, u32[]{:S(2)}) collective-permute-start(bf16[32,768]{1,0:T(8,128)(2,1)S(1)} %get-tuple-element.28), channel_id=1, source_target_pairs={{0,4},{4,0},{8,12},{12,8},{16,20},{20,16},{24,28},{28,24},{1,5},{5... | collective-permute-start | bytes 147464 | tf_op jit(solution)/shard_map/ppermute | solution.py:428
  54.5 0.8 %pad_maximum_fusion = f32[1024,128]{1,0:T(8,128)} fusion(f32[512,128]{1,0:T(8,128)S(1)} %get-tuple-element.25, f32[512,128]{1,0:T(8,128)S(1)} %get-tuple-element.23), kind=kLoop, calls=%fused_computation.20 | loop fusion | flops 131072 | bytes 1048576 | tf_op jit(solution)/shard_map/concatenate | solution.py:362
  55.3 1.2 %collective-permute-done.13 = bf16[32,768]{1,0:T(8,128)(2,1)S(1)} collective-permute-done((bf16[32,768]{1,0:T(8,128)(2,1)S(1)}, bf16[32,768]{1,0:T(8,128)(2,1)S(1)}, u32[]{:S(2)}, u32[]{:S(2)}) %collective-permute-start.13) | collective-permute-done | bytes 49184 | tf_op jit(solution)/shard_map/ppermute | solution.py:428
  56.5 0.7 %collective-permute-done.12 = bf16[32,768]{1,0:T(8,128)(2,1)S(1)} collective-permute-done((bf16[32,768]{1,0:T(8,128)(2,1)S(1)}, bf16[32,768]{1,0:T(8,128)(2,1)S(1)}, u32[]{:S(2)}, u32[]{:S(2)}) %collective-permute-start.12) | collective-permute-done | bytes 49184 | tf_op jit(solution)/shard_map/ppermute | solution.py:428
  57.2 0.7 %fusion.51 = f32[768,32]{0,1:T(8,128)} fusion(bf16[32,768]{1,0:T(8,128)(2,1)S(1)} %collective-permute-done.14, bf16[32,768]{1,0:T(8,128)(2,1)S(1)} %collective-permute-done.13, bf16[32,768]{1,0:T(8,128)(2,1)S(1)} %collective-permute-done.12, f32[4,32,768]{2,1,0:T(8,128)S(1)} %bitcast.70, s32[]{:T(128)S(6)} %select_n.101), kind=kLoop, calls=%fused_computation.39 | loop fusion | flops 147456 | bytes 344068 | tf_op jit(solution)/shard_map/transpose | solution.py:431
  (23 shorter events, 3.5 us)
Async XLA Ops:
  0.6 1.0 %copy-start = (f32[64,16,128]{2,1,0:T(8,128)S(1)}, f32[64,16,128]{2,1,0:T(8,128)}, u32[]{:S(2)}) copy-start(f32[64,16,128]{2,1,0:T(8,128)} %param.6) | copy-start | bytes 1572868
  1.7 0.7 %copy-start.1 = (s32[16,128]{1,0:T(8,128)S(1)}, s32[16,128]{1,0:T(8,128)}, u32[]{:S(2)}) copy-start(s32[16,128]{1,0:T(8,128)} %refs_1_.1) | copy-start | bytes 24580
  2.4 0.7 %copy-start.2 = (f32[16]{0:T(128)S(1)}, f32[16]{0:T(128)}, u32[]{:S(2)}) copy-start(f32[16]{0:T(128)} %refs_2_.1) | copy-start | bytes 196
  3.0 0.7 %copy-start.3 = (f32[16]{0:T(128)S(1)}, f32[16]{0:T(128)}, u32[]{:S(2)}) copy-start(f32[16]{0:T(128)} %refs_3_.1) | copy-start | bytes 196
  3.7 0.7 %copy-start.4 = (f32[9]{0:T(128)S(1)}, f32[9]{0:T(128)}, u32[]{:S(2)}) copy-start(f32[9]{0:T(128)} %refs_4_.1) | copy-start | bytes 112
  5.3 8.9 %collective-permute-start = (f32[65,8,128]{2,1,0:T(8,128)S(1)}, f32[65,8,128]{2,1,0:T(8,128)S(1)}, u32[]{:S(2)}, u32[]{:S(2)}) collective-permute-start(f32[65,8,128]{2,1,0:T(8,128)S(1)} %get-tuple-element.18), channel_id=1, source_target_pairs={{0,8},{4,12},{8,0},{12,4},{16,24},{20,28},{24,16},{28,20},{1,9},{5... | collective-permute-start | bytes 798728 | tf_op jit(solution)/shard_map/ppermute | solution.py:321
  5.9 8.4 %collective-permute-start.1 = (f32[65,8,128]{2,1,0:T(8,128)S(1)}, f32[65,8,128]{2,1,0:T(8,128)S(1)}, u32[]{:S(2)}, u32[]{:S(2)}) collective-permute-start(f32[65,8,128]{2,1,0:T(8,128)S(1)} %get-tuple-element.19), channel_id=1, source_target_pairs={{8,16},{12,20},{16,8},{20,12},{9,17},{13,21},{17,9},{21,13},{10,18... | collective-permute-start | bytes 798728 | tf_op jit(solution)/shard_map/ppermute | solution.py:321
  6.6 7.7 %collective-permute-start.2 = (f32[18,8,128]{2,1,0:T(8,128)S(1)}, f32[18,8,128]{2,1,0:T(8,128)S(1)}, u32[]{:S(2)}, u32[]{:S(2)}) collective-permute-start(f32[18,8,128]{2,1,0:T(8,128)S(1)} %get-tuple-element.20), channel_id=1, source_target_pairs={{0,4},{4,0},{8,12},{12,8},{16,20},{20,16},{24,28},{28,24},{1,5},{5... | collective-permute-start | bytes 221192 | tf_op jit(solution)/shard_map/ppermute | solution.py:321
  9.2 5.1 %collective-permute-start.3 = (f32[9,8,128]{2,1,0:T(8,128)S(1)}, f32[9,8,128]{2,1,0:T(8,128)S(1)}, u32[]{:S(2)}, u32[]{:S(2)}) collective-permute-start(f32[9,8,128]{2,1,0:T(8,128)S(1)} %get-tuple-element.21), channel_id=1, source_target_pairs={{0,12},{4,8},{8,4},{12,0},{16,28},{20,24},{24,20},{28,16},{1,13},{... | collective-permute-start | bytes 110600 | tf_op jit(solution)/shard_map/ppermute | solution.py:321
  11.8 2.4 %collective-permute-start.4 = (f32[9,8,128]{2,1,0:T(8,128)S(1)}, f32[9,8,128]{2,1,0:T(8,128)S(1)}, u32[]{:S(2)}, u32[]{:S(2)}) collective-permute-start(f32[9,8,128]{2,1,0:T(8,128)S(1)} %get-tuple-element.22), channel_id=1, source_target_pairs={{8,20},{12,16},{16,12},{20,8},{9,21},{13,17},{17,13},{21,9},{10,22... | collective-permute-start | bytes 110600 | tf_op jit(solution)/shard_map/ppermute | solution.py:321
  12.6 15.5 %copy-start.5 = (bf16[768,16,128]{2,1,0:T(8,128)(2,1)S(1)}, bf16[768,16,128]{2,1,0:T(8,128)(2,1)}, u32[]{:S(2)}) copy-start(bf16[768,16,128]{2,1,0:T(8,128)(2,1)} %param.7) | copy-start | bytes 9437188
  23.8 5.9 %collective-permute-start.6 = (bf16[32,2048]{1,0:T(8,128)(2,1)S(1)}, bf16[32,2048]{1,0:T(8,128)(2,1)S(1)}, u32[]{:S(2)}, u32[]{:S(2)}) collective-permute-start(bf16[32,2048]{1,0:T(8,128)(2,1)S(1)} %get-tuple-element.27), channel_id=1, source_target_pairs={{0,1},{1,3},{3,2},{2,0},{4,5},{5,7},{7,6},{6,4},{8,9},{9,11},{11,1... | collective-permute-start | bytes 393224 | tf_op jit(solution)/shard_map/ppermute | solution.py:392
  25.4 6.4 %collective-permute-start.5 = (bf16[32,2048]{1,0:T(8,128)(2,1)S(1)}, bf16[32,2048]{1,0:T(8,128)(2,1)S(1)}, u32[]{:S(2)}, u32[]{:S(2)}) collective-permute-start(bf16[32,2048]{1,0:T(8,128)(2,1)S(1)} %get-tuple-element.26), channel_id=1, source_target_pairs={{0,1},{1,3},{3,2},{2,0},{4,5},{5,7},{7,6},{6,4},{8,9},{9,11},{11,1... | collective-permute-start | bytes 393224 | tf_op jit(solution)/shard_map/ppermute | solution.py:392
  29.7 5.9 %collective-permute-start.8 = (bf16[32,2048]{1,0:T(8,128)(2,1)S(1)}, bf16[32,2048]{1,0:T(8,128)(2,1)S(1)}, u32[]{:S(2)}, u32[]{:S(2)}) collective-permute-start(bf16[32,2048]{1,0:T(8,128)(2,1)S(1)} %collective-permute-done.6), channel_id=1, source_target_pairs={{0,1},{1,3},{3,2},{2,0},{4,5},{5,7},{7,6},{6,4},{8,9},{9,11},{11,1... | collective-permute-start | bytes 393224 | tf_op jit(solution)/shard_map/ppermute | solution.py:392
  31.8 7.3 %collective-permute-start.7 = (bf16[32,2048]{1,0:T(8,128)(2,1)S(1)}, bf16[32,2048]{1,0:T(8,128)(2,1)S(1)}, u32[]{:S(2)}, u32[]{:S(2)}) collective-permute-start(bf16[32,2048]{1,0:T(8,128)(2,1)S(1)} %collective-permute-done.5), channel_id=1, source_target_pairs={{0,1},{1,3},{3,2},{2,0},{4,5},{5,7},{7,6},{6,4},{8,9},{9,11},{11,1... | collective-permute-start | bytes 393224 | tf_op jit(solution)/shard_map/ppermute | solution.py:392
  35.6 6.0 %collective-permute-start.10 = (bf16[32,2048]{1,0:T(8,128)(2,1)S(1)}, bf16[32,2048]{1,0:T(8,128)(2,1)S(1)}, u32[]{:S(2)}, u32[]{:S(2)}) collective-permute-start(bf16[32,2048]{1,0:T(8,128)(2,1)S(1)} %collective-permute-done.8), channel_id=1, source_target_pairs={{0,1},{1,3},{3,2},{2,0},{4,5},{5,7},{7,6},{6,4},{8,9},{9,11},{11,1... | collective-permute-start | bytes 393224 | tf_op jit(solution)/shard_map/ppermute | solution.py:392
  39.1 6.8 %collective-permute-start.9 = (bf16[32,2048]{1,0:T(8,128)(2,1)S(1)}, bf16[32,2048]{1,0:T(8,128)(2,1)S(1)}, u32[]{:S(2)}, u32[]{:S(2)}) collective-permute-start(bf16[32,2048]{1,0:T(8,128)(2,1)S(1)} %collective-permute-done.7), channel_id=1, source_target_pairs={{0,1},{1,3},{3,2},{2,0},{4,5},{5,7},{7,6},{6,4},{8,9},{9,11},{11,1... | collective-permute-start | bytes 393224 | tf_op jit(solution)/shard_map/ppermute | solution.py:392
  47.1 1.5 %collective-permute-start.11 = (bf16[2,2,32,768]{3,2,1,0:T(8,128)(2,1)S(1)}, bf16[2,2,32,768]{3,2,1,0:T(8,128)(2,1)S(1)}, u32[]{:S(2)}, u32[]{:S(2)}) collective-permute-start(bf16[2,2,32,768]{3,2,1,0:T(8,128)(2,1)S(1)} %fusion.48), channel_id=1, source_target_pairs={{0,8},{4,12},{8,0},{12,4},{16,24},{20,28},{24,16},{28,20},{1,9},{5... | collective-permute-start | bytes 589832 | tf_op jit(solution)/shard_map/ppermute | solution.py:415
  48.7 6.6 %collective-permute-start.14 = (bf16[32,768]{1,0:T(8,128)(2,1)S(1)}, bf16[32,768]{1,0:T(8,128)(2,1)S(1)}, u32[]{:S(2)}, u32[]{:S(2)}) collective-permute-start(bf16[32,768]{1,0:T(8,128)(2,1)S(1)} %get-tuple-element.29), channel_id=1, source_target_pairs={{0,20},{4,16},{8,28},{12,24},{16,4},{20,0},{24,12},{28,8},{1,21},{... | collective-permute-start | bytes 147464 | tf_op jit(solution)/shard_map/ppermute | solution.py:428
  52.4 4.1 %collective-permute-start.13 = (bf16[32,768]{1,0:T(8,128)(2,1)S(1)}, bf16[32,768]{1,0:T(8,128)(2,1)S(1)}, u32[]{:S(2)}, u32[]{:S(2)}) collective-permute-start(bf16[32,768]{1,0:T(8,128)(2,1)S(1)} %get-tuple-element.30), channel_id=1, source_target_pairs={{0,16},{4,20},{8,24},{12,28},{16,0},{20,4},{24,8},{28,12},{1,17},{... | collective-permute-start | bytes 147464 | tf_op jit(solution)/shard_map/ppermute | solution.py:428
  53.1 4.1 %collective-permute-start.12 = (bf16[32,768]{1,0:T(8,128)(2,1)S(1)}, bf16[32,768]{1,0:T(8,128)(2,1)S(1)}, u32[]{:S(2)}, u32[]{:S(2)}) collective-permute-start(bf16[32,768]{1,0:T(8,128)(2,1)S(1)} %get-tuple-element.28), channel_id=1, source_target_pairs={{0,4},{4,0},{8,12},{12,8},{16,20},{20,16},{24,28},{28,24},{1,5},{5... | collective-permute-start | bytes 147464 | tf_op jit(solution)/shard_map/ppermute | solution.py:428

commit v4 on v3

--- a/solution.py
+++ b/solution.py
@@ -6,6 +6,7 @@
 from jax.experimental import pallas as pl
 from jax.experimental.pallas import tpu as pltpu
 from jax.sharding import PartitionSpec as P
+
 
 DEG = 8
 SUB = 8
@@ -252,6 +253,7 @@
                 for g, total in enumerate(across(rows[r])):
                     def put(r=r, g=g, total=total):
                         y_ref[x + r, g] = total
+
                     stores.append(put)
             return stores
 
@@ -312,7 +314,7 @@
         scratch_shapes=small + [pltpu.SemaphoreType.DMA((5,))],
         compiler_params=pltpu.CompilerParams(vmem_limit_bytes=VMEM_GRANT),
         name="pack",
-    )(flat, cell_ids, mat_diag, mat_cond, cheb_coef)
+    )(*(pltpu.with_memory_space_constraint(v, pltpu.HBM) for v in (flat, cell_ids, mat_diag, mat_cond, cheb_coef)))
 
     def swap(value, kind_x, kind_y):
         pairs = pairing(kind_x, kind_y, size_x, size_y)
@@ -335,30 +337,36 @@
     tall = width_x + 2 * DEG
     n_chunks = CHUNKS if groups % (2 * CHUNKS) == 0 else 1
     part = groups // n_chunks
-    table_shape = jax.ShapeDtypeStruct((7, tall, LANES), F32)
     field = pltpu.VMEM((tall, part + 1, SUB, LANES), F32)
     smooth = []
     low = []
-    table = []
     for chunk in range(n_chunks):
         out_shape = [
-            jax.ShapeDtypeStruct((part * SUB * width_x, width_y), F32),
-            jax.ShapeDtypeStruct((part * SUB, width_x * width_y), BF16),
+            pltpu.VMEM((part * SUB * width_x, width_y), F32),
+            pltpu.VMEM((part * SUB, width_x * width_y), BF16),
         ]
-        got = pl.pallas_call(
+        scratch = [field] * 4 + [pltpu.VMEM((DEG + 1, SUB, LANES), F32)]
+        operands = [params, flat, ids, even, odd, strip, strip_even, strip_odd]
+        in_specs = [vmem()] * 8
+        if chunk == 0:
+            out_shape += [pltpu.VMEM((7, tall, LANES), F32)]
+        else:
+            operands += [table]
+            in_specs += [vmem()]
+        call = pl.pallas_call(
             functools.partial(filter_kernel, part, groups, chunk * part, width_x, chunk == 0),
-            out_shape=out_shape + ([table_shape] if chunk == 0 else []),
-            in_specs=[vmem()] * (8 + len(table)),
-            out_specs=[vmem()] * (3 if chunk == 0 else 2),
-            scratch_shapes=[field] * 4 + [pltpu.VMEM((DEG + 1, SUB, LANES), F32)],
+            out_shape=out_shape,
+            in_specs=in_specs,
+            out_specs=[vmem()] * len(out_shape),
+            scratch_shapes=scratch,
             compiler_params=pltpu.CompilerParams(vmem_limit_bytes=VMEM_GRANT),
             cost_estimate=pl.CostEstimate(flops=part * 3000000, bytes_accessed=part * 200000, transcendentals=0),
-            name=f"filter{chunk}",
-        )(params, flat, ids, even, odd, strip, strip_even, strip_odd, *table)
+        )
+        got = call(*operands)
         smooth.append(got[0])
         low.append(got[1])
         if chunk == 0:
-            table = got[2:]
+            table = got[2]
     smooth = smooth[0] if n_chunks == 1 else jnp.concatenate(smooth)
     return smooth.reshape(adjoint.shape), low
 
@@ -385,28 +393,26 @@
     before = [0] * size
     for a, b in hop:
         before[b] = a
-    products = []
-    owners = []
     pieces = list(low)
+    whole = jnp.zeros((size, sum(p.shape[0] for p in pieces), rows.shape[0]), F32)
     for step in range(size):
-        following = [lax.ppermute(p, "cr", hop) for p in pieces] if step < size - 1 else None
+        following = []
+        if step < size - 1:
+            for piece in pieces:
+                following.append(lax.ppermute(piece, "cr", hop))
         piece = pieces[0] if len(pieces) == 1 else jnp.concatenate(pieces)
-        products.append(lax.dot_general(piece, rows, (((1,), (1,)), ((), ())), preferred_element_type=F32))
-        owners.append(stepped(before, me, step))
+        product = lax.dot_general(piece, rows, (((1,), (1,)), ((), ())), preferred_element_type=F32)
+        whole = lax.dynamic_update_slice(whole, product[None], (stepped(before, me, step), 0, 0))
         pieces = following
-    return products, owners
-
-
-def reduced(products, owners):
-    size = len(products)
-    cols, n_rows = products[0].shape
+    return whole
+
+
+def reduced(whole):
+    size, cols, n_rows = whole.shape
     size_x = lax.axis_size("sx")
     size_y = lax.axis_size("sy")
     plane = size_x * size_y
     share = size * cols // plane
-    whole = jnp.zeros((size, cols, n_rows), F32)
-    for product, owner in zip(products, owners):
-        whole = lax.dynamic_update_slice(whole, product[None], (owner, 0, 0))
     whole = whole.reshape(size_x // 2, 2, size_y, share, n_rows)
     core = lax.axis_index("sx") % 2
     keep = lax.dynamic_index_in_dim(whole, core, 1, keepdims=False)
@@ -434,8 +440,7 @@
 def on_device(adjoint, sensor_rows, cell_ids, mat_diag, mat_cond, cheb_coef):
     smoothed, low = filtered(adjoint, cell_ids, mat_diag, mat_cond, cheb_coef)
     rows = sensor_rows.reshape(sensor_rows.shape[0], -1)
-    products, owners = gathered_product(low, rows)
-    return smoothed, reduced(products, owners)
+    return smoothed, reduced(gathered_product(low, rows))
 
 
 def solution(mesh):

time: 58.1 us -> 54.8 us (0.943)
  local copies, waits for them, and re-layouts: 3.81 us -> 0.12 us
    unnamed x12 -> x2, local copies, waits for them, and re-layouts: 3.7 us -> 0.01 us
  transfers between devices with their start and end apart: 15 -> 15, of which waited for: 10 -> 10; matrix products, arithmetic and copies ran while one was open for 7% -> 8% of each run, Pallas kernels for 0% -> 0%
where the time goes in v4:
time: 54.8 us; the launch traced here: 54.6 us
  starting transfers between devices  23.4 us (43%)
  waiting for transfers between devices  13.5 us (25%)
  Pallas kernels  11 us (20%)
  matrix products  4.32 us (8%)
  other arithmetic  1.53 us (3%)
  between operations  0.8 us (1%)
    ppermute x6, starting transfers between devices, gathered_product(): following.append(lax.ppermute(piece, 'cr', hop))  10.1 us
    pallas_call x2, Pallas kernels, filtered(): got = call(*operands)  9.5 us
    ppermute x6, waiting for transfers between devices, gathered_product(): following.append(lax.ppermute(piece, 'cr', hop))  8.72 us
    ppermute x5, starting transfers between devices, swap(): return lax.ppermute(value, ('sx', 'sy'), pairs)  7.14 us
    ppermute x3, starting transfers between devices, reduced(): arrived.append(lax.ppermute(out, ('sx', 'sy'), pairs))  5.81 us
    dot_general x4, matrix products, gathered_product(): lax.dot_general(piece, rows, (((1,), (1,)), ((), ())), preferred_element_...  4.32 us
    ppermute x3, waiting for transfers between devices, reduced(): arrived.append(lax.ppermute(out, ('sx', 'sy'), pairs))  1.87 us
    ppermute x5, waiting for transfers between devices, swap(): return lax.ppermute(value, ('sx', 'sy'), pairs)  1.7 us
  transfers between devices with their start and end apart: 15, of which 10 were waited for; matrix products, arithmetic and copies ran while one was open for 8% of the time, Pallas kernels for 0%

profile of v4, /device:TPU:0, one launch (start us, length us, event | category | flops | bytes accessed | tf_op | source)
XLA Modules:
  0.0 54.6 jit_solution(6551244297366345491)
XLA Ops:
  0.6 1.5 %pack.1 = (f32[1024,128]{1,0:T(8,128)S(1)}, s32[16,128]{1,0:T(8,128)S(1)}, f32[3,8,128]{2,1,0:T(8,128)S(1)}, f32[65,8,128]{2,1,0:T(8,128)S(1)}, f32[65,8,128]{2,...) custom-call(f32[1024,128]{1,0:T(8,128)} %bitcast.70, ...), custom_call_target="tpu_custom_call" | custom-call | tf_op jit(solution)/shard_map/pack/pallas_call | solution.py:303
  2.1 0.6 %collective-permute-start = (f32[65,8,128]{2,1,0:T(8,128)S(1)}, f32[65,8,128]{2,1,0:T(8,128)S(1)}, u32[]{:S(2)}, u32[]{:S(2)}) collective-permute-start(f32[65,8,128]{2,1,0:T(8,128)S(1)} %get-tuple-element.18), channel_id=1, source_target_pairs={{0,8},{4,12},{8,0},{12,4},{16,24},{20,28},{24,16},{28,20},{1,9},{5... | collective-permute-start | bytes 798728 | tf_op jit(solution)/shard_map/ppermute | solution.py:323
  2.7 0.7 %collective-permute-start.1 = (f32[65,8,128]{2,1,0:T(8,128)S(1)}, f32[65,8,128]{2,1,0:T(8,128)S(1)}, u32[]{:S(2)}, u32[]{:S(2)}) collective-permute-start(f32[65,8,128]{2,1,0:T(8,128)S(1)} %get-tuple-element.19), channel_id=1, source_target_pairs={{8,16},{12,20},{16,8},{20,12},{9,17},{13,21},{17,9},{21,13},{10,18... | collective-permute-start | bytes 798728 | tf_op jit(solution)/shard_map/ppermute | solution.py:323
  3.3 2.6 %collective-permute-start.2 = (f32[18,8,128]{2,1,0:T(8,128)S(1)}, f32[18,8,128]{2,1,0:T(8,128)S(1)}, u32[]{:S(2)}, u32[]{:S(2)}) collective-permute-start(f32[18,8,128]{2,1,0:T(8,128)S(1)} %get-tuple-element.20), channel_id=1, source_target_pairs={{0,4},{4,0},{8,12},{12,8},{16,20},{20,16},{24,28},{28,24},{1,5},{5... | collective-permute-start | bytes 221192 | tf_op jit(solution)/shard_map/ppermute | solution.py:323
  5.9 2.7 %collective-permute-start.3 = (f32[9,8,128]{2,1,0:T(8,128)S(1)}, f32[9,8,128]{2,1,0:T(8,128)S(1)}, u32[]{:S(2)}, u32[]{:S(2)}) collective-permute-start(f32[9,8,128]{2,1,0:T(8,128)S(1)} %get-tuple-element.21), channel_id=1, source_target_pairs={{0,12},{4,8},{8,4},{12,0},{16,28},{20,24},{24,20},{28,16},{1,13},{... | collective-permute-start | bytes 110600 | tf_op jit(solution)/shard_map/ppermute | solution.py:323
  8.6 0.7 %collective-permute-start.4 = (f32[9,8,128]{2,1,0:T(8,128)S(1)}, f32[9,8,128]{2,1,0:T(8,128)S(1)}, u32[]{:S(2)}, u32[]{:S(2)}) collective-permute-start(f32[9,8,128]{2,1,0:T(8,128)S(1)} %get-tuple-element.22), channel_id=1, source_target_pairs={{8,20},{12,16},{16,12},{20,8},{9,21},{13,17},{17,13},{21,9},{10,22... | collective-permute-start | bytes 110600 | tf_op jit(solution)/shard_map/ppermute | solution.py:323
  9.3 1.7 %collective-permute-done.3.refs_6_ = f32[9,8,128]{2,1,0:T(8,128)S(1)} collective-permute-done((f32[9,8,128]{2,1,0:T(8,128)S(1)}, f32[9,8,128]{2,1,0:T(8,128)S(1)}, u32[]{:S(2)}, u32[]{:S(2)}) %collective-permute-start.3) | collective-permute-done | bytes 36896 | tf_op jit(solution)/shard_map/ppermute | solution.py:323
  11.0 4.8 %shard_map.77 = (f32[512,128]{1,0:T(8,128)S(1)}, bf16[32,2048]{1,0:T(8,128)(2,1)S(1)}, f32[7,32,128]{2,1,0:T(8,128)S(1)}) custom-call(f32[3,8,128]{2,1,0:T(8,128)S(1)} %get-tuple-element.15.refs_0_, f32[1024,128]{1,0:T(8,128)S(1)} %get-tuple-element.16.refs_1_, s32[16,128]{1,0:T(8,128)S(1)} %get-tuple-element.17.refs_2_, ...), custom_call_target="tpu_custom_call" | custom-call | flops 12000000 | bytes 800000 | tf_op jit(solution)/shard_map/pallas_call | solution.py:365
  15.9 4.7 %shard_map.78 = (f32[512,128]{1,0:T(8,128)S(1)}, bf16[32,2048]{1,0:T(8,128)(2,1)S(1)}) custom-call(f32[3,8,128]{2,1,0:T(8,128)S(1)} %get-tuple-element.15.refs_0_, f32[1024,128]{1,0:T(8,128)S(1)} %get-tuple-element.16.refs_1_, s32[16,128]{1,0:T(8,128)S(1)} %get-tuple-element.17.refs_2_, f32[65,8,128]{2,1,0:T(8,128)S(1)} %collective-permute-done.refs_3_, ...), custom_call_target="tpu_custom_call" | custom-call | flops 12000000 | bytes 800000 | tf_op jit(solution)/shard_map/pallas_call | solution.py:365
  20.6 1.6 %collective-permute-start.6 = (bf16[32,2048]{1,0:T(8,128)(2,1)S(1)}, bf16[32,2048]{1,0:T(8,128)(2,1)S(1)}, u32[]{:S(2)}, u32[]{:S(2)}) collective-permute-start(bf16[32,2048]{1,0:T(8,128)(2,1)S(1)} %get-tuple-element.27), channel_id=1, source_target_pairs={{0,1},{1,3},{3,2},{2,0},{4,5},{5,7},{7,6},{6,4},{8,9},{9,11},{11,1... | collective-permute-start | bytes 393224 | tf_op jit(solution)/shard_map/ppermute | solution.py:402
  22.2 2.6 %collective-permute-start.5 = (bf16[32,2048]{1,0:T(8,128)(2,1)S(1)}, bf16[32,2048]{1,0:T(8,128)(2,1)S(1)}, u32[]{:S(2)}, u32[]{:S(2)}) collective-permute-start(bf16[32,2048]{1,0:T(8,128)(2,1)S(1)} %get-tuple-element.26), channel_id=1, source_target_pairs={{0,1},{1,3},{3,2},{2,0},{4,5},{5,7},{7,6},{6,4},{8,9},{9,11},{11,1... | collective-permute-start | bytes 393224 | tf_op jit(solution)/shard_map/ppermute | solution.py:402
  24.9 1.1 %fusion.15 = f32[4,64,768]{2,1,0:T(8,128)S(1)} fusion(f32[4,64,768]{2,1,0:T(8,128)S(1)} %broadcast_in_dim.15, s32[]{:T(128)S(6)} %select_n.84, bf16[96,8,16,128]{3,2,1,0:T(8,128)(2,1)S(1)} %bitcast.72, bf16[32,2048]{1,0:T(8,128)(2,1)S(1)} %get-tuple-element.27, bf16[32,2048]{1,0:T(8,128)(2,1)S(1)} %get-tuple-element.26), kind=kOutput, calls=%fused_computation.13 | convolution fusion | flops 201850880 | bytes 3604484 | tf_op jit(solution)/shard_map/dot_general | solution.py:404
  25.9 0.5 collective-permute-done.6
  26.5 0.8 %collective-permute-start.8 = (bf16[32,2048]{1,0:T(8,128)(2,1)S(1)}, bf16[32,2048]{1,0:T(8,128)(2,1)S(1)}, u32[]{:S(2)}, u32[]{:S(2)}) collective-permute-start(bf16[32,2048]{1,0:T(8,128)(2,1)S(1)} %collective-permute-done.6), channel_id=1, source_target_pairs={{0,1},{1,3},{3,2},{2,0},{4,5},{5,7},{7,6},{6,4},{8,9},{9,11},{11,1... | collective-permute-start | bytes 393224 | tf_op jit(solution)/shard_map/ppermute | solution.py:402
  27.3 1.3 %collective-permute-done.5 = bf16[32,2048]{1,0:T(8,128)(2,1)S(1)} collective-permute-done((bf16[32,2048]{1,0:T(8,128)(2,1)S(1)}, bf16[32,2048]{1,0:T(8,128)(2,1)S(1)}, u32[]{:S(2)}, u32[]{:S(2)}) %collective-permute-start.5) | collective-permute-done | bytes 131104 | tf_op jit(solution)/shard_map/ppermute | solution.py:402
  28.6 2.5 %collective-permute-start.7 = (bf16[32,2048]{1,0:T(8,128)(2,1)S(1)}, bf16[32,2048]{1,0:T(8,128)(2,1)S(1)}, u32[]{:S(2)}, u32[]{:S(2)}) collective-permute-start(bf16[32,2048]{1,0:T(8,128)(2,1)S(1)} %collective-permute-done.5), channel_id=1, source_target_pairs={{0,1},{1,3},{3,2},{2,0},{4,5},{5,7},{7,6},{6,4},{8,9},{9,11},{11,1... | collective-permute-start | bytes 393224 | tf_op jit(solution)/shard_map/ppermute | solution.py:402
  31.1 1.1 %fusion.21 = f32[4,64,768]{2,1,0:T(8,128)S(1)} fusion(f32[4,64,768]{2,1,0:T(8,128)S(1)} %fusion.15, s32[]{:T(128)S(6)} %select_n.88, bf16[96,8,16,128]{3,2,1,0:T(8,128)(2,1)S(1)} %bitcast.73, bf16[32,2048]{1,0:T(8,128)(2,1)S(1)} %collective-permute-done.6, bf16[32,2048]{1,0:T(8,128)(2,1)S(1)} %collective-permute-done.5), kind=kOutput, calls=%fused_computation.15 | convolution fusion | flops 201850880 | bytes 3604484 | tf_op jit(solution)/shard_map/dot_general | solution.py:404
  32.4 1.6 %collective-permute-start.10 = (bf16[32,2048]{1,0:T(8,128)(2,1)S(1)}, bf16[32,2048]{1,0:T(8,128)(2,1)S(1)}, u32[]{:S(2)}, u32[]{:S(2)}) collective-permute-start(bf16[32,2048]{1,0:T(8,128)(2,1)S(1)} %collective-permute-done.8), channel_id=1, source_target_pairs={{0,1},{1,3},{3,2},{2,0},{4,5},{5,7},{7,6},{6,4},{8,9},{9,11},{11,1... | collective-permute-start | bytes 393224 | tf_op jit(solution)/shard_map/ppermute | solution.py:402
  33.9 2.0 %collective-permute-done.7 = bf16[32,2048]{1,0:T(8,128)(2,1)S(1)} collective-permute-done((bf16[32,2048]{1,0:T(8,128)(2,1)S(1)}, bf16[32,2048]{1,0:T(8,128)(2,1)S(1)}, u32[]{:S(2)}, u32[]{:S(2)}) %collective-permute-start.7) | collective-permute-done | bytes 131104 | tf_op jit(solution)/shard_map/ppermute | solution.py:402
  35.9 1.0 %collective-permute-start.9 = (bf16[32,2048]{1,0:T(8,128)(2,1)S(1)}, bf16[32,2048]{1,0:T(8,128)(2,1)S(1)}, u32[]{:S(2)}, u32[]{:S(2)}) collective-permute-start(bf16[32,2048]{1,0:T(8,128)(2,1)S(1)} %collective-permute-done.7), channel_id=1, source_target_pairs={{0,1},{1,3},{3,2},{2,0},{4,5},{5,7},{7,6},{6,4},{8,9},{9,11},{11,1... | collective-permute-start | bytes 393224 | tf_op jit(solution)/shard_map/ppermute | solution.py:402
  36.9 1.1 %fusion.27 = f32[4,64,768]{2,1,0:T(8,128)S(1)} fusion(f32[4,64,768]{2,1,0:T(8,128)S(1)} %fusion.21, s32[]{:T(128)S(6)} %select_n.92, bf16[96,8,16,128]{3,2,1,0:T(8,128)(2,1)S(1)} %bitcast.74, bf16[32,2048]{1,0:T(8,128)(2,1)S(1)} %collective-permute-done.8, bf16[32,2048]{1,0:T(8,128)(2,1)S(1)} %collective-permute-done.7), kind=kOutput, calls=%fused_computation.17 | convolution fusion | flops 201850880 | bytes 3604484 | tf_op jit(solution)/shard_map/dot_general | solution.py:404
  38.0 0.4 collective-permute-done.10
  38.4 4.3 %collective-permute-done.9 = bf16[32,2048]{1,0:T(8,128)(2,1)S(1)} collective-permute-done((bf16[32,2048]{1,0:T(8,128)(2,1)S(1)}, bf16[32,2048]{1,0:T(8,128)(2,1)S(1)}, u32[]{:S(2)}, u32[]{:S(2)}) %collective-permute-start.9) | collective-permute-done | bytes 131104 | tf_op jit(solution)/shard_map/ppermute | solution.py:402
  42.7 1.1 %fusion.33 = f32[4,64,768]{2,1,0:T(8,128)S(1)} fusion(f32[4,64,768]{2,1,0:T(8,128)S(1)} %fusion.27, s32[]{:T(128)S(6)} %select_n.96, bf16[96,8,16,128]{3,2,1,0:T(8,128)(2,1)S(1)} %bitcast.75, bf16[32,2048]{1,0:T(8,128)(2,1)S(1)} %collective-permute-done.10, bf16[32,2048]{1,0:T(8,128)(2,1)S(1)} %collective-permute-done.9), kind=kOutput, calls=%fused_computation.19 | convolution fusion | flops 201850880 | bytes 3604484 | tf_op jit(solution)/shard_map/dot_general | solution.py:404
  44.2 1.2 %collective-permute-done.11 = bf16[2,2,32,768]{3,2,1,0:T(8,128)(2,1)S(1)} collective-permute-done((bf16[2,2,32,768]{3,2,1,0:T(8,128)(2,1)S(1)}, bf16[2,2,32,768]{3,2,1,0:T(8,128)(2,1)S(1)}, u32[]{:S(2)}, u32[]{:S(2)}) %collective-permute-start.11) | collective-permute-done | bytes 196640 | tf_op jit(solution)/shard_map/ppermute | solution.py:421
  45.4 3.8 %collective-permute-start.14 = (bf16[32,768]{1,0:T(8,128)(2,1)S(1)}, bf16[32,768]{1,0:T(8,128)(2,1)S(1)}, u32[]{:S(2)}, u32[]{:S(2)}) collective-permute-start(bf16[32,768]{1,0:T(8,128)(2,1)S(1)} %get-tuple-element.29), channel_id=1, source_target_pairs={{0,20},{4,16},{8,28},{12,24},{16,4},{20,0},{24,12},{28,8},{1,21},{... | collective-permute-start | bytes 147464 | tf_op jit(solution)/shard_map/ppermute | solution.py:434
  49.2 0.7 %collective-permute-start.13 = (bf16[32,768]{1,0:T(8,128)(2,1)S(1)}, bf16[32,768]{1,0:T(8,128)(2,1)S(1)}, u32[]{:S(2)}, u32[]{:S(2)}) collective-permute-start(bf16[32,768]{1,0:T(8,128)(2,1)S(1)} %get-tuple-element.30), channel_id=1, source_target_pairs={{0,16},{4,20},{8,24},{12,28},{16,0},{20,4},{24,8},{28,12},{1,17},{... | collective-permute-start | bytes 147464 | tf_op jit(solution)/shard_map/ppermute | solution.py:434
  49.8 1.4 %collective-permute-start.12 = (bf16[32,768]{1,0:T(8,128)(2,1)S(1)}, bf16[32,768]{1,0:T(8,128)(2,1)S(1)}, u32[]{:S(2)}, u32[]{:S(2)}) collective-permute-start(bf16[32,768]{1,0:T(8,128)(2,1)S(1)} %get-tuple-element.28), channel_id=1, source_target_pairs={{0,4},{4,0},{8,12},{12,8},{16,20},{20,16},{24,28},{28,24},{1,5},{5... | collective-permute-start | bytes 147464 | tf_op jit(solution)/shard_map/ppermute | solution.py:434
  51.2 0.8 %pad_maximum_fusion = f32[1024,128]{1,0:T(8,128)} fusion(f32[512,128]{1,0:T(8,128)S(1)} %get-tuple-element.25, f32[512,128]{1,0:T(8,128)S(1)} %get-tuple-element.23), kind=kLoop, calls=%fused_computation.20 | loop fusion | flops 131072 | bytes 1048576 | tf_op jit(solution)/shard_map/concatenate | solution.py:370
  52.1 1.2 %collective-permute-done.13 = bf16[32,768]{1,0:T(8,128)(2,1)S(1)} collective-permute-done((bf16[32,768]{1,0:T(8,128)(2,1)S(1)}, bf16[32,768]{1,0:T(8,128)(2,1)S(1)}, u32[]{:S(2)}, u32[]{:S(2)}) %collective-permute-start.13) | collective-permute-done | bytes 49184 | tf_op jit(solution)/shard_map/ppermute | solution.py:434
  53.3 0.7 %collective-permute-done.12 = bf16[32,768]{1,0:T(8,128)(2,1)S(1)} collective-permute-done((bf16[32,768]{1,0:T(8,128)(2,1)S(1)}, bf16[32,768]{1,0:T(8,128)(2,1)S(1)}, u32[]{:S(2)}, u32[]{:S(2)}) %collective-permute-start.12) | collective-permute-done | bytes 49184 | tf_op jit(solution)/shard_map/ppermute | solution.py:434
  53.9 0.7 %fusion.51 = f32[768,32]{0,1:T(8,128)} fusion(bf16[32,768]{1,0:T(8,128)(2,1)S(1)} %collective-permute-done.14, bf16[32,768]{1,0:T(8,128)(2,1)S(1)} %collective-permute-done.13, bf16[32,768]{1,0:T(8,128)(2,1)S(1)} %collective-permute-done.12, f32[4,32,768]{2,1,0:T(8,128)S(1)} %bitcast.69, s32[]{:T(128)S(6)} %select_n.101), kind=kLoop, calls=%fused_computation.39 | loop fusion | flops 147456 | bytes 344068 | tf_op jit(solution)/shard_map/transpose | solution.py:437
  (13 shorter events, 0.7 us)
Async XLA Ops:
  2.1 8.9 %collective-permute-start = (f32[65,8,128]{2,1,0:T(8,128)S(1)}, f32[65,8,128]{2,1,0:T(8,128)S(1)}, u32[]{:S(2)}, u32[]{:S(2)}) collective-permute-start(f32[65,8,128]{2,1,0:T(8,128)S(1)} %get-tuple-element.18), channel_id=1, source_target_pairs={{0,8},{4,12},{8,0},{12,4},{16,24},{20,28},{24,16},{28,20},{1,9},{5... | collective-permute-start | bytes 798728 | tf_op jit(solution)/shard_map/ppermute | solution.py:323
  2.7 8.4 %collective-permute-start.1 = (f32[65,8,128]{2,1,0:T(8,128)S(1)}, f32[65,8,128]{2,1,0:T(8,128)S(1)}, u32[]{:S(2)}, u32[]{:S(2)}) collective-permute-start(f32[65,8,128]{2,1,0:T(8,128)S(1)} %get-tuple-element.19), channel_id=1, source_target_pairs={{8,16},{12,20},{16,8},{20,12},{9,17},{13,21},{17,9},{21,13},{10,18... | collective-permute-start | bytes 798728 | tf_op jit(solution)/shard_map/ppermute | solution.py:323
  3.3 7.7 %collective-permute-start.2 = (f32[18,8,128]{2,1,0:T(8,128)S(1)}, f32[18,8,128]{2,1,0:T(8,128)S(1)}, u32[]{:S(2)}, u32[]{:S(2)}) collective-permute-start(f32[18,8,128]{2,1,0:T(8,128)S(1)} %get-tuple-element.20), channel_id=1, source_target_pairs={{0,4},{4,0},{8,12},{12,8},{16,20},{20,16},{24,28},{28,24},{1,5},{5... | collective-permute-start | bytes 221192 | tf_op jit(solution)/shard_map/ppermute | solution.py:323
  5.9 5.1 %collective-permute-start.3 = (f32[9,8,128]{2,1,0:T(8,128)S(1)}, f32[9,8,128]{2,1,0:T(8,128)S(1)}, u32[]{:S(2)}, u32[]{:S(2)}) collective-permute-start(f32[9,8,128]{2,1,0:T(8,128)S(1)} %get-tuple-element.21), channel_id=1, source_target_pairs={{0,12},{4,8},{8,4},{12,0},{16,28},{20,24},{24,20},{28,16},{1,13},{... | collective-permute-start | bytes 110600 | tf_op jit(solution)/shard_map/ppermute | solution.py:323
  8.6 2.4 %collective-permute-start.4 = (f32[9,8,128]{2,1,0:T(8,128)S(1)}, f32[9,8,128]{2,1,0:T(8,128)S(1)}, u32[]{:S(2)}, u32[]{:S(2)}) collective-permute-start(f32[9,8,128]{2,1,0:T(8,128)S(1)} %get-tuple-element.22), channel_id=1, source_target_pairs={{8,20},{12,16},{16,12},{20,8},{9,21},{13,17},{17,13},{21,9},{10,22... | collective-permute-start | bytes 110600 | tf_op jit(solution)/shard_map/ppermute | solution.py:323
  9.3 15.5 %copy-start = (bf16[768,16,128]{2,1,0:T(8,128)(2,1)S(1)}, bf16[768,16,128]{2,1,0:T(8,128)(2,1)}, u32[]{:S(2)}) copy-start(bf16[768,16,128]{2,1,0:T(8,128)(2,1)} %param.7) | copy-start | bytes 9437188
  20.6 5.9 %collective-permute-start.6 = (bf16[32,2048]{1,0:T(8,128)(2,1)S(1)}, bf16[32,2048]{1,0:T(8,128)(2,1)S(1)}, u32[]{:S(2)}, u32[]{:S(2)}) collective-permute-start(bf16[32,2048]{1,0:T(8,128)(2,1)S(1)} %get-tuple-element.27), channel_id=1, source_target_pairs={{0,1},{1,3},{3,2},{2,0},{4,5},{5,7},{7,6},{6,4},{8,9},{9,11},{11,1... | collective-permute-start | bytes 393224 | tf_op jit(solution)/shard_map/ppermute | solution.py:402
  22.2 6.4 %collective-permute-start.5 = (bf16[32,2048]{1,0:T(8,128)(2,1)S(1)}, bf16[32,2048]{1,0:T(8,128)(2,1)S(1)}, u32[]{:S(2)}, u32[]{:S(2)}) collective-permute-start(bf16[32,2048]{1,0:T(8,128)(2,1)S(1)} %get-tuple-element.26), channel_id=1, source_target_pairs={{0,1},{1,3},{3,2},{2,0},{4,5},{5,7},{7,6},{6,4},{8,9},{9,11},{11,1... | collective-permute-start | bytes 393224 | tf_op jit(solution)/shard_map/ppermute | solution.py:402
  26.5 5.9 %collective-permute-start.8 = (bf16[32,2048]{1,0:T(8,128)(2,1)S(1)}, bf16[32,2048]{1,0:T(8,128)(2,1)S(1)}, u32[]{:S(2)}, u32[]{:S(2)}) collective-permute-start(bf16[32,2048]{1,0:T(8,128)(2,1)S(1)} %collective-permute-done.6), channel_id=1, source_target_pairs={{0,1},{1,3},{3,2},{2,0},{4,5},{5,7},{7,6},{6,4},{8,9},{9,11},{11,1... | collective-permute-start | bytes 393224 | tf_op jit(solution)/shard_map/ppermute | solution.py:402
  28.6 7.3 %collective-permute-start.7 = (bf16[32,2048]{1,0:T(8,128)(2,1)S(1)}, bf16[32,2048]{1,0:T(8,128)(2,1)S(1)}, u32[]{:S(2)}, u32[]{:S(2)}) collective-permute-start(bf16[32,2048]{1,0:T(8,128)(2,1)S(1)} %collective-permute-done.5), channel_id=1, source_target_pairs={{0,1},{1,3},{3,2},{2,0},{4,5},{5,7},{7,6},{6,4},{8,9},{9,11},{11,1... | collective-permute-start | bytes 393224 | tf_op jit(solution)/shard_map/ppermute | solution.py:402
  32.4 6.0 %collective-permute-start.10 = (bf16[32,2048]{1,0:T(8,128)(2,1)S(1)}, bf16[32,2048]{1,0:T(8,128)(2,1)S(1)}, u32[]{:S(2)}, u32[]{:S(2)}) collective-permute-start(bf16[32,2048]{1,0:T(8,128)(2,1)S(1)} %collective-permute-done.8), channel_id=1, source_target_pairs={{0,1},{1,3},{3,2},{2,0},{4,5},{5,7},{7,6},{6,4},{8,9},{9,11},{11,1... | collective-permute-start | bytes 393224 | tf_op jit(solution)/shard_map/ppermute | solution.py:402
  35.9 6.8 %collective-permute-start.9 = (bf16[32,2048]{1,0:T(8,128)(2,1)S(1)}, bf16[32,2048]{1,0:T(8,128)(2,1)S(1)}, u32[]{:S(2)}, u32[]{:S(2)}) collective-permute-start(bf16[32,2048]{1,0:T(8,128)(2,1)S(1)} %collective-permute-done.7), channel_id=1, source_target_pairs={{0,1},{1,3},{3,2},{2,0},{4,5},{5,7},{7,6},{6,4},{8,9},{9,11},{11,1... | collective-permute-start | bytes 393224 | tf_op jit(solution)/shard_map/ppermute | solution.py:402
  43.8 1.5 %collective-permute-start.11 = (bf16[2,2,32,768]{3,2,1,0:T(8,128)(2,1)S(1)}, bf16[2,2,32,768]{3,2,1,0:T(8,128)(2,1)S(1)}, u32[]{:S(2)}, u32[]{:S(2)}) collective-permute-start(bf16[2,2,32,768]{3,2,1,0:T(8,128)(2,1)S(1)} %fusion.48), channel_id=1, source_target_pairs={{0,8},{4,12},{8,0},{12,4},{16,24},{20,28},{24,16},{28,20},{1,9},{5... | collective-permute-start | bytes 589832 | tf_op jit(solution)/shard_map/ppermute | solution.py:421
  45.4 6.6 %collective-permute-start.14 = (bf16[32,768]{1,0:T(8,128)(2,1)S(1)}, bf16[32,768]{1,0:T(8,128)(2,1)S(1)}, u32[]{:S(2)}, u32[]{:S(2)}) collective-permute-start(bf16[32,768]{1,0:T(8,128)(2,1)S(1)} %get-tuple-element.29), channel_id=1, source_target_pairs={{0,20},{4,16},{8,28},{12,24},{16,4},{20,0},{24,12},{28,8},{1,21},{... | collective-permute-start | bytes 147464 | tf_op jit(solution)/shard_map/ppermute | solution.py:434
  49.2 4.1 %collective-permute-start.13 = (bf16[32,768]{1,0:T(8,128)(2,1)S(1)}, bf16[32,768]{1,0:T(8,128)(2,1)S(1)}, u32[]{:S(2)}, u32[]{:S(2)}) collective-permute-start(bf16[32,768]{1,0:T(8,128)(2,1)S(1)} %get-tuple-element.30), channel_id=1, source_target_pairs={{0,16},{4,20},{8,24},{12,28},{16,0},{20,4},{24,8},{28,12},{1,17},{... | collective-permute-start | bytes 147464 | tf_op jit(solution)/shard_map/ppermute | solution.py:434
  49.8 4.1 %collective-permute-start.12 = (bf16[32,768]{1,0:T(8,128)(2,1)S(1)}, bf16[32,768]{1,0:T(8,128)(2,1)S(1)}, u32[]{:S(2)}, u32[]{:S(2)}) collective-permute-start(bf16[32,768]{1,0:T(8,128)(2,1)S(1)} %get-tuple-element.28), channel_id=1, source_target_pairs={{0,4},{4,0},{8,12},{12,8},{16,20},{20,16},{24,28},{28,24},{1,5},{5... | collective-permute-start | bytes 147464 | tf_op jit(solution)/shard_map/ppermute | solution.py:434

commit v5 on v4

--- a/solution.py
+++ b/solution.py
@@ -79,16 +79,17 @@
             for g in range(groups):
                 tile = adj_ref[pl.ds(g * SUB * width_x + row, SUB, stride=width_x), :]
                 strip = jnp.where((lane // SIDE) == g, lane_gather(tile, index), strip)
-            strip_refs[3 * kind][row] = jnp.where(keep, strip, 0.0)
+            strip_refs[2 * kind][row] = jnp.where(keep, strip, 0.0)
         for tile_x in range(width_x // SUB):
             ids = ids_ref[tile_x * SUB : (tile_x + 1) * SUB, :].astype(F32) + 1.0
-            strip_refs[3 * kind][width_x + tile_x] = jnp.where(keep, lane_gather(ids, index), 0.0)
+            strip_refs[2 * kind][width_x + tile_x] = jnp.where(keep, lane_gather(ids, index), 0.0)
         for which in range(2):
             upper = upper_x if which == 0 else 1 - upper_x
             base = upper * (width_x - DEG)
+            to, at = (row_refs[0], DEG * groups + 1 + kind * (DEG + 1)) if which == 0 else (strip_refs[2 * kind + 1], 0)
             for row in range(DEG):
-                strip_refs[3 * kind + 1 + which][row] = strip_refs[3 * kind][base + row]
-            strip_refs[3 * kind + 1 + which][DEG] = strip_refs[3 * kind][width_x + upper * (width_x // SUB - 1)]
+                to[at + row] = strip_refs[2 * kind][base + row]
+            to[at + DEG] = strip_refs[2 * kind][width_x + upper * (width_x // SUB - 1)]
     for i, ref in enumerate((diag_ref, cond_ref)):
         tile = jnp.zeros((SUB, LANES), F32)
         for m in range(ref.shape[0]):
@@ -114,13 +115,14 @@
 
 
 def filter_kernel(groups, all_groups, offset, width_x, first, *refs):
-    params_ref, adj_ref, ids_ref, even_ref, odd_ref, strip_ref, strip_even_ref, strip_odd_ref = refs[:8]
+    params_ref, adj_ref, ids_ref, even_ref, odd_ref, strip_ref, strip_odd_ref = refs[:7]
     if first:
-        smooth_ref, low_ref, table = refs[8:11]
+        smooth_ref, low_ref, table = refs[7:10]
     else:
-        table, smooth_ref, low_ref = refs[8:11]
-    u_ref, a_ref, b_ref, y_ref, power = refs[11:]
+        table, smooth_ref, low_ref = refs[7:10]
+    u_ref, a_ref, b_ref, y_ref, power = refs[10:]
     tall = width_x + 2 * DEG
+    beyond = width_x + width_x // SUB
     lane = lax.broadcasted_iota(jnp.int32, (SUB, LANES), 1)
     even_x = is_even("sx")
     for k in range(DEG + 1):
@@ -173,7 +175,7 @@
             x0 = tall - DEG if high else 0
             from_even = even_x if high else jnp.logical_not(even_x)
             lookup(jnp.where(from_even, even_ref[DEG * all_groups], odd_ref[DEG * all_groups]), x0, False)
-            ids = jnp.where(from_even, strip_even_ref[DEG], strip_odd_ref[DEG])
+            ids = jnp.where(from_even, strip_ref[beyond + DEG], strip_odd_ref[DEG])
             lookup(lane_gather(ids, repeat), x0, True)
         for tile_x in range(width_x // SUB):
             x0 = DEG + tile_x * SUB
@@ -189,7 +191,7 @@
             for g in range(groups):
                 at = row * all_groups + offset + g
                 tiles.append(jnp.where(from_even, even_ref[at], odd_ref[at]) * scale)
-            strip = jnp.where(from_even, strip_even_ref[row], strip_odd_ref[row])
+            strip = jnp.where(from_even, strip_ref[beyond + row], strip_odd_ref[row])
             place_row(x0 + row, tiles + [strip * spread(COND_S, x0 + row)])
     for row in range(width_x):
         x = DEG + row
@@ -296,7 +298,11 @@
     size_y = lax.axis_size("sy")
     flat = adjoint.reshape(cols * width_x, width_y)
     n_kinds = 2 if size_y > 2 else 1
-    row_shape = jax.ShapeDtypeStruct((DEG * groups + 1, SUB, LANES), F32)
+    row_tiles = DEG * groups + 1
+    row_shapes = [
+        jax.ShapeDtypeStruct((row_tiles + n_kinds * (DEG + 1), SUB, LANES), F32),
+        jax.ShapeDtypeStruct((row_tiles, SUB, LANES), F32),
+    ]
     strip_shape = jax.ShapeDtypeStruct((width_x + width_x // SUB, SUB, LANES), F32)
     corner_shape = jax.ShapeDtypeStruct((DEG + 1, SUB, LANES), F32)
     small = [pltpu.SMEM(v.shape, F32) for v in (mat_diag, mat_cond, cheb_coef)]
@@ -307,10 +313,10 @@
             jax.ShapeDtypeStruct(cell_ids.shape, jnp.int32),
             jax.ShapeDtypeStruct((3, SUB, LANES), F32),
         ]
-        + [row_shape] * 2
-        + [strip_shape, corner_shape, corner_shape] * n_kinds,
+        + row_shapes
+        + [strip_shape, corner_shape] * n_kinds,
         in_specs=[hbm()] * 5,
-        out_specs=[vmem()] * (5 + 3 * n_kinds),
+        out_specs=[vmem()] * (5 + 2 * n_kinds),
         scratch_shapes=small + [pltpu.SemaphoreType.DMA((5,))],
         compiler_params=pltpu.CompilerParams(vmem_limit_bytes=VMEM_GRANT),
         name="pack",
@@ -322,18 +328,15 @@
             return jnp.zeros_like(value)
         return lax.ppermute(value, ("sx", "sy"), pairs)
 
+    even = swap(packed[0], 0, None)
     odd = swap(packed[1], 1, None)
-    even = swap(packed[0], 0, None)
     strips = []
     for kind in range(n_kinds):
-        strips.append(
-            (
-                swap(packed[2 + 3 * kind], None, kind),
-                swap(packed[3 + 3 * kind], 0, kind),
-                swap(packed[4 + 3 * kind], 1, kind),
-            )
-        )
-    strip, strip_even, strip_odd = (functools.reduce(jnp.add, part) for part in zip(*strips))
+        corner = swap(packed[3 + 2 * kind], 1, kind)
+        start = row_tiles + kind * (DEG + 1)
+        tall_strip = jnp.concatenate([packed[2 + 2 * kind], even[start : start + DEG + 1]])
+        strips.append((swap(tall_strip, None, kind), corner))
+    strip, strip_odd = (functools.reduce(jnp.add, part) for part in zip(*strips))
     tall = width_x + 2 * DEG
     n_chunks = CHUNKS if groups % (2 * CHUNKS) == 0 else 1
     part = groups // n_chunks
@@ -346,8 +349,8 @@
             pltpu.VMEM((part * SUB, width_x * width_y), BF16),
         ]
         scratch = [field] * 4 + [pltpu.VMEM((DEG + 1, SUB, LANES), F32)]
-        operands = [params, flat, ids, even, odd, strip, strip_even, strip_odd]
-        in_specs = [vmem()] * 8
+        operands = [params, flat, ids, even, odd, strip, strip_odd]
+        in_specs = [vmem()] * 7
         if chunk == 0:
             out_shape += [pltpu.VMEM((7, tall, LANES), F32)]
         else:

time: 54.8 us -> 55 us (level)
    ppermute x5 -> x4, starting transfers between devices: 7.14 us -> 4.82 us  [swap(): return lax.ppermute(value, ('sx', 'sy'), pairs)]
    ppermute x6, starting transfers between devices: 10.1 us -> 11.5 us  [gathered_product(): following.append(lax.ppermute(piece, 'cr', hop))]
    ppermute x6, waiting for transfers between devices: 8.72 us -> 7.52 us  [gathered_product(): following.append(lax.ppermute(piece, 'cr', hop))]
    ppermute x3, starting transfers between devices: 5.81 us -> 6.64 us  [reduced(): arrived.append(lax.ppermute(out, ('sx', 'sy'), pairs))]
    ppermute x5 -> x4, waiting for transfers between devices: 1.7 us -> 2.53 us  [swap(): return lax.ppermute(value, ('sx', 'sy'), pairs)]
  transfers between devices with their start and end apart: 15 -> 14, of which waited for: 10 -> 11; matrix products, arithmetic and copies ran while one was open for 8% -> 8% of each run, Pallas kernels for 0% -> 0%
where the time goes in v5:
time: 55 us; the launch traced here: 54.9 us
  starting transfers between devices  23.7 us (43%)
  waiting for transfers between devices  13.4 us (24%)
  Pallas kernels  11 us (20%)
  matrix products  4.32 us (8%)
  other arithmetic  1.54 us (3%)
  between operations  0.81 us (1%)
    ppermute x6, starting transfers between devices, gathered_product(): following.append(lax.ppermute(piece, 'cr', hop))  11.5 us
    pallas_call x2, Pallas kernels, filtered(): got = call(*operands)  9.5 us
    ppermute x6, waiting for transfers between devices, gathered_product(): following.append(lax.ppermute(piece, 'cr', hop))  7.52 us
    ppermute x3, starting transfers between devices, reduced(): arrived.append(lax.ppermute(out, ('sx', 'sy'), pairs))  6.64 us
    ppermute x4, starting transfers between devices, swap(): return lax.ppermute(value, ('sx', 'sy'), pairs)  4.82 us
    dot_general x4, matrix products, gathered_product(): lax.dot_general(piece, rows, (((1,), (1,)), ((), ())), preferred_element_...  4.32 us
    ppermute x4, waiting for transfers between devices, swap(): return lax.ppermute(value, ('sx', 'sy'), pairs)  2.53 us
    ppermute x3, waiting for transfers between devices, reduced(): arrived.append(lax.ppermute(out, ('sx', 'sy'), pairs))  2.26 us
  transfers between devices with their start and end apart: 14, of which 11 were waited for; matrix products, arithmetic and copies ran while one was open for 8% of the time, Pallas kernels for 0%

profile of v5, /device:TPU:0, one launch (start us, length us, event | category | flops | bytes accessed | tf_op | source)
XLA Modules:
  0.0 54.9 jit_solution(17881556225064027447)
XLA Ops:
  0.6 1.5 %pack.1 = (f32[1024,128]{1,0:T(8,128)S(1)}, s32[16,128]{1,0:T(8,128)S(1)}, f32[3,8,128]{2,1,0:T(8,128)S(1)}, f32[74,8,128]{2,1,0:T(8,128)S(1)}, f32[65,8,128]{2,...) custom-call(f32[1024,128]{1,0:T(8,128)} %bitcast.70, s32[16,128]{1,0:T(8,128)} %refs_1_.1, ...), custom_call_target="tpu_custom_call" | custom-call | tf_op jit(solution)/shard_map/pack/pallas_call | solution.py:309
  2.1 0.6 %collective-permute-start = (f32[74,8,128]{2,1,0:T(8,128)S(1)}, f32[74,8,128]{2,1,0:T(8,128)S(1)}, u32[]{:S(2)}, u32[]{:S(2)}) collective-permute-start(f32[74,8,128]{2,1,0:T(8,128)S(1)} %get-tuple-element.17), channel_id=1, source_target_pairs={{0,8},{4,12},{8,0},{12,4},{16,24},{20,28},{24,16},{28,20},{1,9},{5... | collective-permute-start | bytes 909320 | tf_op jit(solution)/shard_map/ppermute | solution.py:329
  2.7 0.7 %collective-permute-start.1 = (f32[65,8,128]{2,1,0:T(8,128)S(1)}, f32[65,8,128]{2,1,0:T(8,128)S(1)}, u32[]{:S(2)}, u32[]{:S(2)}) collective-permute-start(f32[65,8,128]{2,1,0:T(8,128)S(1)} %get-tuple-element.18), channel_id=1, source_target_pairs={{8,16},{12,20},{16,8},{20,12},{9,17},{13,21},{17,9},{21,13},{10,18... | collective-permute-start | bytes 798728 | tf_op jit(solution)/shard_map/ppermute | solution.py:329
  3.3 0.5 collective-permute-done.refs_3_
  3.9 2.9 %collective-permute-start.2 = (f32[27,8,128]{2,1,0:T(8,128)S(1)}, f32[27,8,128]{2,1,0:T(8,128)S(1)}, u32[]{:S(2)}, u32[]{:S(2)}) collective-permute-start(f32[27,8,128]{2,1,0:T(8,128)S(1)} %pad_maximum_fusion.1), channel_id=1, source_target_pairs={{0,4},{4,0},{8,12},{12,8},{16,20},{20,16},{24,28},{28,24},{1,5},{5... | collective-permute-start | bytes 331784 | tf_op jit(solution)/shard_map/ppermute | solution.py:329
  6.8 0.7 %collective-permute-start.3 = (f32[9,8,128]{2,1,0:T(8,128)S(1)}, f32[9,8,128]{2,1,0:T(8,128)S(1)}, u32[]{:S(2)}, u32[]{:S(2)}) collective-permute-start(f32[9,8,128]{2,1,0:T(8,128)S(1)} %get-tuple-element.20), channel_id=1, source_target_pairs={{8,20},{12,16},{16,12},{20,8},{9,21},{13,17},{17,13},{21,9},{10,22... | collective-permute-start | bytes 110600 | tf_op jit(solution)/shard_map/ppermute | solution.py:329
  7.6 2.0 %collective-permute-done.2.refs_5_ = f32[27,8,128]{2,1,0:T(8,128)S(1)} collective-permute-done((f32[27,8,128]{2,1,0:T(8,128)S(1)}, f32[27,8,128]{2,1,0:T(8,128)S(1)}, u32[]{:S(2)}, u32[]{:S(2)}) %collective-permute-start.2) | collective-permute-done | bytes 110624 | tf_op jit(solution)/shard_map/ppermute | solution.py:329
  9.6 4.8 %shard_map.77 = (f32[512,128]{1,0:T(8,128)S(1)}, bf16[32,2048]{1,0:T(8,128)(2,1)S(1)}, f32[7,32,128]{2,1,0:T(8,128)S(1)}) custom-call(f32[3,8,128]{2,1,0:T(8,128)S(1)} %get-tuple-element.14.refs_0_, f32[1024,128]{1,0:T(8,128)S(1)} %get-tuple-element.15.refs_1_, s32[16,128]{1,0:T(8,128)S(1)} %get-tuple-element.16.refs_2_, ...), custom_call_target="tpu_custom_call" | custom-call | flops 12000000 | bytes 800000 | tf_op jit(solution)/shard_map/pallas_call | solution.py:368
  14.4 4.7 %shard_map.78 = (f32[512,128]{1,0:T(8,128)S(1)}, bf16[32,2048]{1,0:T(8,128)(2,1)S(1)}) custom-call(f32[3,8,128]{2,1,0:T(8,128)S(1)} %get-tuple-element.14.refs_0_, f32[1024,128]{1,0:T(8,128)S(1)} %get-tuple-element.15.refs_1_, s32[16,128]{1,0:T(8,128)S(1)} %get-tuple-element.16.refs_2_, f32[74,8,128]{2,1,0:T(8,128)S(1)} %collective-permute-done.refs_3_, ...), custom_call_target="tpu_custom_call" | custom-call | flops 12000000 | bytes 800000 | tf_op jit(solution)/shard_map/pallas_call | solution.py:368
  19.1 2.3 %collective-permute-start.5 = (bf16[32,2048]{1,0:T(8,128)(2,1)S(1)}, bf16[32,2048]{1,0:T(8,128)(2,1)S(1)}, u32[]{:S(2)}, u32[]{:S(2)}) collective-permute-start(bf16[32,2048]{1,0:T(8,128)(2,1)S(1)} %get-tuple-element.25), channel_id=1, source_target_pairs={{0,1},{1,3},{3,2},{2,0},{4,5},{5,7},{7,6},{6,4},{8,9},{9,11},{11,1... | collective-permute-start | bytes 393224 | tf_op jit(solution)/shard_map/ppermute | solution.py:405
  21.4 2.6 %collective-permute-start.4 = (bf16[32,2048]{1,0:T(8,128)(2,1)S(1)}, bf16[32,2048]{1,0:T(8,128)(2,1)S(1)}, u32[]{:S(2)}, u32[]{:S(2)}) collective-permute-start(bf16[32,2048]{1,0:T(8,128)(2,1)S(1)} %get-tuple-element.24), channel_id=1, source_target_pairs={{0,1},{1,3},{3,2},{2,0},{4,5},{5,7},{7,6},{6,4},{8,9},{9,11},{11,1... | collective-permute-start | bytes 393224 | tf_op jit(solution)/shard_map/ppermute | solution.py:405
  24.1 1.1 %fusion.15 = f32[4,64,768]{2,1,0:T(8,128)S(1)} fusion(f32[4,64,768]{2,1,0:T(8,128)S(1)} %broadcast_in_dim.15, s32[]{:T(128)S(6)} %select_n.84, bf16[96,8,16,128]{3,2,1,0:T(8,128)(2,1)S(1)} %bitcast.72, bf16[32,2048]{1,0:T(8,128)(2,1)S(1)} %get-tuple-element.25, bf16[32,2048]{1,0:T(8,128)(2,1)S(1)} %get-tuple-element.24), kind=kOutput, calls=%fused_computation.13 | convolution fusion | flops 201850880 | bytes 3604484 | tf_op jit(solution)/shard_map/dot_general | solution.py:407
  25.4 1.2 %collective-permute-start.7 = (bf16[32,2048]{1,0:T(8,128)(2,1)S(1)}, bf16[32,2048]{1,0:T(8,128)(2,1)S(1)}, u32[]{:S(2)}, u32[]{:S(2)}) collective-permute-start(bf16[32,2048]{1,0:T(8,128)(2,1)S(1)} %collective-permute-done.5), channel_id=1, source_target_pairs={{0,1},{1,3},{3,2},{2,0},{4,5},{5,7},{7,6},{6,4},{8,9},{9,11},{11,1... | collective-permute-start | bytes 393224 | tf_op jit(solution)/shard_map/ppermute | solution.py:405
  26.5 0.8 %collective-permute-done.4 = bf16[32,2048]{1,0:T(8,128)(2,1)S(1)} collective-permute-done((bf16[32,2048]{1,0:T(8,128)(2,1)S(1)}, bf16[32,2048]{1,0:T(8,128)(2,1)S(1)}, u32[]{:S(2)}, u32[]{:S(2)}) %collective-permute-start.4) | collective-permute-done | bytes 131104 | tf_op jit(solution)/shard_map/ppermute | solution.py:405
  27.3 2.6 %collective-permute-start.6 = (bf16[32,2048]{1,0:T(8,128)(2,1)S(1)}, bf16[32,2048]{1,0:T(8,128)(2,1)S(1)}, u32[]{:S(2)}, u32[]{:S(2)}) collective-permute-start(bf16[32,2048]{1,0:T(8,128)(2,1)S(1)} %collective-permute-done.4), channel_id=1, source_target_pairs={{0,1},{1,3},{3,2},{2,0},{4,5},{5,7},{7,6},{6,4},{8,9},{9,11},{11,1... | collective-permute-start | bytes 393224 | tf_op jit(solution)/shard_map/ppermute | solution.py:405
  29.9 1.1 %fusion.21 = f32[4,64,768]{2,1,0:T(8,128)S(1)} fusion(f32[4,64,768]{2,1,0:T(8,128)S(1)} %fusion.15, s32[]{:T(128)S(6)} %select_n.88, bf16[96,8,16,128]{3,2,1,0:T(8,128)(2,1)S(1)} %bitcast.73, bf16[32,2048]{1,0:T(8,128)(2,1)S(1)} %collective-permute-done.5, bf16[32,2048]{1,0:T(8,128)(2,1)S(1)} %collective-permute-done.4), kind=kOutput, calls=%fused_computation.15 | convolution fusion | flops 201850880 | bytes 3604484 | tf_op jit(solution)/shard_map/dot_general | solution.py:407
  30.9 1.0 %collective-permute-done.7 = bf16[32,2048]{1,0:T(8,128)(2,1)S(1)} collective-permute-done((bf16[32,2048]{1,0:T(8,128)(2,1)S(1)}, bf16[32,2048]{1,0:T(8,128)(2,1)S(1)}, u32[]{:S(2)}, u32[]{:S(2)}) %collective-permute-start.7) | collective-permute-done | bytes 131104 | tf_op jit(solution)/shard_map/ppermute | solution.py:405
  32.0 0.8 %collective-permute-start.9 = (bf16[32,2048]{1,0:T(8,128)(2,1)S(1)}, bf16[32,2048]{1,0:T(8,128)(2,1)S(1)}, u32[]{:S(2)}, u32[]{:S(2)}) collective-permute-start(bf16[32,2048]{1,0:T(8,128)(2,1)S(1)} %collective-permute-done.7), channel_id=1, source_target_pairs={{0,1},{1,3},{3,2},{2,0},{4,5},{5,7},{7,6},{6,4},{8,9},{9,11},{11,1... | collective-permute-start | bytes 393224 | tf_op jit(solution)/shard_map/ppermute | solution.py:405
  32.8 1.4 %collective-permute-done.6 = bf16[32,2048]{1,0:T(8,128)(2,1)S(1)} collective-permute-done((bf16[32,2048]{1,0:T(8,128)(2,1)S(1)}, bf16[32,2048]{1,0:T(8,128)(2,1)S(1)}, u32[]{:S(2)}, u32[]{:S(2)}) %collective-permute-start.6) | collective-permute-done | bytes 131104 | tf_op jit(solution)/shard_map/ppermute | solution.py:405
  34.2 2.1 %collective-permute-start.8 = (bf16[32,2048]{1,0:T(8,128)(2,1)S(1)}, bf16[32,2048]{1,0:T(8,128)(2,1)S(1)}, u32[]{:S(2)}, u32[]{:S(2)}) collective-permute-start(bf16[32,2048]{1,0:T(8,128)(2,1)S(1)} %collective-permute-done.6), channel_id=1, source_target_pairs={{0,1},{1,3},{3,2},{2,0},{4,5},{5,7},{7,6},{6,4},{8,9},{9,11},{11,1... | collective-permute-start | bytes 393224 | tf_op jit(solution)/shard_map/ppermute | solution.py:405
  36.2 1.1 %fusion.27 = f32[4,64,768]{2,1,0:T(8,128)S(1)} fusion(f32[4,64,768]{2,1,0:T(8,128)S(1)} %fusion.21, s32[]{:T(128)S(6)} %select_n.92, bf16[96,8,16,128]{3,2,1,0:T(8,128)(2,1)S(1)} %bitcast.74, bf16[32,2048]{1,0:T(8,128)(2,1)S(1)} %collective-permute-done.7, bf16[32,2048]{1,0:T(8,128)(2,1)S(1)} %collective-permute-done.6), kind=kOutput, calls=%fused_computation.17 | convolution fusion | flops 201850880 | bytes 3604484 | tf_op jit(solution)/shard_map/dot_general | solution.py:407
  37.3 0.5 collective-permute-done.9
  37.8 3.6 %collective-permute-done.8 = bf16[32,2048]{1,0:T(8,128)(2,1)S(1)} collective-permute-done((bf16[32,2048]{1,0:T(8,128)(2,1)S(1)}, bf16[32,2048]{1,0:T(8,128)(2,1)S(1)}, u32[]{:S(2)}, u32[]{:S(2)}) %collective-permute-start.8) | collective-permute-done | bytes 131104 | tf_op jit(solution)/shard_map/ppermute | solution.py:405
  41.4 1.1 %fusion.33 = f32[4,64,768]{2,1,0:T(8,128)S(1)} fusion(f32[4,64,768]{2,1,0:T(8,128)S(1)} %fusion.27, s32[]{:T(128)S(6)} %select_n.96, bf16[96,8,16,128]{3,2,1,0:T(8,128)(2,1)S(1)} %bitcast.75, bf16[32,2048]{1,0:T(8,128)(2,1)S(1)} %collective-permute-done.9, bf16[32,2048]{1,0:T(8,128)(2,1)S(1)} %collective-permute-done.8), kind=kOutput, calls=%fused_computation.19 | convolution fusion | flops 201850880 | bytes 3604484 | tf_op jit(solution)/shard_map/dot_general | solution.py:407
  42.5 0.8 %collective-permute-start.10 = (bf16[2,2,32,768]{3,2,1,0:T(8,128)(2,1)S(1)}, bf16[2,2,32,768]{3,2,1,0:T(8,128)(2,1)S(1)}, u32[]{:S(2)}, u32[]{:S(2)}) collective-permute-start(bf16[2,2,32,768]{3,2,1,0:T(8,128)(2,1)S(1)} %fusion.48), channel_id=1, source_target_pairs={{0,8},{4,12},{8,0},{12,4},{16,24},{20,28},{24,16},{28,20},{1,9},{5... | collective-permute-start | bytes 589832 | tf_op jit(solution)/shard_map/ppermute | solution.py:424
  43.3 1.1 %collective-permute-done.10 = bf16[2,2,32,768]{3,2,1,0:T(8,128)(2,1)S(1)} collective-permute-done((bf16[2,2,32,768]{3,2,1,0:T(8,128)(2,1)S(1)}, bf16[2,2,32,768]{3,2,1,0:T(8,128)(2,1)S(1)}, u32[]{:S(2)}, u32[]{:S(2)}) %collective-permute-start.10) | collective-permute-done | bytes 196640 | tf_op jit(solution)/shard_map/ppermute | solution.py:424
  44.5 5.6 %collective-permute-start.13 = (bf16[32,768]{1,0:T(8,128)(2,1)S(1)}, bf16[32,768]{1,0:T(8,128)(2,1)S(1)}, u32[]{:S(2)}, u32[]{:S(2)}) collective-permute-start(bf16[32,768]{1,0:T(8,128)(2,1)S(1)} %get-tuple-element.27), channel_id=1, source_target_pairs={{0,20},{4,16},{8,28},{12,24},{16,4},{20,0},{24,12},{28,8},{1,21},{... | collective-permute-start | bytes 147464 | tf_op jit(solution)/shard_map/ppermute | solution.py:437
  50.1 1.0 %collective-permute-start.11 = (bf16[32,768]{1,0:T(8,128)(2,1)S(1)}, bf16[32,768]{1,0:T(8,128)(2,1)S(1)}, u32[]{:S(2)}, u32[]{:S(2)}) collective-permute-start(bf16[32,768]{1,0:T(8,128)(2,1)S(1)} %get-tuple-element.26), channel_id=1, source_target_pairs={{0,4},{4,0},{8,12},{12,8},{16,20},{20,16},{24,28},{28,24},{1,5},{5... | collective-permute-start | bytes 147464 | tf_op jit(solution)/shard_map/ppermute | solution.py:437
  51.1 0.8 %pad_maximum_fusion = f32[1024,128]{1,0:T(8,128)} fusion(f32[512,128]{1,0:T(8,128)S(1)} %get-tuple-element.23, f32[512,128]{1,0:T(8,128)S(1)} %get-tuple-element.21), kind=kLoop, calls=%fused_computation.20 | loop fusion | flops 131072 | bytes 1048576 | tf_op jit(solution)/shard_map/concatenate | solution.py:373
  51.9 0.2 collective-permute-done.13
  52.2 2.0 %collective-permute-done.12 = bf16[32,768]{1,0:T(8,128)(2,1)S(1)} collective-permute-done((bf16[32,768]{1,0:T(8,128)(2,1)S(1)}, bf16[32,768]{1,0:T(8,128)(2,1)S(1)}, u32[]{:S(2)}, u32[]{:S(2)}) %collective-permute-start.12) | collective-permute-done | bytes 49184 | tf_op jit(solution)/shard_map/ppermute | solution.py:437
  54.2 0.7 %fusion.51 = f32[768,32]{0,1:T(8,128)} fusion(bf16[32,768]{1,0:T(8,128)(2,1)S(1)} %collective-permute-done.13, bf16[32,768]{1,0:T(8,128)(2,1)S(1)} %collective-permute-done.12, bf16[32,768]{1,0:T(8,128)(2,1)S(1)} %collective-permute-done.11, f32[4,32,768]{2,1,0:T(8,128)S(1)} %bitcast.69, s32[]{:T(128)S(6)} %select_n.101), kind=kLoop, calls=%fused_computation.40 | loop fusion | flops 147456 | bytes 344068 | tf_op jit(solution)/shard_map/transpose | solution.py:440
  (13 shorter events, 0.4 us)
Async XLA Ops:
  2.1 1.8 %collective-permute-start = (f32[74,8,128]{2,1,0:T(8,128)S(1)}, f32[74,8,128]{2,1,0:T(8,128)S(1)}, u32[]{:S(2)}, u32[]{:S(2)}) collective-permute-start(f32[74,8,128]{2,1,0:T(8,128)S(1)} %get-tuple-element.17), channel_id=1, source_target_pairs={{0,8},{4,12},{8,0},{12,4},{16,24},{20,28},{24,16},{28,20},{1,9},{5... | collective-permute-start | bytes 909320 | tf_op jit(solution)/shard_map/ppermute | solution.py:329
  2.7 4.9 %collective-permute-start.1 = (f32[65,8,128]{2,1,0:T(8,128)S(1)}, f32[65,8,128]{2,1,0:T(8,128)S(1)}, u32[]{:S(2)}, u32[]{:S(2)}) collective-permute-start(f32[65,8,128]{2,1,0:T(8,128)S(1)} %get-tuple-element.18), channel_id=1, source_target_pairs={{8,16},{12,20},{16,8},{20,12},{9,17},{13,21},{17,9},{21,13},{10,18... | collective-permute-start | bytes 798728 | tf_op jit(solution)/shard_map/ppermute | solution.py:329
  3.9 5.7 %collective-permute-start.2 = (f32[27,8,128]{2,1,0:T(8,128)S(1)}, f32[27,8,128]{2,1,0:T(8,128)S(1)}, u32[]{:S(2)}, u32[]{:S(2)}) collective-permute-start(f32[27,8,128]{2,1,0:T(8,128)S(1)} %pad_maximum_fusion.1), channel_id=1, source_target_pairs={{0,4},{4,0},{8,12},{12,8},{16,20},{20,16},{24,28},{28,24},{1,5},{5... | collective-permute-start | bytes 331784 | tf_op jit(solution)/shard_map/ppermute | solution.py:329
  6.8 0.7 %collective-permute-start.3 = (f32[9,8,128]{2,1,0:T(8,128)S(1)}, f32[9,8,128]{2,1,0:T(8,128)S(1)}, u32[]{:S(2)}, u32[]{:S(2)}) collective-permute-start(f32[9,8,128]{2,1,0:T(8,128)S(1)} %get-tuple-element.20), channel_id=1, source_target_pairs={{8,20},{12,16},{16,12},{20,8},{9,21},{13,17},{17,13},{21,9},{10,22... | collective-permute-start | bytes 110600 | tf_op jit(solution)/shard_map/ppermute | solution.py:329
  7.6 16.5 %copy-start = (bf16[768,16,128]{2,1,0:T(8,128)(2,1)S(1)}, bf16[768,16,128]{2,1,0:T(8,128)(2,1)}, u32[]{:S(2)}) copy-start(bf16[768,16,128]{2,1,0:T(8,128)(2,1)} %param.7) | copy-start | bytes 9437188
  19.1 6.3 %collective-permute-start.5 = (bf16[32,2048]{1,0:T(8,128)(2,1)S(1)}, bf16[32,2048]{1,0:T(8,128)(2,1)S(1)}, u32[]{:S(2)}, u32[]{:S(2)}) collective-permute-start(bf16[32,2048]{1,0:T(8,128)(2,1)S(1)} %get-tuple-element.25), channel_id=1, source_target_pairs={{0,1},{1,3},{3,2},{2,0},{4,5},{5,7},{7,6},{6,4},{8,9},{9,11},{11,1... | collective-permute-start | bytes 393224 | tf_op jit(solution)/shard_map/ppermute | solution.py:405
  21.4 5.9 %collective-permute-start.4 = (bf16[32,2048]{1,0:T(8,128)(2,1)S(1)}, bf16[32,2048]{1,0:T(8,128)(2,1)S(1)}, u32[]{:S(2)}, u32[]{:S(2)}) collective-permute-start(bf16[32,2048]{1,0:T(8,128)(2,1)S(1)} %get-tuple-element.24), channel_id=1, source_target_pairs={{0,1},{1,3},{3,2},{2,0},{4,5},{5,7},{7,6},{6,4},{8,9},{9,11},{11,1... | collective-permute-start | bytes 393224 | tf_op jit(solution)/shard_map/ppermute | solution.py:405
  25.4 6.6 %collective-permute-start.7 = (bf16[32,2048]{1,0:T(8,128)(2,1)S(1)}, bf16[32,2048]{1,0:T(8,128)(2,1)S(1)}, u32[]{:S(2)}, u32[]{:S(2)}) collective-permute-start(bf16[32,2048]{1,0:T(8,128)(2,1)S(1)} %collective-permute-done.5), channel_id=1, source_target_pairs={{0,1},{1,3},{3,2},{2,0},{4,5},{5,7},{7,6},{6,4},{8,9},{9,11},{11,1... | collective-permute-start | bytes 393224 | tf_op jit(solution)/shard_map/ppermute | solution.py:405
  27.3 6.9 %collective-permute-start.6 = (bf16[32,2048]{1,0:T(8,128)(2,1)S(1)}, bf16[32,2048]{1,0:T(8,128)(2,1)S(1)}, u32[]{:S(2)}, u32[]{:S(2)}) collective-permute-start(bf16[32,2048]{1,0:T(8,128)(2,1)S(1)} %collective-permute-done.4), channel_id=1, source_target_pairs={{0,1},{1,3},{3,2},{2,0},{4,5},{5,7},{7,6},{6,4},{8,9},{9,11},{11,1... | collective-permute-start | bytes 393224 | tf_op jit(solution)/shard_map/ppermute | solution.py:405
  32.0 5.9 %collective-permute-start.9 = (bf16[32,2048]{1,0:T(8,128)(2,1)S(1)}, bf16[32,2048]{1,0:T(8,128)(2,1)S(1)}, u32[]{:S(2)}, u32[]{:S(2)}) collective-permute-start(bf16[32,2048]{1,0:T(8,128)(2,1)S(1)} %collective-permute-done.7), channel_id=1, source_target_pairs={{0,1},{1,3},{3,2},{2,0},{4,5},{5,7},{7,6},{6,4},{8,9},{9,11},{11,1... | collective-permute-start | bytes 393224 | tf_op jit(solution)/shard_map/ppermute | solution.py:405
  34.2 7.3 %collective-permute-start.8 = (bf16[32,2048]{1,0:T(8,128)(2,1)S(1)}, bf16[32,2048]{1,0:T(8,128)(2,1)S(1)}, u32[]{:S(2)}, u32[]{:S(2)}) collective-permute-start(bf16[32,2048]{1,0:T(8,128)(2,1)S(1)} %collective-permute-done.6), channel_id=1, source_target_pairs={{0,1},{1,3},{3,2},{2,0},{4,5},{5,7},{7,6},{6,4},{8,9},{9,11},{11,1... | collective-permute-start | bytes 393224 | tf_op jit(solution)/shard_map/ppermute | solution.py:405
  42.5 1.8 %collective-permute-start.10 = (bf16[2,2,32,768]{3,2,1,0:T(8,128)(2,1)S(1)}, bf16[2,2,32,768]{3,2,1,0:T(8,128)(2,1)S(1)}, u32[]{:S(2)}, u32[]{:S(2)}) collective-permute-start(bf16[2,2,32,768]{3,2,1,0:T(8,128)(2,1)S(1)} %fusion.48), channel_id=1, source_target_pairs={{0,8},{4,12},{8,0},{12,4},{16,24},{20,28},{24,16},{28,20},{1,9},{5... | collective-permute-start | bytes 589832 | tf_op jit(solution)/shard_map/ppermute | solution.py:424
  44.5 7.7 %collective-permute-start.13 = (bf16[32,768]{1,0:T(8,128)(2,1)S(1)}, bf16[32,768]{1,0:T(8,128)(2,1)S(1)}, u32[]{:S(2)}, u32[]{:S(2)}) collective-permute-start(bf16[32,768]{1,0:T(8,128)(2,1)S(1)} %get-tuple-element.27), channel_id=1, source_target_pairs={{0,20},{4,16},{8,28},{12,24},{16,4},{20,0},{24,12},{28,8},{1,21},{... | collective-permute-start | bytes 147464 | tf_op jit(solution)/shard_map/ppermute | solution.py:437
  50.1 4.1 %collective-permute-start.12 = (bf16[32,768]{1,0:T(8,128)(2,1)S(1)}, bf16[32,768]{1,0:T(8,128)(2,1)S(1)}, u32[]{:S(2)}, u32[]{:S(2)}) collective-permute-start(bf16[32,768]{1,0:T(8,128)(2,1)S(1)} %get-tuple-element.28), channel_id=1, source_target_pairs={{0,16},{4,20},{8,24},{12,28},{16,0},{20,4},{24,8},{28,12},{1,17},{... | collective-permute-start | bytes 147464 | tf_op jit(solution)/shard_map/ppermute | solution.py:437
  50.1 4.1 %collective-permute-start.11 = (bf16[32,768]{1,0:T(8,128)(2,1)S(1)}, bf16[32,768]{1,0:T(8,128)(2,1)S(1)}, u32[]{:S(2)}, u32[]{:S(2)}) collective-permute-start(bf16[32,768]{1,0:T(8,128)(2,1)S(1)} %get-tuple-element.26), channel_id=1, source_target_pairs={{0,4},{4,0},{8,12},{12,8},{16,20},{20,16},{24,28},{28,24},{1,5},{5... | collective-permute-start | bytes 147464 | tf_op jit(solution)/shard_map/ppermute | solution.py:437

commit v6 on v5

--- a/solution.py
+++ b/solution.py
@@ -13,7 +13,7 @@
 LANES = 128
 SIDE = 2 * DEG
 UNROLL = 8
-CHUNKS = 2
+SHARES = (1, 1)
 VMEM_GRANT = 16 * 1024 * 1024
 F32 = jnp.float32
 BF16 = jnp.bfloat16
@@ -69,8 +69,9 @@
         base = pl.multiple_of(upper * (width_x - DEG), SUB)
         for row in range(DEG):
             for g in range(groups):
-                row_refs[which][row * groups + g] = adj_ref[pl.ds(g * SUB * width_x + base + row, SUB, stride=width_x), :]
-        row_refs[which][DEG * groups] = ids_ref[pl.ds(base, SUB), :].astype(F32) + 1.0
+                tile = adj_ref[pl.ds(g * SUB * width_x + base + row, SUB, stride=width_x), :]
+                row_refs[which][row * groups + g] = tile.astype(BF16)
+        row_refs[which][DEG * groups] = (ids_ref[pl.ds(base, SUB), :].astype(F32) + 1.0).astype(BF16)
     for kind in range(n_kinds):
         upper = upper_y if kind == 0 else 1 - upper_y
         keep = (low_side ^ upper) == 1
@@ -79,10 +80,10 @@
             for g in range(groups):
                 tile = adj_ref[pl.ds(g * SUB * width_x + row, SUB, stride=width_x), :]
                 strip = jnp.where((lane // SIDE) == g, lane_gather(tile, index), strip)
-            strip_refs[2 * kind][row] = jnp.where(keep, strip, 0.0)
+            strip_refs[2 * kind][row] = jnp.where(keep, strip, 0.0).astype(BF16)
         for tile_x in range(width_x // SUB):
             ids = ids_ref[tile_x * SUB : (tile_x + 1) * SUB, :].astype(F32) + 1.0
-            strip_refs[2 * kind][width_x + tile_x] = jnp.where(keep, lane_gather(ids, index), 0.0)
+            strip_refs[2 * kind][width_x + tile_x] = jnp.where(keep, lane_gather(ids, index), 0.0).astype(BF16)
         for which in range(2):
             upper = upper_x if which == 0 else 1 - upper_x
             base = upper * (width_x - DEG)
@@ -170,18 +171,22 @@
             y_ref[x, g] = total
 
     repeat = lane & (SIDE - 1)
+
+    def pick(from_even, one, other):
+        return jnp.where(from_even, one.astype(F32), other.astype(F32))
+
     if first:
         for high in (False, True):
             x0 = tall - DEG if high else 0
             from_even = even_x if high else jnp.logical_not(even_x)
-            lookup(jnp.where(from_even, even_ref[DEG * all_groups], odd_ref[DEG * all_groups]), x0, False)
-            ids = jnp.where(from_even, strip_ref[beyond + DEG], strip_odd_ref[DEG])
+            lookup(pick(from_even, even_ref[DEG * all_groups], odd_ref[DEG * all_groups]), x0, False)
+            ids = pick(from_even, strip_ref[beyond + DEG], strip_odd_ref[DEG])
             lookup(lane_gather(ids, repeat), x0, True)
         for tile_x in range(width_x // SUB):
             x0 = DEG + tile_x * SUB
             cond = lookup(ids_ref[tile_x * SUB : (tile_x + 1) * SUB, :] + 1, x0, False)
             table[INVERSE, x0 : x0 + SUB, :] = 1.0 / cond
-            lookup(lane_gather(strip_ref[width_x + tile_x], repeat), x0, True)
+            lookup(lane_gather(strip_ref[width_x + tile_x].astype(F32), repeat), x0, True)
     for high in (False, True):
         x0 = tall - DEG if high else 0
         from_even = even_x if high else jnp.logical_not(even_x)
@@ -190,8 +195,8 @@
             tiles = []
             for g in range(groups):
                 at = row * all_groups + offset + g
-                tiles.append(jnp.where(from_even, even_ref[at], odd_ref[at]) * scale)
-            strip = jnp.where(from_even, strip_ref[beyond + row], strip_odd_ref[row])
+                tiles.append(pick(from_even, even_ref[at], odd_ref[at]) * scale)
+            strip = pick(from_even, strip_ref[beyond + row], strip_odd_ref[row])
             place_row(x0 + row, tiles + [strip * spread(COND_S, x0 + row)])
     for row in range(width_x):
         x = DEG + row
@@ -199,7 +204,7 @@
         tiles = []
         for g in range(groups):
             tiles.append(adj_ref[pl.ds((offset + g) * SUB * width_x + row, SUB, stride=width_x), :] * scale)
-        place_row(x, tiles + [strip_ref[row] * spread(COND_S, x)])
+        place_row(x, tiles + [strip_ref[row].astype(F32) * spread(COND_S, x)])
 
     def swept(lo, body, after=None):
         n = tall - 2 * lo
@@ -211,11 +216,8 @@
 
         step(lo, UNROLL, None, 0)
 
-        def run(i, carry):
+        for i in range(1, blocks):
             step(lo + i * UNROLL, UNROLL, lo + (i - 1) * UNROLL, UNROLL)
-            return carry
-
-        lax.fori_loop(1, blocks, run, 0)
         x = lo + blocks * UNROLL
         if rest:
             step(x, rest, x - UNROLL, UNROLL)
@@ -273,12 +275,19 @@
                 value = inverse * (power[0] * u_ref[x + r, g] + d * rows[r + 1][g]) + cond * total
                 smooth_ref[pl.ds(g * SUB * width_x + at, SUB, stride=width_x), :] = value
                 out.append(value)
-            column = at * LANES if isinstance(at, int) else pl.multiple_of(at * LANES, LANES)
+            column = at * LANES
             for g in range(0, groups, 2):
                 both = jnp.concatenate(out[g : g + 2], axis=0)
                 low_ref[pl.ds(g * SUB, 2 * SUB), pl.ds(column, LANES)] = both.astype(BF16)
 
     swept(DEG, last)
+
+
+def chunk_sizes(groups):
+    unit = groups // sum(SHARES)
+    if groups % sum(SHARES) or any(unit * share % 2 for share in SHARES):
+        return (groups,)
+    return tuple(unit * share for share in SHARES)
 
 
 def vmem():
@@ -300,11 +309,11 @@
     n_kinds = 2 if size_y > 2 else 1
     row_tiles = DEG * groups + 1
     row_shapes = [
-        jax.ShapeDtypeStruct((row_tiles + n_kinds * (DEG + 1), SUB, LANES), F32),
-        jax.ShapeDtypeStruct((row_tiles, SUB, LANES), F32),
+        jax.ShapeDtypeStruct((row_tiles + n_kinds * (DEG + 1), SUB, LANES), BF16),
+        jax.ShapeDtypeStruct((row_tiles, SUB, LANES), BF16),
     ]
-    strip_shape = jax.ShapeDtypeStruct((width_x + width_x // SUB, SUB, LANES), F32)
-    corner_shape = jax.ShapeDtypeStruct((DEG + 1, SUB, LANES), F32)
+    strip_shape = jax.ShapeDtypeStruct((width_x + width_x // SUB, SUB, LANES), BF16)
+    corner_shape = jax.ShapeDtypeStruct((DEG + 1, SUB, LANES), BF16)
     small = [pltpu.SMEM(v.shape, F32) for v in (mat_diag, mat_cond, cheb_coef)]
     flat, ids, params, *packed = pl.pallas_call(
         functools.partial(pack_kernel, groups, width_x, n_kinds),
@@ -338,12 +347,11 @@
         strips.append((swap(tall_strip, None, kind), corner))
     strip, strip_odd = (functools.reduce(jnp.add, part) for part in zip(*strips))
     tall = width_x + 2 * DEG
-    n_chunks = CHUNKS if groups % (2 * CHUNKS) == 0 else 1
-    part = groups // n_chunks
-    field = pltpu.VMEM((tall, part + 1, SUB, LANES), F32)
+    parts = chunk_sizes(groups)
     smooth = []
     low = []
-    for chunk in range(n_chunks):
+    for chunk, part in enumerate(parts):
+        field = pltpu.VMEM((tall, part + 1, SUB, LANES), F32)
         out_shape = [
             pltpu.VMEM((part * SUB * width_x, width_y), F32),
             pltpu.VMEM((part * SUB, width_x * width_y), BF16),
@@ -357,7 +365,7 @@
             operands += [table]
             in_specs += [vmem()]
         call = pl.pallas_call(
-            functools.partial(filter_kernel, part, groups, chunk * part, width_x, chunk == 0),
+            functools.partial(filter_kernel, part, groups, sum(parts[:chunk]), width_x, chunk == 0),
             out_shape=out_shape,
             in_specs=in_specs,
             out_specs=[vmem()] * len(out_shape),
@@ -370,7 +378,7 @@
         low.append(got[1])
         if chunk == 0:
             table = got[2]
-    smooth = smooth[0] if n_chunks == 1 else jnp.concatenate(smooth)
+    smooth = smooth[0] if len(parts) == 1 else jnp.concatenate(smooth)
     return smooth.reshape(adjoint.shape), low
 
 

time: 55 us -> 53.2 us (0.967)
  Pallas kernels: 11 us -> 8.46 us
  matrix products: 4.32 us -> 6.21 us
  waiting for transfers between devices: 13.4 us -> 11.8 us
    pallas_call x2, Pallas kernels: 9.5 us -> 6.98 us  [filtered(): got = call(*operands)]
    dot_general x4, matrix products: 4.32 us -> 6.21 us  [gathered_product(): lax.dot_general(piece, rows, (((1,), (1,)), ((), ())), preferred_element_...]
    ppermute x1, starting transfers between devices: 0.76 us -> 1.84 us  [reduced(): total = keep + lax.ppermute(send, ('sx', 'sy'), half).astype(F32)]
    ppermute x6, waiting for transfers between devices: 7.52 us -> 6.57 us  [gathered_product(): following.append(lax.ppermute(piece, 'cr', hop))]
    ppermute x6, starting transfers between devices: 11.5 us -> 10.7 us  [gathered_product(): following.append(lax.ppermute(piece, 'cr', hop))]
    ppermute x4, waiting for transfers between devices: 2.53 us -> 1.75 us  [swap(): return lax.ppermute(value, ('sx', 'sy'), pairs)]
  transfers between devices with their start and end apart: 14 -> 14, of which waited for: 11 -> 9; matrix products, arithmetic and copies ran while one was open for 8% -> 11% of each run, Pallas kernels for 0% -> 0%
where the time goes in v6:
time: 53.2 us; the launch traced here: 53 us
  starting transfers between devices  24.1 us (45%)
  waiting for transfers between devices  11.8 us (22%)
  Pallas kernels  8.46 us (16%)
  matrix products  6.21 us (12%)
  other arithmetic  1.53 us (3%)
  between operations  0.8 us (2%)
    ppermute x6, starting transfers between devices, gathered_product(): following.append(lax.ppermute(piece, 'cr', hop))  10.7 us
    pallas_call x2, Pallas kernels, filtered(): got = call(*operands)  6.98 us
    ppermute x3, starting transfers between devices, reduced(): arrived.append(lax.ppermute(out, ('sx', 'sy'), pairs))  6.74 us
    ppermute x6, waiting for transfers between devices, gathered_product(): following.append(lax.ppermute(piece, 'cr', hop))  6.57 us
    dot_general x4, matrix products, gathered_product(): lax.dot_general(piece, rows, (((1,), (1,)), ((), ())), preferred_element_...  6.21 us
    ppermute x4, starting transfers between devices, swap(): return lax.ppermute(value, ('sx', 'sy'), pairs)  4.8 us
    ppermute x3, waiting for transfers between devices, reduced(): arrived.append(lax.ppermute(out, ('sx', 'sy'), pairs))  2.38 us
    ppermute x1, starting transfers between devices, reduced(): total = keep + lax.ppermute(send, ('sx', 'sy'), half).astype(F32)  1.84 us
  transfers between devices with their start and end apart: 14, of which 9 were waited for; matrix products, arithmetic and copies ran while one was open for 11% of the time, Pallas kernels for 0%

profile of v6, /device:TPU:0, one launch (start us, length us, event | category | flops | bytes accessed | tf_op | source)
XLA Modules:
  0.0 53.0 jit_solution(9194431587548288807)
XLA Ops:
  0.6 1.5 %pack.1 = (f32[1024,128]{1,0:T(8,128)S(1)}, s32[16,128]{1,0:T(8,128)S(1)}, f32[3,8,128]{2,1,0:T(8,128)S(1)}, bf16[74,8,128]{2,1,0:T(8,128)(2,1)S(1)}, bf16[65,8,...) custom-call(f32[1024,128]{1,0:T(8,128)} %bitcast.70, s32[16,128]{1,0:T(8,128)} %refs_1_.1, ...), custom_call_target="tpu_custom_call" | custom-call | tf_op jit(solution)/shard_map/pack/pallas_call | solution.py:318
  2.1 0.6 %collective-permute-start = (bf16[74,8,128]{2,1,0:T(8,128)(2,1)S(1)}, bf16[74,8,128]{2,1,0:T(8,128)(2,1)S(1)}, u32[]{:S(2)}, u32[]{:S(2)}) collective-permute-start(bf16[74,8,128]{2,1,0:T(8,128)(2,1)S(1)} %get-tuple-element.17), channel_id=1, source_target_pairs={{0,8},{4,12},{8,0},{12,4},{16,24},{20,28},{24,16},{28,20},{1,9},{5... | collective-permute-start | bytes 454664 | tf_op jit(solution)/shard_map/ppermute | solution.py:338
  2.7 0.7 %collective-permute-start.1 = (bf16[65,8,128]{2,1,0:T(8,128)(2,1)S(1)}, bf16[65,8,128]{2,1,0:T(8,128)(2,1)S(1)}, u32[]{:S(2)}, u32[]{:S(2)}) collective-permute-start(bf16[65,8,128]{2,1,0:T(8,128)(2,1)S(1)} %get-tuple-element.18), channel_id=1, source_target_pairs={{8,16},{12,20},{16,8},{20,12},{9,17},{13,21},{17,9},{21,13},{10,18... | collective-permute-start | bytes 399368 | tf_op jit(solution)/shard_map/ppermute | solution.py:338
  3.3 0.3 collective-permute-done.refs_3_
  3.7 2.9 %collective-permute-start.2 = (bf16[27,8,128]{2,1,0:T(8,128)(2,1)S(1)}, bf16[27,8,128]{2,1,0:T(8,128)(2,1)S(1)}, u32[]{:S(2)}, u32[]{:S(2)}) collective-permute-start(bf16[27,8,128]{2,1,0:T(8,128)(2,1)S(1)} %pad_maximum_fusion.1), channel_id=1, source_target_pairs={{0,4},{4,0},{8,12},{12,8},{16,20},{20,16},{24,28},{28,24},{1,5},{5... | collective-permute-start | bytes 165896 | tf_op jit(solution)/shard_map/ppermute | solution.py:338
  6.6 0.7 %collective-permute-start.3 = (bf16[9,8,128]{2,1,0:T(8,128)(2,1)S(1)}, bf16[9,8,128]{2,1,0:T(8,128)(2,1)S(1)}, u32[]{:S(2)}, u32[]{:S(2)}) collective-permute-start(bf16[9,8,128]{2,1,0:T(8,128)(2,1)S(1)} %get-tuple-element.20), channel_id=1, source_target_pairs={{8,20},{12,16},{16,12},{20,8},{9,21},{13,17},{17,13},{21,9},{10,22... | collective-permute-start | bytes 55304 | tf_op jit(solution)/shard_map/ppermute | solution.py:338
  7.4 1.4 %collective-permute-done.2.refs_5_ = bf16[27,8,128]{2,1,0:T(8,128)(2,1)S(1)} collective-permute-done((bf16[27,8,128]{2,1,0:T(8,128)(2,1)S(1)}, bf16[27,8,128]{2,1,0:T(8,128)(2,1)S(1)}, u32[]{:S(2)}, u32[]{:S(2)}) %collective-permute-start.2) | collective-permute-done | bytes 55328 | tf_op jit(solution)/shard_map/ppermute | solution.py:338
  8.8 3.5 %shard_map.77 = (f32[512,128]{1,0:T(8,128)S(1)}, bf16[32,2048]{1,0:T(8,128)(2,1)S(1)}, f32[7,32,128]{2,1,0:T(8,128)S(1)}) custom-call(f32[3,8,128]{2,1,0:T(8,128)S(1)} %get-tuple-element.14.refs_0_, f32[1024,128]{1,0:T(8,128)S(1)} %get-tuple-element.15.refs_1_, s32[16,128]{1,0:T(8,128)S(1)} %get-tuple-element.16.refs_2_, ...), custom_call_target="tpu_custom_call" | custom-call | flops 12000000 | bytes 800000 | tf_op jit(solution)/shard_map/pallas_call | solution.py:376
  12.3 3.4 %shard_map.78 = (f32[512,128]{1,0:T(8,128)S(1)}, bf16[32,2048]{1,0:T(8,128)(2,1)S(1)}) custom-call(f32[3,8,128]{2,1,0:T(8,128)S(1)} %get-tuple-element.14.refs_0_, f32[1024,128]{1,0:T(8,128)S(1)} %get-tuple-element.15.refs_1_, s32[16,128]{1,0:T(8,128)S(1)} %get-tuple-element.16.refs_2_, bf16[74,8,128]{2,1,0:T(8,128)(2,1)S(1)} %collective-permute-done.refs_3_, ...), custom_call_target="tpu_custom_call" | custom-call | flops 12000000 | bytes 800000 | tf_op jit(solution)/shard_map/pallas_call | solution.py:376
  15.8 2.1 %collective-permute-start.5 = (bf16[32,2048]{1,0:T(8,128)(2,1)S(1)}, bf16[32,2048]{1,0:T(8,128)(2,1)S(1)}, u32[]{:S(2)}, u32[]{:S(2)}) collective-permute-start(bf16[32,2048]{1,0:T(8,128)(2,1)S(1)} %get-tuple-element.25), channel_id=1, source_target_pairs={{0,1},{1,3},{3,2},{2,0},{4,5},{5,7},{7,6},{6,4},{8,9},{9,11},{11,1... | collective-permute-start | bytes 393224 | tf_op jit(solution)/shard_map/ppermute | solution.py:413
  17.9 2.6 %collective-permute-start.4 = (bf16[32,2048]{1,0:T(8,128)(2,1)S(1)}, bf16[32,2048]{1,0:T(8,128)(2,1)S(1)}, u32[]{:S(2)}, u32[]{:S(2)}) collective-permute-start(bf16[32,2048]{1,0:T(8,128)(2,1)S(1)} %get-tuple-element.24), channel_id=1, source_target_pairs={{0,1},{1,3},{3,2},{2,0},{4,5},{5,7},{7,6},{6,4},{8,9},{9,11},{11,1... | collective-permute-start | bytes 393224 | tf_op jit(solution)/shard_map/ppermute | solution.py:413
  20.5 0.1 broadcast_in_dim.15
  20.6 3.0 %fusion.15 = f32[4,64,768]{2,1,0:T(8,128)S(1)} fusion(f32[4,64,768]{2,1,0:T(8,128)S(1)} %broadcast_in_dim.15, s32[]{:T(128)S(6)} %select_n.84, bf16[96,8,16,128]{3,2,1,0:T(8,128)(2,1)} %bitcast.72, bf16[32,2048]{1,0:T(8,128)(2,1)S(1)} %get-tuple-element.25, bf16[32,2048]{1,0:T(8,128)(2,1)S(1)} %get-tuple-element.24), kind=kOutput, calls=%fused_computation.13 | convolution fusion | flops 201850880 | bytes 3604484 | tf_op jit(solution)/shard_map/dot_general | solution.py:415
  23.5 0.5 collective-permute-start.7
  24.0 2.3 %collective-permute-start.6 = (bf16[32,2048]{1,0:T(8,128)(2,1)S(1)}, bf16[32,2048]{1,0:T(8,128)(2,1)S(1)}, u32[]{:S(2)}, u32[]{:S(2)}) collective-permute-start(bf16[32,2048]{1,0:T(8,128)(2,1)S(1)} %collective-permute-done.4), channel_id=1, source_target_pairs={{0,1},{1,3},{3,2},{2,0},{4,5},{5,7},{7,6},{6,4},{8,9},{9,11},{11,1... | collective-permute-start | bytes 393224 | tf_op jit(solution)/shard_map/ppermute | solution.py:413
  26.4 1.1 %fusion.21 = f32[4,64,768]{2,1,0:T(8,128)S(1)} fusion(f32[4,64,768]{2,1,0:T(8,128)S(1)} %fusion.15, s32[]{:T(128)S(6)} %select_n.88, bf16[96,8,16,128]{3,2,1,0:T(8,128)(2,1)S(1)} %bitcast.73, bf16[32,2048]{1,0:T(8,128)(2,1)S(1)} %collective-permute-done.5, bf16[32,2048]{1,0:T(8,128)(2,1)S(1)} %collective-permute-done.4), kind=kOutput, calls=%fused_computation.15 | convolution fusion | flops 201850880 | bytes 3604484 | tf_op jit(solution)/shard_map/dot_general | solution.py:415
  27.5 2.0 %collective-permute-done.7 = bf16[32,2048]{1,0:T(8,128)(2,1)S(1)} collective-permute-done((bf16[32,2048]{1,0:T(8,128)(2,1)S(1)}, bf16[32,2048]{1,0:T(8,128)(2,1)S(1)}, u32[]{:S(2)}, u32[]{:S(2)}) %collective-permute-start.7) | collective-permute-done | bytes 131104 | tf_op jit(solution)/shard_map/ppermute | solution.py:413
  29.5 0.6 %collective-permute-start.9 = (bf16[32,2048]{1,0:T(8,128)(2,1)S(1)}, bf16[32,2048]{1,0:T(8,128)(2,1)S(1)}, u32[]{:S(2)}, u32[]{:S(2)}) collective-permute-start(bf16[32,2048]{1,0:T(8,128)(2,1)S(1)} %collective-permute-done.7), channel_id=1, source_target_pairs={{0,1},{1,3},{3,2},{2,0},{4,5},{5,7},{7,6},{6,4},{8,9},{9,11},{11,1... | collective-permute-start | bytes 393224 | tf_op jit(solution)/shard_map/ppermute | solution.py:413
  30.1 0.8 %collective-permute-done.6 = bf16[32,2048]{1,0:T(8,128)(2,1)S(1)} collective-permute-done((bf16[32,2048]{1,0:T(8,128)(2,1)S(1)}, bf16[32,2048]{1,0:T(8,128)(2,1)S(1)}, u32[]{:S(2)}, u32[]{:S(2)}) %collective-permute-start.6) | collective-permute-done | bytes 131104 | tf_op jit(solution)/shard_map/ppermute | solution.py:413
  30.9 2.6 %collective-permute-start.8 = (bf16[32,2048]{1,0:T(8,128)(2,1)S(1)}, bf16[32,2048]{1,0:T(8,128)(2,1)S(1)}, u32[]{:S(2)}, u32[]{:S(2)}) collective-permute-start(bf16[32,2048]{1,0:T(8,128)(2,1)S(1)} %collective-permute-done.6), channel_id=1, source_target_pairs={{0,1},{1,3},{3,2},{2,0},{4,5},{5,7},{7,6},{6,4},{8,9},{9,11},{11,1... | collective-permute-start | bytes 393224 | tf_op jit(solution)/shard_map/ppermute | solution.py:413
  33.5 1.1 %fusion.27 = f32[4,64,768]{2,1,0:T(8,128)S(1)} fusion(f32[4,64,768]{2,1,0:T(8,128)S(1)} %fusion.21, s32[]{:T(128)S(6)} %select_n.92, bf16[96,8,16,128]{3,2,1,0:T(8,128)(2,1)S(1)} %bitcast.74, bf16[32,2048]{1,0:T(8,128)(2,1)S(1)} %collective-permute-done.7, bf16[32,2048]{1,0:T(8,128)(2,1)S(1)} %collective-permute-done.6), kind=kOutput, calls=%fused_computation.17 | convolution fusion | flops 201850880 | bytes 3604484 | tf_op jit(solution)/shard_map/dot_general | solution.py:415
  34.5 1.5 %collective-permute-done.9 = bf16[32,2048]{1,0:T(8,128)(2,1)S(1)} collective-permute-done((bf16[32,2048]{1,0:T(8,128)(2,1)S(1)}, bf16[32,2048]{1,0:T(8,128)(2,1)S(1)}, u32[]{:S(2)}, u32[]{:S(2)}) %collective-permute-start.9) | collective-permute-done | bytes 131104 | tf_op jit(solution)/shard_map/ppermute | solution.py:413
  36.0 2.3 %collective-permute-done.8 = bf16[32,2048]{1,0:T(8,128)(2,1)S(1)} collective-permute-done((bf16[32,2048]{1,0:T(8,128)(2,1)S(1)}, bf16[32,2048]{1,0:T(8,128)(2,1)S(1)}, u32[]{:S(2)}, u32[]{:S(2)}) %collective-permute-start.8) | collective-permute-done | bytes 131104 | tf_op jit(solution)/shard_map/ppermute | solution.py:413
  38.3 1.1 %fusion.33 = f32[4,64,768]{2,1,0:T(8,128)S(1)} fusion(f32[4,64,768]{2,1,0:T(8,128)S(1)} %fusion.27, s32[]{:T(128)S(6)} %select_n.96, bf16[96,8,16,128]{3,2,1,0:T(8,128)(2,1)S(1)} %bitcast.75, bf16[32,2048]{1,0:T(8,128)(2,1)S(1)} %collective-permute-done.9, bf16[32,2048]{1,0:T(8,128)(2,1)S(1)} %collective-permute-done.8), kind=kOutput, calls=%fused_computation.19 | convolution fusion | flops 201850880 | bytes 3604484 | tf_op jit(solution)/shard_map/dot_general | solution.py:415
  39.4 1.8 %collective-permute-start.10 = (bf16[2,2,32,768]{3,2,1,0:T(8,128)(2,1)S(1)}, bf16[2,2,32,768]{3,2,1,0:T(8,128)(2,1)S(1)}, u32[]{:S(2)}, u32[]{:S(2)}) collective-permute-start(bf16[2,2,32,768]{3,2,1,0:T(8,128)(2,1)S(1)} %fusion.48), channel_id=1, source_target_pairs={{0,8},{4,12},{8,0},{12,4},{16,24},{20,28},{24,16},{28,20},{1,9},{5... | collective-permute-start | bytes 589832 | tf_op jit(solution)/shard_map/ppermute | solution.py:432
  41.2 1.1 %collective-permute-done.10 = bf16[2,2,32,768]{3,2,1,0:T(8,128)(2,1)S(1)} collective-permute-done((bf16[2,2,32,768]{3,2,1,0:T(8,128)(2,1)S(1)}, bf16[2,2,32,768]{3,2,1,0:T(8,128)(2,1)S(1)}, u32[]{:S(2)}, u32[]{:S(2)}) %collective-permute-start.10) | collective-permute-done | bytes 196640 | tf_op jit(solution)/shard_map/ppermute | solution.py:432
  42.4 5.9 %collective-permute-start.13 = (bf16[32,768]{1,0:T(8,128)(2,1)S(1)}, bf16[32,768]{1,0:T(8,128)(2,1)S(1)}, u32[]{:S(2)}, u32[]{:S(2)}) collective-permute-start(bf16[32,768]{1,0:T(8,128)(2,1)S(1)} %get-tuple-element.27), channel_id=1, source_target_pairs={{0,20},{4,16},{8,28},{12,24},{16,4},{20,0},{24,12},{28,8},{1,21},{... | collective-permute-start | bytes 147464 | tf_op jit(solution)/shard_map/ppermute | solution.py:445
  48.2 0.9 %collective-permute-start.11 = (bf16[32,768]{1,0:T(8,128)(2,1)S(1)}, bf16[32,768]{1,0:T(8,128)(2,1)S(1)}, u32[]{:S(2)}, u32[]{:S(2)}) collective-permute-start(bf16[32,768]{1,0:T(8,128)(2,1)S(1)} %get-tuple-element.26), channel_id=1, source_target_pairs={{0,4},{4,0},{8,12},{12,8},{16,20},{20,16},{24,28},{28,24},{1,5},{5... | collective-permute-start | bytes 147464 | tf_op jit(solution)/shard_map/ppermute | solution.py:445
  49.1 0.8 %pad_maximum_fusion = f32[1024,128]{1,0:T(8,128)} fusion(f32[512,128]{1,0:T(8,128)S(1)} %get-tuple-element.23, f32[512,128]{1,0:T(8,128)S(1)} %get-tuple-element.21), kind=kLoop, calls=%fused_computation.20 | loop fusion | flops 131072 | bytes 1048576 | tf_op jit(solution)/shard_map/concatenate | solution.py:381
  50.0 0.4 collective-permute-done.13
  50.3 2.0 %collective-permute-done.12 = bf16[32,768]{1,0:T(8,128)(2,1)S(1)} collective-permute-done((bf16[32,768]{1,0:T(8,128)(2,1)S(1)}, bf16[32,768]{1,0:T(8,128)(2,1)S(1)}, u32[]{:S(2)}, u32[]{:S(2)}) %collective-permute-start.12) | collective-permute-done | bytes 49184 | tf_op jit(solution)/shard_map/ppermute | solution.py:445
  52.3 0.7 %fusion.51 = f32[768,32]{0,1:T(8,128)} fusion(bf16[32,768]{1,0:T(8,128)(2,1)S(1)} %collective-permute-done.13, bf16[32,768]{1,0:T(8,128)(2,1)S(1)} %collective-permute-done.12, bf16[32,768]{1,0:T(8,128)(2,1)S(1)} %collective-permute-done.11, f32[4,32,768]{2,1,0:T(8,128)S(1)} %bitcast.69, s32[]{:T(128)S(6)} %select_n.101), kind=kLoop, calls=%fused_computation.39 | loop fusion | flops 147456 | bytes 344068 | tf_op jit(solution)/shard_map/transpose | solution.py:448
  (13 shorter events, 0.1 us)
Async XLA Ops:
  2.1 1.6 %collective-permute-start = (bf16[74,8,128]{2,1,0:T(8,128)(2,1)S(1)}, bf16[74,8,128]{2,1,0:T(8,128)(2,1)S(1)}, u32[]{:S(2)}, u32[]{:S(2)}) collective-permute-start(bf16[74,8,128]{2,1,0:T(8,128)(2,1)S(1)} %get-tuple-element.17), channel_id=1, source_target_pairs={{0,8},{4,12},{8,0},{12,4},{16,24},{20,28},{24,16},{28,20},{1,9},{5... | collective-permute-start | bytes 454664 | tf_op jit(solution)/shard_map/ppermute | solution.py:338
  2.7 4.7 %collective-permute-start.1 = (bf16[65,8,128]{2,1,0:T(8,128)(2,1)S(1)}, bf16[65,8,128]{2,1,0:T(8,128)(2,1)S(1)}, u32[]{:S(2)}, u32[]{:S(2)}) collective-permute-start(bf16[65,8,128]{2,1,0:T(8,128)(2,1)S(1)} %get-tuple-element.18), channel_id=1, source_target_pairs={{8,16},{12,20},{16,8},{20,12},{9,17},{13,21},{17,9},{21,13},{10,18... | collective-permute-start | bytes 399368 | tf_op jit(solution)/shard_map/ppermute | solution.py:338
  3.7 5.1 %collective-permute-start.2 = (bf16[27,8,128]{2,1,0:T(8,128)(2,1)S(1)}, bf16[27,8,128]{2,1,0:T(8,128)(2,1)S(1)}, u32[]{:S(2)}, u32[]{:S(2)}) collective-permute-start(bf16[27,8,128]{2,1,0:T(8,128)(2,1)S(1)} %pad_maximum_fusion.1), channel_id=1, source_target_pairs={{0,4},{4,0},{8,12},{12,8},{16,20},{20,16},{24,28},{28,24},{1,5},{5... | collective-permute-start | bytes 165896 | tf_op jit(solution)/shard_map/ppermute | solution.py:338
  6.6 0.7 %collective-permute-start.3 = (bf16[9,8,128]{2,1,0:T(8,128)(2,1)S(1)}, bf16[9,8,128]{2,1,0:T(8,128)(2,1)S(1)}, u32[]{:S(2)}, u32[]{:S(2)}) collective-permute-start(bf16[9,8,128]{2,1,0:T(8,128)(2,1)S(1)} %get-tuple-element.20), channel_id=1, source_target_pairs={{8,20},{12,16},{16,12},{20,8},{9,21},{13,17},{17,13},{21,9},{10,22... | collective-permute-start | bytes 55304 | tf_op jit(solution)/shard_map/ppermute | solution.py:338
  12.3 14.0 %copy-start = (bf16[768,16,128]{2,1,0:T(8,128)(2,1)S(1)}, bf16[768,16,128]{2,1,0:T(8,128)(2,1)}, u32[]{:S(2)}) copy-start(bf16[768,16,128]{2,1,0:T(8,128)(2,1)} %param.7) | copy-start | bytes 9437188
  15.8 7.8 %collective-permute-start.5 = (bf16[32,2048]{1,0:T(8,128)(2,1)S(1)}, bf16[32,2048]{1,0:T(8,128)(2,1)S(1)}, u32[]{:S(2)}, u32[]{:S(2)}) collective-permute-start(bf16[32,2048]{1,0:T(8,128)(2,1)S(1)} %get-tuple-element.25), channel_id=1, source_target_pairs={{0,1},{1,3},{3,2},{2,0},{4,5},{5,7},{7,6},{6,4},{8,9},{9,11},{11,1... | collective-permute-start | bytes 393224 | tf_op jit(solution)/shard_map/ppermute | solution.py:413
  17.9 6.1 %collective-permute-start.4 = (bf16[32,2048]{1,0:T(8,128)(2,1)S(1)}, bf16[32,2048]{1,0:T(8,128)(2,1)S(1)}, u32[]{:S(2)}, u32[]{:S(2)}) collective-permute-start(bf16[32,2048]{1,0:T(8,128)(2,1)S(1)} %get-tuple-element.24), channel_id=1, source_target_pairs={{0,1},{1,3},{3,2},{2,0},{4,5},{5,7},{7,6},{6,4},{8,9},{9,11},{11,1... | collective-permute-start | bytes 393224 | tf_op jit(solution)/shard_map/ppermute | solution.py:413
  23.5 5.9 %collective-permute-start.7 = (bf16[32,2048]{1,0:T(8,128)(2,1)S(1)}, bf16[32,2048]{1,0:T(8,128)(2,1)S(1)}, u32[]{:S(2)}, u32[]{:S(2)}) collective-permute-start(bf16[32,2048]{1,0:T(8,128)(2,1)S(1)} %collective-permute-done.5), channel_id=1, source_target_pairs={{0,1},{1,3},{3,2},{2,0},{4,5},{5,7},{7,6},{6,4},{8,9},{9,11},{11,1... | collective-permute-start | bytes 393224 | tf_op jit(solution)/shard_map/ppermute | solution.py:413
  24.0 6.8 %collective-permute-start.6 = (bf16[32,2048]{1,0:T(8,128)(2,1)S(1)}, bf16[32,2048]{1,0:T(8,128)(2,1)S(1)}, u32[]{:S(2)}, u32[]{:S(2)}) collective-permute-start(bf16[32,2048]{1,0:T(8,128)(2,1)S(1)} %collective-permute-done.4), channel_id=1, source_target_pairs={{0,1},{1,3},{3,2},{2,0},{4,5},{5,7},{7,6},{6,4},{8,9},{9,11},{11,1... | collective-permute-start | bytes 393224 | tf_op jit(solution)/shard_map/ppermute | solution.py:413
  29.5 6.5 %collective-permute-start.9 = (bf16[32,2048]{1,0:T(8,128)(2,1)S(1)}, bf16[32,2048]{1,0:T(8,128)(2,1)S(1)}, u32[]{:S(2)}, u32[]{:S(2)}) collective-permute-start(bf16[32,2048]{1,0:T(8,128)(2,1)S(1)} %collective-permute-done.7), channel_id=1, source_target_pairs={{0,1},{1,3},{3,2},{2,0},{4,5},{5,7},{7,6},{6,4},{8,9},{9,11},{11,1... | collective-permute-start | bytes 393224 | tf_op jit(solution)/shard_map/ppermute | solution.py:413
  30.9 7.4 %collective-permute-start.8 = (bf16[32,2048]{1,0:T(8,128)(2,1)S(1)}, bf16[32,2048]{1,0:T(8,128)(2,1)S(1)}, u32[]{:S(2)}, u32[]{:S(2)}) collective-permute-start(bf16[32,2048]{1,0:T(8,128)(2,1)S(1)} %collective-permute-done.6), channel_id=1, source_target_pairs={{0,1},{1,3},{3,2},{2,0},{4,5},{5,7},{7,6},{6,4},{8,9},{9,11},{11,1... | collective-permute-start | bytes 393224 | tf_op jit(solution)/shard_map/ppermute | solution.py:413
  39.4 2.9 %collective-permute-start.10 = (bf16[2,2,32,768]{3,2,1,0:T(8,128)(2,1)S(1)}, bf16[2,2,32,768]{3,2,1,0:T(8,128)(2,1)S(1)}, u32[]{:S(2)}, u32[]{:S(2)}) collective-permute-start(bf16[2,2,32,768]{3,2,1,0:T(8,128)(2,1)S(1)} %fusion.48), channel_id=1, source_target_pairs={{0,8},{4,12},{8,0},{12,4},{16,24},{20,28},{24,16},{28,20},{1,9},{5... | collective-permute-start | bytes 589832 | tf_op jit(solution)/shard_map/ppermute | solution.py:432
  42.4 7.9 %collective-permute-start.13 = (bf16[32,768]{1,0:T(8,128)(2,1)S(1)}, bf16[32,768]{1,0:T(8,128)(2,1)S(1)}, u32[]{:S(2)}, u32[]{:S(2)}) collective-permute-start(bf16[32,768]{1,0:T(8,128)(2,1)S(1)} %get-tuple-element.27), channel_id=1, source_target_pairs={{0,20},{4,16},{8,28},{12,24},{16,4},{20,0},{24,12},{28,8},{1,21},{... | collective-permute-start | bytes 147464 | tf_op jit(solution)/shard_map/ppermute | solution.py:445
  48.2 4.1 %collective-permute-start.12 = (bf16[32,768]{1,0:T(8,128)(2,1)S(1)}, bf16[32,768]{1,0:T(8,128)(2,1)S(1)}, u32[]{:S(2)}, u32[]{:S(2)}) collective-permute-start(bf16[32,768]{1,0:T(8,128)(2,1)S(1)} %get-tuple-element.28), channel_id=1, source_target_pairs={{0,16},{4,20},{8,24},{12,28},{16,0},{20,4},{24,8},{28,12},{1,17},{... | collective-permute-start | bytes 147464 | tf_op jit(solution)/shard_map/ppermute | solution.py:445
  48.2 4.1 %collective-permute-start.11 = (bf16[32,768]{1,0:T(8,128)(2,1)S(1)}, bf16[32,768]{1,0:T(8,128)(2,1)S(1)}, u32[]{:S(2)}, u32[]{:S(2)}) collective-permute-start(bf16[32,768]{1,0:T(8,128)(2,1)S(1)} %get-tuple-element.26), channel_id=1, source_target_pairs={{0,4},{4,0},{8,12},{12,8},{16,20},{20,16},{24,28},{28,24},{1,5},{5... | collective-permute-start | bytes 147464 | tf_op jit(solution)/shard_map/ppermute | solution.py:445
